TPU v7x, 32 devices: a whole 2x2x4 slice. The times are simulated.
32 devices in a mesh: dp: 8 (over z, x), wshard: 4 (over y, core).
Axes of the slice: x: 2, y: 2, z: 4, core: 2. Of those that a mesh axis runs over, the one named last changes fastest.
Arguments:
- tokens: bfloat16 [16384, 1024], P(('dp', 'wshard')), may hold values from -6 to 6
- cotangent: bfloat16 [16384, 1024], P(('dp', 'wshard')), may hold values from -6 to 6
- span_starts: int32 [32], P(('dp', 'wshard')), may hold values from 0 to 256
- routes: int32 [16384, 2], P(('dp', 'wshard')), may hold values from 0 to 7, all different within a row; in each aligned block of 512 rows (0 to 511, 512 to 1023, ...) at most 160 rows name the same one
- norm_gains: float32 [2, 1024], replicated, may hold values from 0.5 to 1.5
- bias_table: float32 [32, 16], replicated, may hold values from -4 to 4
- router: bfloat16 [1024, 8], replicated, may hold values from -0.1875 to 0.1875
- attn_qkv: bfloat16 [3, 1024, 1024], P(None, None, 'wshard'), may hold values from -0.1875 to 0.1875
- attn_out: bfloat16 [1024, 1024], P(None, 'wshard'), may hold values from -1.5 to 1.5
- expert_in: bfloat16 [8, 2, 1024, 2816], P('dp', None, None, 'wshard'), may hold values from -0.1875 to 0.1875
- expert_down: bfloat16 [8, 2816, 1024], P('dp', 'wshard'), may hold values from -0.109375 to 0.109375
Outputs:
- output: bfloat16 [16384, 1024], P(('dp', 'wshard'))
- grad_tokens: bfloat16 [16384, 1024], P(('dp', 'wshard'))
- grad_norm_gains: float32 [2, 1024], replicated
- grad_bias_table: float32 [32, 16], replicated
- grad_router: float32 [1024, 8], replicated
- grad_attn_qkv: float32 [3, 1024, 1024], P(None, None, 'wshard')
- grad_attn_out: float32 [1024, 1024], P(None, 'wshard')
- grad_expert_in: float32 [8, 2, 1024, 2816], P('dp', None, None, 'wshard')
- grad_expert_down: float32 [8, 2816, 1024], P('dp', 'wshard')
Inputs may be any that keep to these rules, and one draw needn't show every extreme that they name: `routes`: each token names two different experts; among the rows of one device no expert is named more than 160 times, a bound that some block reaches. `span_starts`: the picture span of a sequence covers 256 positions inside it.
All inputs are finite; a program needn't handle non-finite values.
Results may differ from a plain program's by a relative error of at most 0.015.
The roundings to bfloat16 on the way count: a program that leaves them out, or rounds other values in their place, can miss the bound.
Values may be sent and summed in bfloat16 or wider, within the bound.
A program may use at most 256 MiB of HBM per device.

v0:
```python
import jax
import jax.numpy as jnp
from jax import lax
from jax.sharding import PartitionSpec as P

PIC = 256


PRECISE = lax.Precision.HIGHEST
EPSILON = 1e-06
MASKED_SCORE = -1e30
BUCKET_EDGES = (8, 11, 16, 23, 32, 45, 64, 91)


def bucket_ones(seq_length, bucket_count):
    positions = jnp.arange(seq_length, dtype=jnp.int32)
    offset = positions[:, None] - positions[None, :]
    magnitude = jnp.abs(offset)
    coarse = 7 + sum(((magnitude >= bound).astype(jnp.int32) for bound in BUCKET_EDGES))
    bucket = jnp.where(magnitude < 8, magnitude, coarse) + 16 * (offset < 0).astype(jnp.int32)
    labels = jnp.arange(bucket_count, dtype=jnp.int32)
    return (bucket.reshape(1, -1) == labels[:, None]).astype(jnp.float32)


def visible_of(span_start, seq_length):
    positions = jnp.arange(seq_length, dtype=jnp.int32)
    inside = (positions >= span_start) & (positions < span_start + PIC)
    return (positions[None, :] <= positions[:, None]) | inside[:, None] & inside[None, :]


def gelu_mix(gate_pre, up_pre):
    inner = 0.7978845608028654 * (gate_pre + 0.044715 * gate_pre * gate_pre * gate_pre)
    return 0.5 * gate_pre * (1.0 + jnp.tanh(inner)) * up_pre


def norm_forward(values, gain):
    recip = lax.rsqrt(jnp.mean(values * values, -1, keepdims=True) + EPSILON)
    unit = values * recip
    return (unit * gain, unit, recip)


def norm_backward(grad_normed, unit, recip, gain):
    grad_gain = jnp.sum(grad_normed * unit, 0)
    scaled = grad_normed * gain
    grad_input = recip * (scaled - unit * jnp.mean(scaled * unit, -1, keepdims=True))
    return (grad_input, grad_gain)


def per_device(
    tokens,
    cotangent,
    span_starts,
    routes,
    norm_gains,
    bias_table,
    router,
    attn_qkv,
    attn_out,
    expert_in,
    expert_down,
):
    seq_count = span_starts.shape[0]
    tok_count, model_width = tokens.shape
    seq_length = tok_count // seq_count
    head_count = bias_table.shape[1]
    head_size = model_width // head_count
    expert_count = router.shape[1]
    capacity = (10 * tok_count + 4 * expert_count - 1) // (4 * expert_count)
    owner_count = expert_count * capacity
    qkv_full, out_full = (
        lax.all_gather(attn_qkv, "wshard", axis=2, tiled=True),
        lax.all_gather(attn_out, "wshard", axis=1, tiled=True),
    )
    tokens_f = tokens.astype(jnp.float32)
    normed_first, unit_first, recip_first = norm_forward(tokens_f, norm_gains[0])
    normed_one = normed_first.astype(jnp.bfloat16)
    projected = jnp.einsum(
        "td,cde->cte", normed_one, qkv_full, preferred_element_type=jnp.float32
    ).astype(jnp.bfloat16)
    heads_view = projected.reshape(3, seq_count, seq_length, head_count, head_size)
    table_ones = bucket_ones(seq_length, bias_table.shape[0])
    bias_full = jnp.dot(bias_table.T, table_ones, precision=PRECISE).reshape(
        head_count, seq_length, seq_length
    )

    def scores_of(query_rows, key_rows, span_start):
        raw_scores = (
            jnp.einsum("ihd,jhd->hij", query_rows, key_rows, preferred_element_type=jnp.float32)
            * 0.125
            + bias_full
        )
        return jnp.where(visible_of(span_start, seq_length)[None], raw_scores, MASKED_SCORE)

    def attend_one(pieces):
        query_rows, key_rows, value_rows, span_start = pieces
        raw_scores = scores_of(query_rows, key_rows, span_start)
        row_max = jnp.max(raw_scores, -1, keepdims=True)
        exponent = jnp.exp(raw_scores - row_max)
        row_total = jnp.sum(exponent, -1, keepdims=True)
        probs_low = (exponent / row_total).astype(jnp.bfloat16)
        mixed_rows = jnp.einsum(
            "hij,jhd->ihd", probs_low, value_rows, preferred_element_type=jnp.float32
        )
        return (mixed_rows.astype(jnp.bfloat16), (row_max + jnp.log(row_total))[..., 0])

    mixed, log_totals = lax.map(
        attend_one, (heads_view[0], heads_view[1], heads_view[2], span_starts)
    )
    mixed_flat = mixed.reshape(tok_count, model_width)
    hidden = tokens_f + jnp.dot(mixed_flat, out_full, preferred_element_type=jnp.float32)
    normed_second, unit_second, recip_second = norm_forward(hidden, norm_gains[1])
    normed_two = normed_second.astype(jnp.bfloat16)
    logits = jnp.dot(normed_two, router, preferred_element_type=jnp.float32)
    chosen_mask = (routes[:, :, None] == jnp.arange(expert_count, dtype=jnp.int32)).astype(
        jnp.float32
    )
    chosen = jnp.sum(logits[:, None, :] * chosen_mask, -1)
    chosen_exp = jnp.exp(chosen - jnp.max(chosen, -1, keepdims=True))
    gate_probs = chosen_exp / jnp.sum(chosen_exp, -1, keepdims=True)
    flat_routes = routes.reshape(-1)
    route_hits = (flat_routes[:, None] == jnp.arange(expert_count, dtype=jnp.int32)).astype(
        jnp.int32
    )
    before = jnp.cumsum(route_hits, 0) - route_hits
    slot_dest = flat_routes * capacity + jnp.sum(before * route_hits, 1)
    outgoing = (
        jnp.zeros((owner_count, model_width), jnp.bfloat16)
        .at[slot_dest]
        .set(jnp.repeat(normed_two, 2, axis=0))
    )
    outgoing = outgoing.reshape(expert_count, capacity, model_width)
    arrived_rows = lax.all_to_all(outgoing, "dp", split_axis=0, concat_axis=0, tiled=True).reshape(
        -1, model_width
    )
    in_full, down_full = (
        lax.all_gather(expert_in, "wshard", axis=3, tiled=True),
        lax.all_gather(expert_down, "wshard", axis=1, tiled=True),
    )
    pre_acts = jnp.einsum(
        "rd,cdf->crf", arrived_rows, in_full[0], preferred_element_type=jnp.float32
    )
    act = gelu_mix(pre_acts[0], pre_acts[1]).astype(jnp.bfloat16)
    made = jnp.dot(act, down_full[0], preferred_element_type=jnp.float32).astype(jnp.bfloat16)
    returned = lax.all_to_all(
        made.reshape(expert_count, capacity, model_width),
        "dp",
        split_axis=0,
        concat_axis=0,
        tiled=True,
    )
    picked = (
        returned.reshape(-1, model_width)[slot_dest]
        .astype(jnp.float32)
        .reshape(tok_count, 2, model_width)
    )
    output = hidden + jnp.sum(gate_probs[:, :, None] * picked, 1)
    grad_out = cotangent.astype(jnp.float32)
    grad_gate = jnp.sum(grad_out[:, None, :] * picked, -1)
    grad_picked = (
        (gate_probs[:, :, None] * grad_out[:, None, :])
        .reshape(tok_count * 2, model_width)
        .astype(jnp.bfloat16)
    )
    grad_made = jnp.zeros((owner_count, model_width), jnp.bfloat16).at[slot_dest].set(grad_picked)
    grad_made = grad_made.reshape(expert_count, capacity, model_width)
    grad_arrived, rows_again = (
        lax.all_to_all(grad_made, "dp", split_axis=0, concat_axis=0, tiled=True),
        lax.all_to_all(outgoing, "dp", split_axis=0, concat_axis=0, tiled=True),
    )
    owner_rows = rows_again.reshape(-1, model_width)
    grad_arrived = grad_arrived.reshape(-1, model_width)
    weights_in_back, weights_down_back = (
        lax.all_gather(expert_in, "wshard", axis=3, tiled=True),
        lax.all_gather(expert_down, "wshard", axis=1, tiled=True),
    )
    pre_back = jnp.einsum(
        "rd,cdf->crf", owner_rows, weights_in_back[0], preferred_element_type=jnp.float32
    )
    act_back = gelu_mix(pre_back[0], pre_back[1]).astype(jnp.bfloat16)
    grad_act = jnp.einsum(
        "rd,fd->rf", grad_arrived, weights_down_back[0], preferred_element_type=jnp.float32
    )
    grad_down = jnp.einsum("rf,rd->fd", act_back, grad_arrived, preferred_element_type=jnp.float32)
    _, pull_mix = jax.vjp(gelu_mix, pre_back[0], pre_back[1])
    grad_gate_pre, grad_up_pre = pull_mix(grad_act)
    grads_low = jnp.stack([grad_gate_pre, grad_up_pre]).astype(jnp.bfloat16)
    grad_in = jnp.einsum("rd,crf->cdf", owner_rows, grads_low, preferred_element_type=jnp.float32)
    grad_rows = jnp.einsum(
        "crf,cdf->rd", grads_low, weights_in_back[0], preferred_element_type=jnp.float32
    ).astype(jnp.bfloat16)
    grad_expert_in, grad_expert_down = (
        lax.psum_scatter(
            grad_in[None].astype(jnp.bfloat16), "wshard", scatter_dimension=3, tiled=True
        ).astype(jnp.float32),
        lax.psum_scatter(
            grad_down[None].astype(jnp.bfloat16), "wshard", scatter_dimension=1, tiled=True
        ).astype(jnp.float32),
    )
    grad_back = lax.all_to_all(
        grad_rows.reshape(expert_count, capacity, model_width),
        "dp",
        split_axis=0,
        concat_axis=0,
        tiled=True,
    )
    grad_normed_two = jnp.sum(
        grad_back.reshape(-1, model_width)[slot_dest]
        .astype(jnp.float32)
        .reshape(tok_count, 2, model_width),
        1,
    )
    grad_chosen = gate_probs * (grad_gate - jnp.sum(gate_probs * grad_gate, -1, keepdims=True))
    grad_logits = jnp.sum(grad_chosen[:, :, None] * chosen_mask, 1)
    grad_router_local = jnp.dot(normed_two.astype(jnp.float32).T, grad_logits, precision=PRECISE)
    grad_normed_two = grad_normed_two + jnp.dot(
        grad_logits, router.astype(jnp.float32).T, precision=PRECISE
    )
    grad_hidden_norm, grad_gain_two = norm_backward(
        grad_normed_two, unit_second, recip_second, norm_gains[1]
    )
    grad_hidden = grad_out + grad_hidden_norm
    qkv_back, out_back = (
        lax.all_gather(attn_qkv, "wshard", axis=2, tiled=True),
        lax.all_gather(attn_out, "wshard", axis=1, tiled=True),
    )
    grad_branch = grad_hidden.astype(jnp.bfloat16)
    grad_out_proj = jnp.einsum(
        "ti,to->io", mixed_flat, grad_branch, preferred_element_type=jnp.float32
    )
    grad_mixed = jnp.einsum(
        "to,io->ti", grad_branch, out_back, preferred_element_type=jnp.float32
    ).astype(jnp.bfloat16)
    grad_mixed = grad_mixed.reshape(seq_count, seq_length, head_count, head_size)

    def attend_back(bias_sum, pieces):
        query_rows, key_rows, value_rows, span_start, log_rows, grad_mix = pieces
        raw_scores = scores_of(query_rows, key_rows, span_start)
        probs = jnp.exp(raw_scores - log_rows[..., None])
        probs_low = probs.astype(jnp.bfloat16)
        grad_probs = jnp.einsum(
            "ihd,jhd->hij", grad_mix, value_rows, preferred_element_type=jnp.float32
        )
        grad_value = jnp.einsum(
            "hij,ihd->jhd", probs_low, grad_mix, preferred_element_type=jnp.float32
        ).astype(jnp.bfloat16)
        grad_raw = (probs * (grad_probs - jnp.sum(probs * grad_probs, -1, keepdims=True))).astype(
            jnp.bfloat16
        )
        grad_query = (
            jnp.einsum("hij,jhd->ihd", grad_raw, key_rows, preferred_element_type=jnp.float32)
            * 0.125
        ).astype(jnp.bfloat16)
        grad_key = (
            jnp.einsum("hij,ihd->jhd", grad_raw, query_rows, preferred_element_type=jnp.float32)
            * 0.125
        ).astype(jnp.bfloat16)
        return (
            bias_sum + grad_raw.astype(jnp.float32),
            jnp.stack([grad_query, grad_key, grad_value]),
        )

    bias_sum, grad_heads = lax.scan(
        attend_back,
        jnp.zeros((head_count, seq_length, seq_length), jnp.float32),
        (heads_view[0], heads_view[1], heads_view[2], span_starts, log_totals, grad_mixed),
    )
    grad_projected = jnp.transpose(grad_heads, (1, 0, 2, 3, 4)).reshape(3, tok_count, model_width)
    grad_qkv_local = jnp.einsum(
        "td,cte->cde", normed_one, grad_projected, preferred_element_type=jnp.float32
    )
    grad_normed_one = jnp.einsum(
        "cte,cde->td", grad_projected, qkv_back, preferred_element_type=jnp.float32
    )
    grad_tokens_norm, grad_gain_one = norm_backward(
        grad_normed_one, unit_first, recip_first, norm_gains[0]
    )
    grad_tokens = (grad_hidden + grad_tokens_norm).astype(jnp.bfloat16)
    grad_table_local = lax.dot_general(
        table_ones, bias_sum.reshape(head_count, -1), (((1,), (1,)), ((), ())), precision=PRECISE
    )
    qkv_part, out_part = (
        lax.psum_scatter(
            grad_qkv_local.astype(jnp.bfloat16), "wshard", scatter_dimension=2, tiled=True
        ).astype(jnp.float32),
        lax.psum_scatter(
            grad_out_proj.astype(jnp.bfloat16), "wshard", scatter_dimension=1, tiled=True
        ).astype(jnp.float32),
    )
    grad_attn_qkv, grad_attn_out = lax.psum((qkv_part, out_part), "dp")
    grad_norm_gains, grad_bias_table, grad_router = lax.psum(
        (jnp.stack([grad_gain_one, grad_gain_two]), grad_table_local, grad_router_local),
        ("dp", "wshard"),
    )
    return (
        output.astype(jnp.bfloat16),
        grad_tokens,
        grad_norm_gains,
        grad_bias_table,
        grad_router,
        grad_attn_qkv,
        grad_attn_out,
        grad_expert_in,
        grad_expert_down,
    )


def solution(mesh):
    return jax.shard_map(
        per_device,
        mesh=mesh,
        in_specs=(
            P(("dp", "wshard"), None),
            P(("dp", "wshard"), None),
            P(("dp", "wshard")),
            P(("dp", "wshard"), None),
            P(),
            P(),
            P(),
            P(None, None, "wshard"),
            P(None, "wshard"),
            P("dp", None, None, "wshard"),
            P("dp", "wshard", None),
        ),
        out_specs=(
            P(("dp", "wshard"), None),
            P(("dp", "wshard"), None),
            P(),
            P(),
            P(),
            P(None, None, "wshard"),
            P(None, "wshard"),
            P("dp", None, None, "wshard"),
            P("dp", "wshard", None),
        ),
        check_vma=False,
    )
```

profile of v0, /device:TPU:0, one launch (start us, length us, event | category | flops | bytes accessed | tf_op | source)
XLA Modules:
  0.0 823.3 jit_solution(8955648224389265078)
XLA Ops:
  8.7 6.4 copy.118
  17.4 10.8 %fusion.1 = f32[262144,16]{0,1:T(8,128)S(1)} fusion(f32[32,16]{0,1:T(8,128)S(1)} %copy-done.49, s32[262144]{0:T(1024)S(1)} %fusion.69), kind=kOutput, calls=%fused_computation.6 | convolution fusion | flops 1619001344 | bytes 17827840 | tf_op jit(solution)/shard_map/dot_general | solution.py:82
  28.3 19.1 %copy.142 = f32[2,8,512,512]{3,2,1,0:T(8,128)} copy(f32[2,8,512,512]{3,1,2,0:T(8,128)S(1)} %bitcast.182) | data formatting | bytes 33554432
  47.4 17.7 %copy.112 = f32[16,512,512]{1,2,0:T(8,128)} copy(f32[16,512,512]{2,1,0:T(8,128)} %bitcast.183) | data formatting | bytes 33554432 | tf_op jit(solution)/shard_map/reshape | solution.py:82
  66.1 2.3 reduce-window.6
  69.8 6.8 convert_bitcast_fusion.3
  77.9 1.3 copy.109
  79.8 1.9 copy.111
  81.7 11.8 %fusion.89 = (f32[16,512]{1,0:T(8,128)S(1)}, f32[16,512,512]{1,2,0:T(8,128)}) fusion(f32[16,512,512]{1,2,0:T(8,128)} %copy.112, bf16[512,16,64]{0,2,1:T(8,128)(2,1)S(1)} %bitcast.187, bf16[512,16,64]{0,2,1:T(8,128)(2,1)S(1)} %bitcast.184, pred[512,512]{0,1:T(8,128)(4,1)S(1)} %fusion.71), kind=kOutput, calls=%fused_computation.149 | convolution fusion | flops 553639936 | bytes 35946496 | tf_op jit(solution)/shard_map/while/body/eval_jaxpr/ihd,jhd->hij/dot_general | solution.py:88
  93.5 11.3 %fusion.5 = f32[16,512]{1,0:T(8,128)S(1)} fusion(f32[16,512,512]{1,2,0:T(8,128)} %get-tuple-element.129, f32[16,512]{1,0:T(8,128)S(1)} %get-tuple-element.128), kind=kLoop, calls=%fused_computation.21 | loop fusion | flops 8380416 | bytes 16842752 | tf_op jit(solution)/shard_map/while/body/eval_jaxpr/reduce_sum | solution.py:99
  105.5 7.7 fusion.60
  113.2 3.3 multiply_reduce_fusion.5
  116.6 1.3 copy-done.2
  119.2 2.2 reshape.426
  121.5 8.2 scatter_custom_fusion
  129.7 7.0 all-to-all-start
  137.3 3.1 mul.336
  140.4 6.1 mul.337
  148.4 8.4 %scatter_custom_fusion.1 = bf16[1280,1024]{1,0:T(8,128)(2,1)} fusion(s32[1024]{0:T(1024)S(1)} %bitcast.214, f32[1024,1024]{1,0:T(8,128)} %mul.337, f32[1024]{0:T(1024)S(1)} %div.49, bf16[]{:T(256)} %constant.98.clone.1), kind=kCustom, calls=%fused_computation.84 | custom fusion | flops 2097152 | bytes 6819842 | tf_op jit(solution)/shard_map/scatter | solution.py:164
  156.8 39.4 %all-to-all-done = bf16[8,160,1024]{2,1,0:T(8,128)(2,1)} async-done(((bf16[8,160,1024]{2,1,0:T(8,128)(2,1)}), bf16[8,160,1024]{2,1,0:T(8,128)(2,1)}, u32[]{:S(2)}, u32[]{:S(2)}) %all-to-all-start) | async-done | bytes 2621472 | tf_op jit(solution)/shard_map/all_to_all | solution.py:132
  196.2 3.8 all-to-all-start.2
  200.1 28.7 %copy.119 = bf16[1,2,1024,2816]{3,2,1,0:T(8,128)(2,1)} copy(bf16[1,2,1024,2816]{2,1,0,3:T(2,128)(2,1)} %all-gather.9.cloned.1.call-done) | data formatting | bytes 23068672 | tf_op jit(solution)/shard_map/all_gather | solution.py:136
  228.8 23.9 %convolution_bitcast_fusion = f32[2,1280,2816]{2,1,0:T(8,128)} fusion(bf16[1280,1024,1]{1,0,2:T(8,128)(2,1)} %bitcast.16, bf16[1,2,1024,2816]{3,2,1,0:T(8,128)(2,1)} %copy.119), kind=kOutput, calls=%fused_computation.12 | convolution fusion | flops 14763950080 | bytes 42991616 | tf_op jit(solution)/shard_map/rd,cdf->crf/dot_general | solution.py:139
  252.8 6.9 all-to-all-done.2
  259.7 27.5 %fusion.33 = (bf16[1,1280,2816]{2,1,0:T(8,128)(2,1)}, bf16[1,1280,2816]{2,1,0:T(8,128)(2,1)}) fusion(f32[2,1280,2816]{2,1,0:T(8,128)} %convolution_bitcast_fusion, bf16[1280,1024]{1,0:T(8,128)(2,1)S(1)} %bitcast.199, bf16[1,2816,1024]{2,1,0:T(8,128)(2,1)} %all-gather.11.cloned.1.call-done), kind=kOutput, calls=%fused_computation.55 | convolution fusion | flops 7482900480 | bytes 51642368 | tf_op jit(solution)/shard_map/rd,fd->rf/dot_general | solution.py:180
  287.2 22.1 %bitcast_convert_fusion = bf16[1280,1024]{1,0:T(8,128)(2,1)} fusion(bf16[1,2,1024,2816]{3,2,1,0:T(8,128)(2,1)} %copy.119, bf16[1,1280,2816]{2,1,0:T(8,128)(2,1)} %get-tuple-element.120, bf16[1,1280,2816]{2,1,0:T(8,128)(2,1)} %get-tuple-element.119), kind=kOutput, calls=%fused_computation.61 | convolution fusion | flops 14772469760 | bytes 28573696 | tf_op jit(solution)/shard_map/crf,cdf->rd/dot_general | solution.py:188
  309.3 3.7 all-to-all-start.3
  312.9 10.9 %fusion.15 = bf16[1,1280,2816]{2,1,0:T(8,128)(2,1)S(1)} fusion(f32[2,1280,2816]{2,1,0:T(8,128)} %convolution_bitcast_fusion), kind=kLoop, calls=%fused_computation.31 | loop fusion | flops 36044800 | bytes 36044800 | tf_op jit(solution)/shard_map/convert_element_type | solution.py:142
  323.9 2.9 copy-done.18
  326.8 10.8 %fusion.41 = bf16[1280,1024]{1,0:T(8,128)(2,1)} fusion(bf16[1,2816,1024]{2,1,0:T(8,128)(2,1)} %all-gather.11.cloned.1.call-done, bf16[1,1280,2816]{2,1,0:T(8,128)(2,1)S(1)} %fusion.15), kind=kOutput, calls=%fused_computation.65 | convolution fusion | flops 7383285760 | bytes 15597568 | tf_op jit(solution)/shard_map/dot_general | solution.py:143
  337.5 35.1 %all-to-all-done.3 = bf16[8,160,1024]{2,1,0:T(8,128)(2,1)S(1)} async-done(((bf16[8,160,1024]{2,1,0:T(8,128)(2,1)}), bf16[8,160,1024]{2,1,0:T(8,128)(2,1)S(1)}, u32[]{:S(2)}, u32[]{:S(2)}) %all-to-all-start.3) | async-done | bytes 2621472 | tf_op jit(solution)/shard_map/all_to_all | solution.py:199
  372.6 4.4 all-to-all-start.1
  377.0 2.8 convert_element_type.252
  379.9 5.3 gather_fusion.1
  385.2 5.4 reshape.405
  390.6 45.4 %all-to-all-done.1 = bf16[8,160,1024]{2,1,0:T(8,128)(2,1)} async-done(((bf16[8,160,1024]{2,1,0:T(8,128)(2,1)}), bf16[8,160,1024]{2,1,0:T(8,128)(2,1)}, u32[]{:S(2)}, u32[]{:S(2)}) %all-to-all-start.1) | async-done | bytes 2621472 | tf_op jit(solution)/shard_map/all_to_all | solution.py:144
  436.0 7.1 gather_fusion
  443.1 4.0 reshape.404
  447.1 10.8 %multiply_reduce_fusion.1 = (f32[512,2]{1,0:T(8,128)S(1)}, f32[512,1024]{1,0:T(8,128)}) fusion(f32[512,2,1024]{2,1,0:T(2,128)} %reshape.404, f32[512,1024]{1,0:T(8,128)} %convert_element_type.252, f32[512,2]{1,0:T(8,128)S(1)} %copy-done.25), kind=kLoop, calls=%fused_computation.62 | loop fusion | flops 3668992 | bytes 8396800 | tf_op jit(solution)/shard_map/reduce_sum | solution.py:158
  458.1 8.7 %reduce_sum.156 = f32[512,1024]{1,0:T(8,128)} reduce(f32[512,2,1024]{2,1,0:T(2,128)} %reshape.405, f32[]{:T(128)} %constant.35.clone.1), dimensions={1}, to_apply=%region_13.14 | reduce | flops 524288 | bytes 6291460 | tf_op jit(solution)/shard_map/reduce_sum | solution.py:206
  466.8 3.4 multiply_reduce_fusion.3
  470.2 1.7 multiply_add_fusion.2
  472.0 1.3 copy-done.16
  473.3 2.6 convolution_convert_fusion
  475.9 12.6 %convert_bitcast_fusion.2 = bf16[1,2816,1024]{2,1,0:T(8,128)(2,1)} fusion(bf16[1280,1024]{1,0:T(8,128)(2,1)S(1)} %bitcast.200, bf16[1,1280,2816]{2,1,0:T(8,128)(2,1)} %copy-done.18), kind=kOutput, calls=%fused_computation.60 | convolution fusion | flops 7384858624 | bytes 15597568 | tf_op jit(solution)/shard_map/rf,rd->fd/dot_general | solution.py:183
  490.1 2.9 convolution_convert_fusion.1
  493.7 8.9 %fusion.61 = bf16[16,64,512]{2,1,0:T(8,128)(2,1)S(1)} fusion(bf16[512,16,64]{0,2,1:T(8,128)(2,1)S(1)} %bitcast.189, f32[16,512,512]{1,2,0:T(8,128)} %get-tuple-element.129, f32[16,512]{1,0:T(8,128)S(1)} %log_add_fusion), kind=kOutput, calls=%fused_computation.99 | convolution fusion | flops 545783808 | bytes 18907136 | tf_op jit(solution)/shard_map/while/body/eval_jaxpr/hij,ihd->jhd/dot_general | solution.py:243
  502.6 1.3 copy.129
  503.9 8.3 %multiply_reduce_fusion = (f32[16,512]{1,0:T(8,128)S(1)}, f32[16,512,512]{1,2,0:T(8,128)S(1)}) fusion(f32[16,512,512]{1,2,0:T(8,128)} %get-tuple-element.129, f32[16,512]{1,0:T(8,128)S(1)} %log_add_fusion, bf16[512,16,64]{0,2,1:T(8,128)(2,1)} %bitcast.190, bf16[512,16,64]{0,2,1:T(8,128)(2,1)} %bitcast.193), kind=kOutput, calls=%fused_computation.14 | convolution fusion | flops 549445632 | bytes 35717120 | tf_op jit(solution)/shard_map/while/body/eval_jaxpr/ihd,jhd->hij/dot_general | solution.py:240
  512.3 9.9 %multiply_convert_fusion = bf16[16,512,512]{1,2,0:T(8,128)(2,1)S(1)} fusion(f32[16,512,512]{1,2,0:T(8,128)S(1)} %get-tuple-element.134, f32[16,512,512]{1,2,0:T(8,128)} %get-tuple-element.129, f32[16,512]{1,0:T(8,128)S(1)} %get-tuple-element.133, f32[16,512]{1,0:T(8,128)S(1)} %log_add_fusion), kind=kLoop, calls=%fused_computation.13 | loop fusion | flops 16777216 | bytes 42008576 | tf_op jit(solution)/shard_map/while/body/eval_jaxpr/convert_element_type | solution.py:246
  522.2 4.7 multiply_convert_fusion.4
  527.0 1.3 copy.128
  528.3 5.9 multiply_convert_fusion.5
  535.0 8.2 convert_bitcast_fusion.1
  543.2 22.0 %convert_bitcast_fusion = bf16[1,2,1024,2816]{2,3,1,0:T(8,128)(2,1)} fusion(bf16[1280,1024,1]{1,0,2:T(8,128)(2,1)} %bitcast.16, bf16[1,1280,2816]{2,1,0:T(8,128)(2,1)} %get-tuple-element.120, bf16[1,1280,2816]{2,1,0:T(8,128)(2,1)} %get-tuple-element.119), kind=kOutput, calls=%fused_computation.45 | convolution fusion | flops 14776926208 | bytes 28573696 | tf_op jit(solution)/shard_map/rd,crf->cdf/dot_general | solution.py:187
  565.3 15.8 %copy.144 = bf16[2,8,512,512]{3,1,2,0:T(8,128)(2,1)} copy(bf16[2,8,512,512]{2,3,1,0:T(8,128)(2,1)} %bitcast.180) | data formatting | bytes 16777216
  581.1 8.2 fusion.56
  589.9 5.2 fusion
  595.1 38.8 %all-reduce = (f32[2,1024]{1,0:T(2,128)}, f32[32,16]{0,1:T(8,128)}, f32[1024,8]{0,1:T(8,128)}) all-reduce(f32[2,1024]{1,0:T(2,128)S(1)} %pad_maximum_fusion.10, f32[32,16]{0,1:T(8,128)S(1)} %fusion, f32[1024,8]{0,1:T(8,128)S(1)} %fusion.93), channel_id=1, replica_groups=mesh['dp'=8,'wshard'=4] {'dp','wshard'}, use_global_device_ids=true, to_apply=%region_22.23 | all-reduce | flops 10752 | bytes 86016 | tf_op jit(solution)/shard_map/psum | solution.py:290
  634.0 4.2 fusion.55
  638.2 3.8 convert_element_type.279
  642.1 166.6 %all-reduce.3 = (f32[3,1024,256]{1,2,0:T(8,128)S(1)}, f32[1024,256]{1,0:T(8,128)}) all-reduce(bf16[3,1024,256]{1,2,0:T(8,128)(2,1)} %reduce-scatter.5.cloned.1.call-done, bf16[1024,256]{1,0:T(8,128)(2,1)} %reduce-scatter.7.cloned.1.call-done), channel_id=1, replica_groups=mesh['dp'=8,'wshard'=4] {'dp'}, use_global_device_ids=true, to_apply=%region_26.27 | all-reduce | flops 1048576 | bytes 6291456 | tf_op jit(solution)/shard_map/psum | solution.py:289
  808.6 2.4 copy.133
  811.0 5.1 convert_element_type.276
  (173 shorter events, 15.8 us)
Async XLA Ops:
  7.2 139.3 %copy-start = (bf16[1024,8]{0,1:T(8,128)(2,1)S(1)}, bf16[1024,8]{0,1:T(8,128)(2,1)}, u32[]{:S(2)}) copy-start(bf16[1024,8]{0,1:T(8,128)(2,1)} %param.17) | copy-start | bytes 49156
  7.2 62.3 %all-gather.5.cloned.1.call-start = ((), (), s32[]{:S(2)}) async-start(), calls=%async_computation.8 | async-start | bytes 7864320 | tf_op jit(solution)/shard_map/all_gather | solution.py:71
  7.9 105.3 %all-gather.7.cloned.1.call-start = ((), (), s32[]{:S(2)}) async-start(), calls=%async_computation.9 | async-start | bytes 2621440 | tf_op jit(solution)/shard_map/all_gather | solution.py:72
  8.7 6.6 copy-start.37
  8.7 191.4 %all-gather.9.cloned.1.call-start = ((), (), s32[]{:S(2)}) async-start(), calls=%async_computation.10 | async-start | bytes 14417920 | tf_op jit(solution)/shard_map/all_gather | solution.py:136
  15.7 1.6 copy-start.49
  17.4 10.8 %copy-start.19 = (s32[262144]{0:T(1024)}, s32[262144]{0:T(1024)S(1)}, u32[]{:S(2)}) copy-start(s32[262144]{0:T(1024)S(1)} %fusion.69) | copy-start | bytes 3145732
  47.3 21.5 %copy-start.12 = (bf16[512,1024]{1,0:T(8,128)(2,1)S(1)}, bf16[512,1024]{1,0:T(8,128)(2,1)}, u32[]{:S(2)}) copy-start(bf16[512,1024]{1,0:T(8,128)(2,1)} %param.11) | copy-start | bytes 3145732
  47.4 21.9 %copy-start.52 = (f32[2,1024]{1,0:T(2,128)S(1)}, f32[2,1024]{1,0:T(2,128)}, u32[]{:S(2)}) copy-start(f32[2,1024]{1,0:T(2,128)} %param.15) | copy-start | bytes 24580
  69.2 0.6 copy-start.50
  69.2 0.6 copy-start.47
  69.2 47.3 %copy-start.39 = (f32[1,1024]{1,0:T(1,128)}, f32[1,1024]{1,0:T(1,128)S(1)}, u32[]{:S(2)}) copy-start(f32[1,1024]{1,0:T(1,128)S(1)} %get-tuple-element.126) | copy-start | bytes 12292
  79.8 13.7 %copy-start.10 = (bf16[1,512,1024]{1,2,0:T(8,128)(2,1)}, bf16[1,512,1024]{1,2,0:T(8,128)(2,1)S(1)}, u32[]{:S(2)}) copy-start(bf16[1,512,1024]{1,2,0:T(8,128)(2,1)S(1)} %copy.110) | copy-start | bytes 3145732
  81.7 11.8 %copy-start.6 = (bf16[1,512,1024]{1,2,0:T(8,128)(2,1)}, bf16[1,512,1024]{1,2,0:T(8,128)(2,1)S(1)}, u32[]{:S(2)}) copy-start(bf16[1,512,1024]{1,2,0:T(8,128)(2,1)S(1)} %copy.111) | copy-start | bytes 3145732
  93.5 11.4 %copy-start.31 = (f32[16,512]{1,0:T(8,128)}, f32[16,512]{1,0:T(8,128)S(1)}, u32[]{:S(2)}) copy-start(f32[16,512]{1,0:T(8,128)S(1)} %get-tuple-element.128) | copy-start | bytes 98308
  93.5 12.0 %copy-start.21 = (bf16[1,512,1024]{1,2,0:T(8,128)(2,1)S(1)}, bf16[1,512,1024]{1,2,0:T(8,128)(2,1)}, u32[]{:S(2)}) copy-start(bf16[1,512,1024]{1,2,0:T(8,128)(2,1)} %copy.109) | copy-start | bytes 3145732
  104.9 0.6 copy-start.35
  113.2 3.4 copy-start.29
  116.5 1.4 copy-start.2
  116.5 1.4 copy-start.45
  118.1 28.3 %copy-start.4 = (bf16[512,1024]{1,0:T(8,128)(2,1)}, bf16[512,1024]{1,0:T(8,128)(2,1)S(1)}, u32[]{:S(2)}) copy-start(bf16[512,1024]{1,0:T(8,128)(2,1)S(1)} %multiply_convert_fusion.6) | copy-start | bytes 3145732
  121.5 15.8 %copy-start.8 = (bf16[512,1024]{1,0:T(8,128)(2,1)S(1)}, bf16[512,1024]{1,0:T(8,128)(2,1)}, u32[]{:S(2)}) copy-start(bf16[512,1024]{1,0:T(8,128)(2,1)} %param.12) | copy-start | bytes 3145732
  129.7 66.5 %all-to-all-start = ((bf16[8,160,1024]{2,1,0:T(8,128)(2,1)}), bf16[8,160,1024]{2,1,0:T(8,128)(2,1)}, u32[]{:S(2)}, u32[]{:S(2)}) async-start(bf16[8,160,1024]{2,1,0:T(8,128)(2,1)} %bitcast.186), calls=%async_computation | async-start | bytes 5242880 | tf_op jit(solution)/shard_map/all_to_all | solution.py:132
  136.7 116.1 %all-gather.11.cloned.1.call-start = ((), (), s32[]{:S(2)}) async-start(), calls=%async_computation.11 | async-start | bytes 7208960 | tf_op jit(solution)/shard_map/all_gather | solution.py:137
  146.9 0.6 copy-start.33
  146.9 0.6 copy-start.41
  148.2 48.0 %copy-start.24 = (f32[512,2]{1,0:T(8,128)}, f32[512,2]{1,0:T(8,128)S(1)}, u32[]{:S(2)}) copy-start(f32[512,2]{1,0:T(8,128)S(1)} %copy.114) | copy-start | bytes 12292
  196.2 63.4 %all-to-all-start.2 = ((bf16[8,160,1024]{2,1,0:T(8,128)(2,1)}), bf16[8,160,1024]{2,1,0:T(8,128)(2,1)S(1)}, u32[]{:S(2)}, u32[]{:S(2)}) async-start(bf16[8,160,1024]{2,1,0:T(8,128)(2,1)} %bitcast.23), calls=%async_computation.2 | async-start | bytes 5242880 | tf_op jit(solution)/shard_map/all_to_all | solution.py:167
  259.7 27.5 %copy-start.22 = (bf16[8,160,1024]{2,1,0:T(8,128)(2,1)}, bf16[8,160,1024]{2,1,0:T(8,128)(2,1)S(1)}, u32[]{:S(2)}) copy-start(bf16[8,160,1024]{2,1,0:T(8,128)(2,1)S(1)} %all-to-all-done.2) | copy-start | bytes 7864324
  309.3 63.3 %all-to-all-start.3 = ((bf16[8,160,1024]{2,1,0:T(8,128)(2,1)}), bf16[8,160,1024]{2,1,0:T(8,128)(2,1)S(1)}, u32[]{:S(2)}, u32[]{:S(2)}) async-start(bf16[8,160,1024]{2,1,0:T(8,128)(2,1)} %bitcast.202), calls=%async_computation.3 | async-start | bytes 5242880 | tf_op jit(solution)/shard_map/all_to_all | solution.py:199
  323.9 2.9 copy-start.18
  372.6 63.4 %all-to-all-start.1 = ((bf16[8,160,1024]{2,1,0:T(8,128)(2,1)}), bf16[8,160,1024]{2,1,0:T(8,128)(2,1)}, u32[]{:S(2)}, u32[]{:S(2)}) async-start(bf16[8,160,1024]{2,1,0:T(8,128)(2,1)} %bitcast.201), calls=%async_computation.1 | async-start | bytes 5242880 | tf_op jit(solution)/shard_map/all_to_all | solution.py:144
  377.0 261.2 %reduce-scatter.7.cloned.1.call-start = ((), (), s32[]{:S(2)}) async-start(), calls=%async_computation.13 | async-start | bytes 2621440 | tf_op jit(solution)/shard_map/reduce_scatter | solution.py:285
  443.1 4.0 copy-start.25
  447.1 11.0 %copy-start.34 = (f32[512,2]{0,1:T(2,128)S(1)}, f32[512,2]{0,1:T(2,128)}, u32[]{:S(2)}) copy-start(f32[512,2]{0,1:T(2,128)} %copy-done.33) | copy-start | bytes 12292
  447.1 11.0 %copy-start.42 = (f32[512]{0:T(512)S(1)}, f32[512]{0:T(512)}, u32[]{:S(2)}) copy-start(f32[512]{0:T(512)} %copy-done.41) | copy-start | bytes 6148
  447.1 11.0 %copy-start.44 = (f32[512]{0:T(512)S(1)}, f32[512]{0:T(512)}, u32[]{:S(2)}) copy-start(f32[512]{0:T(512)} %copy-done.43) | copy-start | bytes 6148
  447.1 11.0 %copy-start.38 = (s32[512,2]{0,1:T(2,128)S(1)}, s32[512,2]{0,1:T(2,128)}, u32[]{:S(2)}) copy-start(s32[512,2]{0,1:T(2,128)} %param.14) | copy-start | bytes 12292
  457.9 8.9 %copy-start.3 = (f32[512,1024]{1,0:T(8,128)S(1)}, f32[512,1024]{1,0:T(8,128)}, u32[]{:S(2)}) copy-start(f32[512,1024]{1,0:T(8,128)} %copy-done.2) | copy-start | bytes 6291460
  457.9 8.9 %copy-start.40 = (f32[1,1024]{1,0:T(1,128)S(1)}, f32[1,1024]{1,0:T(1,128)}, u32[]{:S(2)}) copy-start(f32[1,1024]{1,0:T(1,128)} %copy-done.39) | copy-start | bytes 12292
  457.9 8.9 %copy-start.46 = (f32[512]{0:T(512)S(1)}, f32[512]{0:T(512)}, u32[]{:S(2)}) copy-start(f32[512]{0:T(512)} %copy-done.45) | copy-start | bytes 6148
  466.8 3.4 copy-start.9
  466.8 3.4 copy-start.15
  470.2 3.1 copy-start.30
  471.9 1.3 copy-start.16
  473.3 2.7 copy-start.23
  475.9 162.3 %reduce-scatter.11.cloned.1.call-start = ((), (), s32[]{:S(2)}) async-start(), calls=%async_computation.15 | async-start | bytes 7208960 | tf_op jit(solution)/shard_map/reduce_scatter | solution.py:195
  488.5 0.8 copy-start.32
  488.5 0.8 copy-start.36
  488.5 1.6 copy-start.17
  488.5 153.5 %reduce-scatter.5.cloned.1.call-start = ((), (), s32[]{:S(2)}) async-start(), calls=%async_computation.12 | async-start | bytes 7864320 | tf_op jit(solution)/shard_map/reduce_scatter | solution.py:282
  493.7 8.9 %copy-start.11 = (bf16[512,1024]{0,1:T(8,128)(2,1)}, bf16[512,1024]{0,1:T(8,128)(2,1)S(1)}, u32[]{:S(2)}) copy-start(bf16[512,1024]{0,1:T(8,128)(2,1)S(1)} %copy.123) | copy-start | bytes 3145732
  522.2 4.8 copy-start.1
  522.2 6.1 copy-start.7
  528.3 6.7 copy-start.13
  528.3 6.7 copy-start.48
  528.3 6.7 copy-start.51
  535.0 8.2 copy-start.28
  543.2 267.8 %reduce-scatter.9.cloned.1.call-start = ((), (), s32[]{:S(2)}) async-start(), calls=%async_computation.14 | async-start | bytes 14417920 | tf_op jit(solution)/shard_map/reduce_scatter | solution.py:192
  565.3 15.8 %copy-start.26 = (bf16[1,512,1024]{2,1,0:T(8,128)(2,1)S(1)}, bf16[1,512,1024]{2,1,0:T(8,128)(2,1)}, u32[]{:S(2)}) copy-start(bf16[1,512,1024]{2,1,0:T(8,128)(2,1)} %copy.129) | copy-start | bytes 3145732
  565.3 15.8 %copy-start.27 = (bf16[1,512,1024]{2,1,0:T(8,128)(2,1)S(1)}, bf16[1,512,1024]{2,1,0:T(8,128)(2,1)}, u32[]{:S(2)}) copy-start(bf16[1,512,1024]{2,1,0:T(8,128)(2,1)} %copy.128) | copy-start | bytes 3145732
  581.1 8.3 %copy-start.5 = (bf16[512,1024]{1,0:T(8,128)(2,1)S(1)}, bf16[512,1024]{1,0:T(8,128)(2,1)}, u32[]{:S(2)}) copy-start(bf16[512,1024]{1,0:T(8,128)(2,1)} %copy-done.4) | copy-start | bytes 3145732
  581.1 8.8 %copy-start.14 = (bf16[2,8,512,512]{3,1,2,0:T(8,128)(2,1)S(1)}, bf16[2,8,512,512]{3,1,2,0:T(8,128)(2,1)}, u32[]{:S(2)}) copy-start(bf16[2,8,512,512]{3,1,2,0:T(8,128)(2,1)} %copy.144) | copy-start | bytes 25165828
  581.1 8.8 %copy-start.20 = (s32[262144]{0:T(1024)S(1)}, s32[262144]{0:T(1024)}, u32[]{:S(2)}) copy-start(s32[262144]{0:T(1024)} %copy-done.19) | copy-start | bytes 3145732
  (1 other events, 0.5 us)
Sparse Core Ops, SparseCore 0:
  9.6 49.9 all-gather.4
  61.1 22.8 all-gather.6
  86.1 76.1 all-gather.8
  163.7 43.3 all-gather.10
  476.0 30.4 reduce-scatter.6
  509.6 54.8 reduce-scatter.10
  567.1 59.1 reduce-scatter.4
  629.0 92.2 reduce-scatter.8
where the time goes:
time: 830 us; the launch traced here: 823 us
  matrix products  219 us (26%)
  blocking collectives  205 us (25%)
  local copies, waits for them, and re-layouts  153 us (18%)
  waiting for transfers between devices  129 us (16%)
  other arithmetic  82.4 us (10%)
  starting transfers between devices  19.2 us (2%)
  between operations  16 us (2%)
    psum x1, blocking collectives, per_device(): grad_attn_qkv, grad_attn_out = lax.psum((qkv_part, out_part), 'dp')  167 us
    unnamed x113, local copies, waits for them, and re-layouts  53.5 us
    all_to_all x1, waiting for transfers between devices, per_device(): lax.all_to_all(made.reshape(expert_count, capacity, model_width), 'dp', s...  45.4 us
    all_to_all x1, waiting for transfers between devices, per_device(): lax.all_to_all(outgoing, 'dp', split_axis=0, concat_axis=0, tiled=True)  39.4 us
    psum x1, blocking collectives, per_device(): lax.psum((jnp.stack([grad_gain_one, grad_gain_two]), grad_table_local, gr...  38.8 us
    all_to_all x1, waiting for transfers between devices, per_device(): lax.all_to_all(grad_rows.reshape(expert_count, capacity, model_width), 'd...  35.1 us
    all_gather x1, local copies, waits for them, and re-layouts, per_device(): lax.all_gather(expert_in, 'wshard', axis=3, tiled=True)  28.7 us
    dot_general x1, matrix products, per_device(): jnp.einsum('rd,fd->rf', grad_arrived, weights_down_back[0], preferred_ele...  27.5 us
  transfers between devices with their start and end apart: 12, of which 4 were waited for; matrix products, arithmetic and copies ran while one was open for 43% of the time, Pallas kernels for 0%

commit v1 on v0

v1 whole, which is shorter than its diff:
```python
import functools

import jax
import jax.numpy as jnp
import numpy as np
from jax import lax
from jax.experimental import pallas as pl
from jax.experimental.pallas import tpu as pltpu
from jax.sharding import PartitionSpec as P

PIC = 256
PRECISE = lax.Precision.HIGHEST
EPSILON = 1e-06
MASKED_SCORE = -1e30
BUCKET_EDGES = (8, 11, 16, 23, 32, 45, 64, 91)
TILE = 128
F32 = jnp.float32
BF16 = jnp.bfloat16
I32 = jnp.int32
VMEM = pl.BlockSpec(memory_space=pltpu.VMEM)
SMEM = pl.BlockSpec(memory_space=pltpu.SMEM)
ANY = pl.BlockSpec(memory_space=pl.ANY)
LIGHT = 1024
EXTRA = 8


def dot_nn(a, b):
    return lax.dot_general(a, b, (((1,), (0,)), ((), ())), preferred_element_type=F32)


def dot_nt(a, b):
    return lax.dot_general(a, b, (((1,), (1,)), ((), ())), preferred_element_type=F32)


def dot_tn(a, b):
    return lax.dot_general(a, b, (((0,), (0,)), ((), ())), preferred_element_type=F32)


def iota(shape, axis):
    return lax.broadcasted_iota(I32, shape, axis)


def shape_of(shape, dtype):
    return jax.ShapeDtypeStruct(shape, dtype)


def call(body, out, args, specs, scratch=(), name=None):
    return pl.pallas_call(
        body,
        out_shape=out,
        in_specs=specs,
        out_specs=jax.tree.map(lambda _: VMEM, out),
        scratch_shapes=list(scratch),
        cost_estimate=pl.CostEstimate(flops=LIGHT, bytes_accessed=LIGHT, transcendentals=0),
        name=name,
    )(*args)


def bucket_of(offset):
    magnitude = np.abs(offset)
    coarse = 7 + sum((magnitude >= bound).astype(np.int32) for bound in BUCKET_EDGES)
    return np.where(magnitude < 8, magnitude, coarse) + 16 * (offset < 0)


def diagonal_ones(bucket_count):
    column = np.arange(2 * TILE)
    signed = np.where(column < TILE, column, column - 2 * TILE)
    offsets = np.concatenate([TILE * step - signed for step in (-1, 0, 1)])
    used = np.tile(column != TILE, 3)
    hit = bucket_of(offsets)[None, :] == np.arange(bucket_count)[:, None]
    near = (hit & used[None, :]).astype(np.float32)
    far = np.zeros((bucket_count, 2 * TILE), np.float32)
    far[bucket_of(np.array(TILE)), :TILE] = 1
    far[bucket_of(np.array(-TILE)), TILE:] = 1
    return np.concatenate([near, far], 1)


def onehot_rows(first, count, slots_row):
    index = iota((count, slots_row.shape[1]), 0) + first
    hit = (index == slots_row[0:1, :]) | (index == slots_row[1:2, :])
    return hit.astype(F32).astype(BF16)


def onehot_columns(slots_column, first, count):
    index = iota((slots_column.shape[0], count), 1) + first
    return index == slots_column


def place_rows(slots_row, rows, out_ref):
    total = out_ref.shape[0]
    step = 256
    for first in range(0, total, step):
        size = min(step, total - first)
        hit = onehot_rows(first, size, slots_row)
        out_ref[first : first + size, :] = dot_nn(hit, rows).astype(BF16)


def route_body(experts, capacity, routes_ref, cot_ref, row_ref, col_ref, out_ref):
    tokens = cot_ref.shape[0]
    first, second = iota((tokens, tokens), 0), iota((tokens, tokens), 1)
    routes = routes_ref[...]
    label = iota((experts, tokens), 0)
    hits = ((routes[0:1] == label) | (routes[1:2] == label)).astype(F32).astype(BF16)
    before = dot_nn(hits, (first < second).astype(F32).astype(BF16))
    slots = []
    for k in range(2):
        own = jnp.sum(jnp.where(routes[k : k + 1] == label, before, 0.0), 0, keepdims=True)
        slots.append(own.astype(I32) + routes[k : k + 1] * capacity)
    slots += [slots[k] + routes[k : k + 1] * EXTRA for k in range(2)]
    slots = jnp.concatenate(slots + slots, 0)
    row_ref[...] = slots
    col_ref[...] = slots.astype(F32).T.astype(I32)
    place_rows(slots, cot_ref[...], out_ref)


def route(routes, cotangent, experts, capacity):
    tokens, width = cotangent.shape
    total = experts * capacity
    return call(
        functools.partial(route_body, experts, capacity),
        (
            shape_of((8, tokens), I32),
            shape_of((tokens, 8), I32),
            shape_of((total, width), BF16),
        ),
        (routes.T, cotangent),
        [VMEM] * 2,
        name="route",
    )


def unit_norm(values):
    recip = lax.rsqrt(jnp.mean(values * values, -1, keepdims=True) + EPSILON)
    return values * recip, recip


def fill_mask(mask_ref, span_start):
    size = mask_ref.shape[0]
    i, j = iota((size, size), 0), iota((size, size), 1)

    def inside(p):
        return (p >= span_start) & (p < span_start + PIC)

    visible = (j <= i) | (inside(i) & inside(j))
    mask_ref[...] = jnp.where(visible, 0.0, MASKED_SCORE)


def head_lanes(which, size):
    lane = iota((1, 2 * size), 1)
    return ((lane >= size) == (which == 1)).astype(F32).astype(BF16)


def bias_tiles(diag_row):
    tiles = []
    for step in range(3):
        row = diag_row[:, 2 * TILE * step : 2 * TILE * (step + 1)]
        wide = jnp.broadcast_to(row, (TILE, 2 * TILE))
        tiles.append(pltpu.roll(wide, 0, 1, stride=1, stride_axis=0)[:, :TILE])
    return tiles, (diag_row[:, 6 * TILE : 7 * TILE], diag_row[:, 7 * TILE :])


def score_tiles(block, query, keys, tiles, far, mask_ref):
    raw = dot_nt(query, keys)
    rows = slice(block * TILE, (block + 1) * TILE)
    result = []
    for other in range(keys.shape[0] // TILE):
        piece = raw[:, other * TILE : (other + 1) * TILE]
        step = block - other
        piece = piece + (far[0] if step >= 2 else far[1] if step <= -2 else tiles[step + 1])
        if step <= 0:
            piece = piece + mask_ref[rows, other * TILE : (other + 1) * TILE]
        result.append(piece)
    return result


def softmax_tiles(pieces):
    top = functools.reduce(jnp.maximum, pieces)
    top = jnp.max(top, -1, keepdims=True)
    powers = [jnp.exp(piece - top) for piece in pieces]
    total = jnp.sum(functools.reduce(jnp.add, powers), -1, keepdims=True)
    scale = 1.0 / total
    return [power * scale for power in powers]


def attend_body(
    group, head_size, where_ref, x_ref, gain_ref, diag_ref, w_ref, qkv_ref, mix_ref,
    norm_ref, mask_ref,
):
    count = x_ref.shape[0]
    fill_mask(mask_ref, where_ref[1])
    unit, _ = unit_norm(x_ref[...].astype(F32))
    norm_ref[...] = (unit * gain_ref[0:1, :]).astype(BF16)
    for c in range(3):
        qkv_ref[c] = dot_nn(norm_ref[...], w_ref[c]).astype(BF16)
    width = 2 * head_size
    heads = w_ref.shape[2] // head_size
    first_head = (where_ref[0] ^ group) * heads

    def pair(p, carry):
        lanes = pl.ds(pl.multiple_of(p * width, width), width)
        query, keys, value = qkv_ref[0, :, lanes], qkv_ref[1, :, lanes], qkv_ref[2, :, lanes]
        mixed = [None] * (count // TILE)
        for which in range(2):
            head = first_head + 2 * p + which
            own = head_lanes(which, head_size)
            own_query, own_value = query * (own * 0.125), value * own
            tiles, far = bias_tiles(diag_ref[pl.ds(head, 1), :])
            for block in range(count // TILE):
                rows = slice(block * TILE, (block + 1) * TILE)
                pieces = score_tiles(block, own_query[rows], keys, tiles, far, mask_ref)
                probs = jnp.concatenate([t.astype(BF16) for t in softmax_tiles(pieces)], 1)
                part = dot_nn(probs, own_value)
                mixed[block] = part if which == 0 else mixed[block] + part
        for block in range(count // TILE):
            rows = slice(block * TILE, (block + 1) * TILE)
            mix_ref[rows, lanes] = mixed[block].astype(BF16)
        return carry

    lax.fori_loop(0, heads // 2, pair, 0)


def attend(group, where, tokens, gains, diag, weights, head_size):
    count, width = tokens.shape
    cols = weights.shape[2]
    return call(
        functools.partial(attend_body, group, head_size),
        (shape_of((3, count, cols), BF16), shape_of((count, cols), BF16)),
        (where, tokens, gains, diag, weights),
        [SMEM] + [VMEM] * 4,
        [pltpu.VMEM((count, width), BF16), pltpu.VMEM((count, count), F32)],
        name="attend",
    )


def attend_back_body(
    group, head_size, where_ref, x_ref, gain_ref, diag_ref, w_ref, qkv_ref, mixgrad_ref,
    sum_ref, wgrad_ref, sum_out_ref, diag_out_ref, norm_t_ref, mask_ref, grads_ref, probs_ref,
    scores_ref,
):
    count = x_ref.shape[0]
    blocks = count // TILE
    fill_mask(mask_ref, where_ref[1])
    unit, _ = unit_norm(x_ref[...].astype(F32))
    norm_t_ref[...] = (unit * gain_ref[0:1, :]).astype(BF16).T
    width = 2 * head_size
    cols = w_ref.shape[2]
    heads = cols // head_size
    place = where_ref[0] ^ group

    def pair(p, carry):
        offset = pl.multiple_of(p * width, width)
        lanes = pl.ds(offset, width)
        query, keys, value = qkv_ref[0, :, lanes], qkv_ref[1, :, lanes], qkv_ref[2, :, lanes]
        outer = mixgrad_ref[:, pl.ds(pl.multiple_of(place * cols + offset, width), width)]
        query_sum, key_sum, value_sum = [None] * blocks, None, None
        for which in range(2):
            head = place * heads + 2 * p + which
            own = head_lanes(which, head_size)
            own_query, own_key, own_outer = query * own, keys * own, outer * own
            scaled = own_query * 0.125
            tiles, far = bias_tiles(diag_ref[pl.ds(head, 1), :])
            near_sums, far_sums = [None] * 3, [None] * 2
            for block in range(blocks):
                rows = slice(block * TILE, (block + 1) * TILE)
                probs = softmax_tiles(
                    score_tiles(block, scaled[rows], keys, tiles, far, mask_ref)
                )
                prob_grads = dot_nt(own_outer[rows], value)
                prob_grads = [
                    prob_grads[:, j * TILE : (j + 1) * TILE] for j in range(blocks)
                ]
                delta = functools.reduce(
                    jnp.add, [a * b for a, b in zip(probs, prob_grads)]
                )
                delta = jnp.sum(delta, -1, keepdims=True)
                low = [(a * (b - delta)).astype(BF16) for a, b in zip(probs, prob_grads)]
                for other in range(blocks):
                    step = block - other
                    wide = low[other].astype(F32)
                    if abs(step) >= 2:
                        side = 0 if step > 0 else 1
                        old = far_sums[side]
                        far_sums[side] = wide if old is None else old + wide
                    else:
                        old = near_sums[step + 1]
                        near_sums[step + 1] = wide if old is None else old + wide
                probs_ref[which, rows, :] = jnp.concatenate([t.astype(BF16) for t in probs], 1)
                low = jnp.concatenate(low, 1)
                scores_ref[which, rows, :] = low
                part = dot_nn(low, own_key)
                query_sum[block] = part if which == 0 else query_sum[block] + part
            part = dot_tn(scores_ref[which], own_query)
            key_sum = part if which == 0 else key_sum + part
            part = dot_tn(probs_ref[which], own_outer)
            value_sum = part if which == 0 else value_sum + part
            local = 2 * p + which
            for step in range(3):
                wide = jnp.concatenate([near_sums[step], jnp.zeros((TILE, TILE), F32)], 1)
                half = TILE // 2
                while half:
                    turned = pltpu.roll(wide[half:], 2 * TILE - half, 1)
                    wide = wide[:half] + turned
                    half //= 2
                for side in range(2):
                    spot = 2 * step + side
                    diag_out_ref[local, spot : spot + 1, :] = wide[:, TILE * side : TILE * (side + 1)]
            for side in range(2):
                diag_out_ref[local, 6 + side : 7 + side, :] = jnp.sum(
                    far_sums[side], 0, keepdims=True
                )
        for block in range(blocks):
            rows = slice(block * TILE, (block + 1) * TILE)
            grads_ref[0, rows, lanes] = (query_sum[block] * 0.125).astype(BF16)
        grads_ref[1, :, lanes] = (key_sum * 0.125).astype(BF16)
        grads_ref[2, :, lanes] = value_sum.astype(BF16)
        return carry

    lax.fori_loop(0, heads // 2, pair, 0)
    total = sum_ref[...] if sum_ref is not None else None
    for c in range(3):
        wgrad_ref[c] = dot_nn(norm_t_ref[...], grads_ref[c]).astype(BF16)
        part = dot_nt(grads_ref[c], w_ref[c])
        total = part if total is None else total + part
    sum_out_ref[...] = total


def attend_back(
    group, where, tokens, gains, diag, weights, qkv, mixed_grad, total, head_size
):
    count, width = tokens.shape
    cols = weights.shape[2]
    heads = cols // head_size
    body = functools.partial(attend_back_body, group, head_size)
    args = (where, tokens, gains, diag, weights, qkv, mixed_grad)
    specs = [SMEM] + [VMEM] * 6
    if total is None:
        full = body

        def body(*refs):
            full(*refs[:7], None, *refs[7:])

    else:
        args, specs = args + (total,), specs + [VMEM]
    return call(
        body,
        (
            shape_of((3, width, cols), BF16),
            shape_of((count, width), F32),
            shape_of((heads, 8, TILE), F32),
        ),
        args,
        specs,
        [
            pltpu.VMEM((width, count), BF16),
            pltpu.VMEM((count, count), F32),
            pltpu.VMEM((3, count, cols), BF16),
            pltpu.VMEM((2, count, count), BF16),
            pltpu.VMEM((2, count, count), BF16),
        ],
        name="attend_back",
    )


def gather_lanes(refs, place, out_ref):
    for group, ref in enumerate(refs):
        cols = ref.shape[1]
        spot = pl.multiple_of((place ^ group) * cols, cols)
        out_ref[:, pl.ds(spot, cols)] = ref[...]


def split_three(value):
    high = value.astype(BF16).astype(F32)
    middle = (value - high).astype(BF16).astype(F32)
    return high, middle, value - high - middle


def dispatch_body(
    groups, experts, where_ref, x_ref, gain_ref, router_ref, row_ref, col_ref, *refs
):
    mix_refs, out_refs = refs[:groups], refs[groups : 2 * groups]
    hidden_ref, norm_ref, gate_ref, sent_ref, mixed_ref = refs[2 * groups :]
    place = where_ref[0]
    gather_lanes(mix_refs, place, mixed_ref)
    for group in range(groups):
        cols = out_refs[group].shape[1]
        lanes = pl.ds(pl.multiple_of((place ^ group) * cols, cols), cols)
        branch = dot_nn(mixed_ref[...], out_refs[group][...])
        hidden_ref[:, lanes] = x_ref[:, lanes].astype(F32) + branch
    unit, _ = unit_norm(hidden_ref[...])
    norm_ref[...] = (unit * gain_ref[1:2, :]).astype(BF16)
    place_rows(row_ref[2:4, :], norm_ref[...], sent_ref)
    logits = dot_nt(norm_ref[...], router_ref[...])
    stride = sent_ref.shape[0] // experts
    capacity = stride - EXTRA
    slots = [col_ref[:, k : k + 1] for k in range(2)]
    lane = iota(logits.shape, 1)
    chosen = []
    for k in range(2):
        own = (lane * capacity <= slots[k]) & (slots[k] < (lane + 1) * capacity)
        chosen.append(jnp.sum(jnp.where(own, logits, 0.0), -1, keepdims=True))
    top = jnp.maximum(chosen[0], chosen[1])
    powers = [jnp.exp(c - top) for c in chosen]
    gates = [power / (powers[0] + powers[1]) for power in powers]
    for k in range(2):
        gate_ref[:, k : k + 1] = gates[k]
    span = -(-capacity // TILE) * TILE
    lane = iota((slots[0].shape[0], span), 1)
    below = iota((EXTRA, span), 0)
    for expert in range(experts):
        label = jnp.where(lane < capacity, lane + expert * capacity, -1)
        part = 0.0
        for k in range(2):
            part = part + jnp.where(label == slots[k], gates[k], 0.0)
        high, middle, low = split_three(jnp.sum(part, 0, keepdims=True))
        block = jnp.where(
            below == 0, high, jnp.where(below == 1, middle, jnp.where(below == 2, low, 0.0))
        )
        first = expert * stride + capacity
        sent_ref[first : first + EXTRA, :span] = block.astype(BF16)


def dispatch(where, tokens, gains, router_t, slots_row, slots_col, mixed, out_weights, capacity):
    count, width = tokens.shape
    groups = len(mixed)
    experts = router_t.shape[0]
    return call(
        functools.partial(dispatch_body, groups, experts),
        (
            shape_of((count, width), F32),
            shape_of((count, width), BF16),
            shape_of((count, 2), F32),
            shape_of((experts * (capacity + EXTRA), width), BF16),
        ),
        (where, tokens, gains, router_t, slots_row, slots_col, *mixed, *out_weights),
        [SMEM] + [VMEM] * (5 + 2 * groups),
        [pltpu.VMEM((count, width), BF16)],
        name="dispatch",
    )


def combine_body(hidden_ref, gate_ref, col_ref, rows_ref, out_ref):
    count = out_ref.shape[0]
    total = rows_ref.shape[0]
    step = min(count, 256)
    for first in range(0, count, step):
        part = slice(first, first + step)
        result = hidden_ref[part, :]
        for k in range(2):
            hit = onehot_columns(col_ref[part, k : k + 1], 0, total).astype(F32).astype(BF16)
            result = result + gate_ref[part, k : k + 1] * dot_nn(hit, rows_ref[...])
        out_ref[part, :] = result.astype(BF16)


def combine(hidden, gates, slots_col, rows):
    count, width = hidden.shape
    return call(
        combine_body,
        shape_of((count, width), BF16),
        (hidden, gates, slots_col, rows),
        [VMEM] * 4,
        name="combine",
    )


def undispatch_body(
    groups, experts, where_ref, gain_ref, router_ref, col_ref, gate_ref, gate_grad_ref, hidden_ref,
    norm_ref, cot_ref, rows_ref, *refs
):
    mix_refs, out_refs = refs[:groups], refs[groups : 2 * groups]
    grad_ref, mixgrad_ref, router_grad_ref, gain_grad_ref = refs[2 * groups : 2 * groups + 4]
    wgrad_refs = refs[2 * groups + 4 : 3 * groups + 4]
    mixed_ref, branch_ref = refs[3 * groups + 4 :]
    place = where_ref[0]
    total = rows_ref.shape[0]
    capacity = total // experts - EXTRA
    gates = [gate_ref[:, k : k + 1] for k in range(2)]
    slots = [col_ref[:, k : k + 1] for k in range(2)]
    gate_grads = []
    hits = None
    for k in range(2):
        hit = onehot_columns(slots[k], 0, gate_grad_ref.shape[1])
        picked = jnp.where(hit, gate_grad_ref[...], 0.0)
        gate_grads.append(jnp.sum(picked, -1, keepdims=True))
        hit = onehot_columns(col_ref[:, 2 + k : 3 + k], 0, total)
        hits = hit if hits is None else hits | hit
    hits = hits.astype(F32).astype(BF16)
    mean = gates[0] * gate_grads[0] + gates[1] * gate_grads[1]
    lane = iota((gates[0].shape[0], 3 * experts), 1)
    part = (lane >= experts).astype(I32) + (lane >= 2 * experts).astype(I32)
    label = lane - part * experts
    logit_grads = 0.0
    for k in range(2):
        own = (label * capacity <= slots[k]) & (slots[k] < (label + 1) * capacity)
        logit_grads = logit_grads + jnp.where(own, gates[k] * (gate_grads[k] - mean), 0.0)
    high, middle, low = split_three(logit_grads)
    split = jnp.where(part == 0, high, jnp.where(part == 1, middle, low)).astype(BF16)
    norm_grad = dot_nn(hits, rows_ref[...]) + dot_nn(split, router_ref[...])
    router_grad = dot_tn(split, norm_ref[...])
    router_grad_ref[...] = (
        router_grad[:experts] + router_grad[experts : 2 * experts] + router_grad[2 * experts :]
    )
    unit, recip = unit_norm(hidden_ref[...])
    gain_grad_ref[...] = jnp.sum(norm_grad * unit, 0, keepdims=True)
    scaled = norm_grad * gain_ref[1:2, :]
    back = recip * (scaled - unit * jnp.mean(scaled * unit, -1, keepdims=True))
    grad_ref[...] = cot_ref[...].astype(F32) + back
    branch_ref[...] = grad_ref[...].astype(BF16)
    gather_lanes(mix_refs, place, mixed_ref)
    mixed_t = mixed_ref[...].T
    result = 0.0
    for group in range(groups):
        cols = out_refs[group].shape[1]
        lanes = pl.ds(pl.multiple_of((place ^ group) * cols, cols), cols)
        branch = branch_ref[:, lanes]
        result = result + dot_nt(branch, out_refs[group][...])
        wgrad_refs[group][...] = dot_nn(mixed_t, branch).astype(BF16)
    mixgrad_ref[...] = result.astype(BF16)


def undispatch(
    where, gains, router_t3, slots_col, gates, gate_grads, hidden, normed, cotangent, rows, mixed,
    out_weights,
):
    count, width = hidden.shape
    groups = len(mixed)
    experts = router_t3.shape[0] // 3
    args = (where, gains, router_t3, slots_col, gates, gate_grads, hidden, normed, cotangent, rows)
    result = call(
        functools.partial(undispatch_body, groups, experts),
        (
            shape_of((count, width), F32),
            shape_of((count, width), BF16),
            shape_of((experts, width), F32),
            shape_of((1, width), F32),
        )
        + tuple(shape_of(w.shape, BF16) for w in out_weights),
        (*args, *mixed, *out_weights),
        [SMEM] + [VMEM] * (9 + 2 * groups),
        [pltpu.VMEM((count, width), BF16)] * 2,
        name="undispatch",
    )
    return result[:4], list(result[4:])


def finish_body(x_ref, gain_ref, norm_grad_ref, grad_ref, out_ref, gain_grad_ref):
    unit, recip = unit_norm(x_ref[...].astype(F32))
    norm_grad = norm_grad_ref[...]
    gain_grad_ref[...] = jnp.sum(norm_grad * unit, 0, keepdims=True)
    scaled = norm_grad * gain_ref[0:1, :]
    back = recip * (scaled - unit * jnp.mean(scaled * unit, -1, keepdims=True))
    out_ref[...] = (grad_ref[...] + back).astype(BF16)


def finish(tokens, gains, norm_grad, grad):
    count, width = tokens.shape
    return call(
        finish_body,
        (shape_of((count, width), BF16), shape_of((1, width), F32)),
        (tokens, gains, norm_grad, grad),
        [VMEM] * 4,
        name="finish",
    )


def expert_body(groups, chunk, rows_ref, outer_ref, gate_ref, *refs):
    in_refs, down_refs = refs[:groups], refs[groups : 2 * groups]
    made_ref, back_ref, outer_out_ref, gate_grad_ref = refs[2 * groups : 2 * groups + 4]
    act_ref, low_ref, buf_ref, sems = refs[2 * groups + 4 :]
    share = down_refs[0].shape[0]
    hidden = share * groups

    def copies(group):
        spot = pl.ds(group * share, share)
        return (
            pltpu.make_async_copy(in_refs[group], buf_ref.at[0:2, spot], sems.at[2 * group]),
            pltpu.make_async_copy(down_refs[group], buf_ref.at[2, spot], sems.at[2 * group + 1]),
        )

    @pl.when(pl.program_id(0) == 0)
    def _():
        for group in range(groups):
            for copy in copies(group):
                copy.start()

    rows = rows_ref[...]
    low_outer = (outer_ref[...].astype(F32) * gate_ref[...]).astype(BF16)
    outer_out_ref[...] = low_outer

    @pl.when(pl.program_id(0) == 0)
    def _():
        for group in range(groups):
            for copy in copies(group):
                copy.wait()

    for first in range(0, hidden, chunk):
        part = slice(first, first + chunk)
        gate, up = dot_nt(rows, buf_ref[0, part, :]), dot_nt(rows, buf_ref[1, part, :])
        act_grad = dot_nt(low_outer, buf_ref[2, part, :])
        square = gate * gate
        inner = gate * (0.7978845608028654 + (0.7978845608028654 * 0.044715) * square)
        rise = 0.5 + 0.5 * jnp.tanh(inner)
        bent = gate * rise
        act_ref[:, part] = (bent * up).astype(BF16)
        slope = rise + bent * (1.0 - rise) * (
            2 * 0.7978845608028654 + (6 * 0.7978845608028654 * 0.044715) * square
        )
        low_ref[0, :, part] = (act_grad * up * slope).astype(BF16)
        low_ref[1, :, part] = (act_grad * bent).astype(BF16)
    made = dot_nn(act_ref[...], buf_ref[2]).astype(BF16)
    made_ref[...] = made
    back = dot_nn(low_ref[0], buf_ref[0]) + dot_nn(low_ref[1], buf_ref[1])
    back_ref[...] = back.astype(BF16)
    gate_grad_ref[...] = jnp.sum(
        outer_ref[...].astype(F32) * made.astype(F32), -1, keepdims=True
    )


def experts_pass(rows, outer, gate_column, in_weights, down_weights, block=320, chunk=256):
    total, width = rows.shape
    groups = len(in_weights)
    hidden = down_weights[0].shape[0] * groups
    row_spec = pl.BlockSpec((block, width), lambda i: (i, 0))
    column = pl.BlockSpec((block, 1), lambda i: (i, 0))
    wide = pl.BlockSpec((block, hidden), lambda i: (i, 0))
    both = pl.BlockSpec((2, block, hidden), lambda i: (0, i, 0))
    return pl.pallas_call(
        functools.partial(expert_body, groups, chunk),
        grid=(total // block,),
        out_shape=(
            shape_of((total, width), BF16),
            shape_of((total, width), BF16),
            shape_of((total, width), BF16),
            shape_of((total, 1), F32),
            shape_of((total, hidden), BF16),
            shape_of((2, total, hidden), BF16),
        ),
        in_specs=[row_spec, row_spec, column] + [ANY] * (2 * groups),
        out_specs=(row_spec, row_spec, row_spec, column, wide, both),
        scratch_shapes=[
            pltpu.VMEM((3, hidden, width), BF16),
            pltpu.SemaphoreType.DMA((2 * groups,)),
        ],
        cost_estimate=pl.CostEstimate(flops=LIGHT, bytes_accessed=LIGHT, transcendentals=0),
        name="experts",
    )(rows, outer, gate_column, *in_weights, *down_weights)


def swap(value, axis, bit):
    size = lax.axis_size(axis)
    return lax.ppermute(value, axis, [(i, i ^ bit) for i in range(size)])


def bits_of(axis):
    size = lax.axis_size(axis)
    return [1 << b for b in range(size.bit_length() - 1)]


def after(value, *others):
    return lax.optimization_barrier((value, *others))[0]


def gather_far(shard, axis):
    held = {0: shard}
    for bit in reversed(bits_of(axis)[1:]):
        held.update({place | bit: swap(piece, axis, bit) for place, piece in held.items()})
    return held


def gather_near(held, axis):
    held = dict(held)
    held.update({place | 1: swap(piece, axis, 1) for place, piece in held.items()})
    return [held[place] for place in sorted(held)]


def scatter_sum(parts, axis):
    held = dict(enumerate(parts))
    bits = bits_of(axis)
    for bit in bits:
        last = bit == bits[-1]
        got = {place ^ bit: swap(piece, axis, bit) for place, piece in held.items() if place & bit}
        held = {
            place: (held[place].astype(F32) + piece.astype(F32)).astype(F32 if last else BF16)
            for place, piece in got.items()
        }
    return held[0]


def halve(value, axis, bit):
    upper = (lax.axis_index(axis) // bit) % 2 == 1
    half = value.shape[0] // 2
    low, high = value[:half], value[half:]
    got = swap(jnp.where(upper, low, high), axis, bit)
    kept = jnp.where(upper, high, low)
    return (kept.astype(F32) + got.astype(F32)).astype(BF16)


def double(value, axis, bit):
    upper = (lax.axis_index(axis) // bit) % 2 == 1
    got = swap(value, axis, bit)
    return jnp.where(upper, jnp.concatenate([got, value]), jnp.concatenate([value, got]))


def sum_over(value, axis, bits):
    for bit in bits:
        value = halve(value, axis, bit)
    for bit in reversed(bits):
        value = double(value, axis, bit)
    return value


def sum_small(value, axes):
    value = value.reshape(-1, TILE)
    for axis in axes:
        for bit in bits_of(axis):
            value = value + swap(value, axis, bit)
    return value.reshape(-1)


def exchange(rows, axis):
    size = lax.axis_size(axis)
    total, width = rows.shape
    blocks = rows.reshape(size, total // size, width)
    return lax.all_to_all(blocks, axis, 0, 0, tiled=True)


def per_device(
    tokens,
    cotangent,
    span_starts,
    routes,
    norm_gains,
    bias_table,
    router,
    attn_qkv,
    attn_out,
    expert_in,
    expert_down,
):
    assert span_starts.shape[0] == 1
    tok_count, model_width = tokens.shape
    buckets, head_count = bias_table.shape
    head_size = model_width // head_count
    experts = router.shape[1]
    capacity = (10 * tok_count + 4 * experts - 1) // (4 * experts)
    total = experts * capacity
    place = lax.axis_index("wshard")
    where = jnp.stack([place.astype(I32), span_starts[0]])
    diag = jnp.asarray(diagonal_ones(buckets))
    diag_bias = jnp.dot(bias_table.T, diag, precision=PRECISE)
    router_t = router.T
    expert_in = jnp.swapaxes(expert_in[0], 1, 2)
    expert_down = expert_down[0]

    qkv_far = gather_far(attn_qkv, "wshard")
    slots_row, slots_col, outer_sent = route(routes, cotangent, experts, capacity)
    outer_rows = exchange(outer_sent, "dp").reshape(total, model_width)
    qkv_all = gather_near(qkv_far, "wshard")
    out_far = gather_far(after(attn_out, qkv_far[2]), "wshard")
    out_all = gather_near(out_far, "wshard")
    in_far = gather_far(after(expert_in, out_far[2]), "wshard")
    in_all = gather_near(in_far, "wshard")
    down_far = gather_far(after(expert_down, in_far[2]), "wshard")
    down_all = gather_near(down_far, "wshard")
    groups = len(qkv_all)

    qkv, mixed = [], []
    turn = after(where, slots_row)
    for g in range(groups):
        one = attend(g, turn, tokens, norm_gains, diag_bias, qkv_all[g], head_size)
        qkv.append(one[0])
        mixed.append(one[1])
        turn = after(where, one[1])
    hidden, normed_two, gates, sent = dispatch(
        turn, tokens, norm_gains, router_t, slots_row, slots_col, mixed, out_all, capacity
    )
    arrived = exchange(sent, "dp")
    rows = arrived[:, :capacity].reshape(total, model_width)
    gate_column = jnp.sum(arrived[:, capacity : capacity + 3, :capacity].astype(F32), 1)
    gate_column = gate_column.reshape(total, 1)

    order = [g for g in range(groups) if g % 2 == 0] + [g for g in range(groups) if g % 2]
    made, back, outer_low, gate_grads, act, low = experts_pass(
        rows, outer_rows, gate_column, [in_all[g] for g in order], [down_all[g] for g in order]
    )
    owners = total // capacity
    extra = jnp.stack(split_three(gate_grads.reshape(owners, capacity)), 1).astype(BF16)
    extra = jnp.pad(extra, ((0, 0), (0, EXTRA - 3), (0, model_width - capacity)))
    message = jnp.concatenate([back.reshape(owners, capacity, model_width), extra], 1)
    back_rows = exchange(message.reshape(-1, model_width), "dp")
    gate_grad_row = jnp.sum(back_rows[:, capacity : capacity + 3, :capacity].astype(F32), 1)
    gate_grad_row = gate_grad_row.reshape(1, total)
    back_rows = back_rows.reshape(-1, model_width)

    half = act.shape[1] // 2
    far_part = [low[0, :, half:], low[1, :, half:], act[:, half:]]
    near_part = [low[0, :, :half], low[1, :, :half], act[:, :half]]
    right = [rows, rows, outer_low]
    sums = []
    for far_one, near_one, rows_one in zip(far_part, near_part, right):
        got = swap(dot_tn(far_one, rows_one).astype(BF16), "wshard", 1)
        sums.append((dot_tn(near_one, rows_one) + got.astype(F32)).astype(BF16))
    share = half // 2
    sums = [s[:share].astype(F32) + swap(s[share:], "wshard", 2).astype(F32) for s in sums]
    grad_expert_in = jnp.swapaxes(jnp.stack(sums[:2]), 1, 2)[None]
    grad_expert_down = sums[2][None]

    (grad_hidden, mixed_grad, router_grad, gain_two), out_grads = undispatch(
        where, norm_gains, jnp.concatenate([router_t] * 3, 0), slots_col, gates, gate_grad_row,
        hidden, normed_two, cotangent, back_rows, mixed, out_all,
    )
    made_rows = exchange(after(made, back_rows), "dp").reshape(total, model_width)
    bits = bits_of("dp")
    other_bits = [bits[1], bits[0]] + bits[2:]
    out_sum = scatter_sum(out_grads, "wshard").astype(BF16)
    grad_attn_out = sum_over(out_sum, "dp", bits).astype(F32)
    small = jnp.concatenate([gain_two.reshape(-1), router_grad.reshape(-1)])
    small = sum_small(small, ("wshard", "dp"))
    gain_two, router_grad = small[:model_width], small[model_width:]

    norm_grad = None
    qkv_grads = [None] * groups
    heads = head_count // groups
    diag_all = jnp.zeros((head_count, diag.shape[1]), F32)
    turn = where
    for g in reversed(range(groups)):
        qkv_grads[g], norm_grad, diag_grad = attend_back(
            g, turn, tokens, norm_gains, diag_bias, qkv_all[g], qkv[g], mixed_grad, norm_grad,
            head_size,
        )
        turn = after(where, diag_grad)
        diag_all = lax.dynamic_update_slice_in_dim(
            diag_all, diag_grad.reshape(heads, -1), (place ^ g) * heads, 0
        )
    grad_tokens, gain_one = finish(tokens, norm_gains, norm_grad, grad_hidden)
    table_grad = lax.dot_general(diag, diag_all, (((1,), (1,)), ((), ())), precision=PRECISE)
    small = jnp.concatenate([gain_one.reshape(-1), table_grad.reshape(-1)])
    small = sum_small(small, ("wshard", "dp"))

    qkv_sum = scatter_sum(qkv_grads, "wshard").astype(BF16)
    wide = qkv_sum.shape[2]
    qkv_sum = qkv_sum.reshape(-1, wide)
    middle = qkv_sum.shape[0] // 2
    qkv_sum = jnp.concatenate(
        [
            sum_over(qkv_sum[:middle], "dp", bits).astype(F32),
            sum_over(qkv_sum[middle:], "dp", other_bits).astype(F32),
        ]
    )
    grad_attn_qkv = qkv_sum.reshape(3, model_width, wide)
    output = combine(hidden, after(gates, grad_tokens), slots_col, made_rows)
    return (
        output,
        grad_tokens,
        jnp.stack([small[:model_width], gain_two]),
        small[model_width:].reshape(buckets, head_count),
        router_grad.reshape(experts, model_width).T,
        grad_attn_qkv,
        grad_attn_out,
        grad_expert_in,
        grad_expert_down,
    )


def solution(mesh):
    return jax.shard_map(
        per_device,
        mesh=mesh,
        in_specs=(
            P(("dp", "wshard"), None),
            P(("dp", "wshard"), None),
            P(("dp", "wshard")),
            P(("dp", "wshard"), None),
            P(),
            P(),
            P(),
            P(None, None, "wshard"),
            P(None, "wshard"),
            P("dp", None, None, "wshard"),
            P("dp", "wshard", None),
        ),
        out_specs=(
            P(("dp", "wshard"), None),
            P(("dp", "wshard"), None),
            P(),
            P(),
            P(),
            P(None, None, "wshard"),
            P(None, "wshard"),
            P("dp", None, None, "wshard"),
            P("dp", "wshard", None),
        ),
        check_vma=False,
    )
```

time: 830 us -> 654 us (0.79)
  blocking collectives: 205 us -> 0 us
  Pallas kernels: 0 us -> 186 us
  matrix products: 219 us -> 48.2 us
  waiting for transfers between devices: 129 us -> 293 us
  local copies, waits for them, and re-layouts: 153 us -> 18.1 us
  starting transfers between devices: 19.2 us -> 69.8 us
  other arithmetic: 82.4 us -> 32.2 us
  between operations: 16 us -> 2.17 us
    psum x2 -> x0, blocking collectives: 205 us -> none  [the longest x1 167 us: per_device(): grad_attn_qkv, grad_attn_out = lax.psum((qkv_part, out_part), 'dp')]
    ppermute x0 -> x52, waiting for transfers between devices: none -> 187 us  [swap(): return lax.ppermute(value, axis, [(i, i ^ bit) for i in range(size)])]
    pallas_call x0 -> x14, Pallas kernels: none -> 186 us  [the longest x13 126 us: call(): pl.pallas_call(body, out_shape=out, in_specs=specs, out_specs=jax.tree.ma...]
    dot_general x23 -> x8, matrix products: 219 us -> 48.2 us  [the longest x6 45.6 us: dot_tn(): lax.dot_general(a, b, (((0,), (0,)), ((), ())), preferred_element_type=F32)]
    ppermute x0 -> x52, starting transfers between devices: none -> 51.1 us  [swap(): return lax.ppermute(value, axis, [(i, i ^ bit) for i in range(size)])]
    unnamed x113 -> x51, local copies, waits for them, and re-layouts: 53.5 us -> 5.83 us
    reduce_sum x9 -> x2, other arithmetic: 31.2 us -> 0.05 us  [the longest x1 0.03 us: per_device(): jnp.sum(back_rows[:, capacity:capacity + 3, :capacity].astype(F32), 1)]
    all_gather x1 -> x0, local copies, waits for them, and re-layouts: 28.7 us -> none  [per_device(): lax.all_gather(expert_in, 'wshard', axis=3, tiled=True)]
  transfers between devices with their start and end apart: 12 -> 56, of which waited for: 4 -> 24; matrix products, arithmetic and copies ran while one was open for 43% -> 13% of each run, Pallas kernels for 0% -> 17%
where the time goes in v1:
time: 654 us; the launch traced here: 650 us
  waiting for transfers between devices  293 us (45%)
  Pallas kernels  186 us (28%)
  starting transfers between devices  69.8 us (11%)
  matrix products  48.2 us (7%)
  other arithmetic  32.2 us (5%)
  local copies, waits for them, and re-layouts  18.1 us (3%)
    ppermute x52, waiting for transfers between devices, swap(): return lax.ppermute(value, axis, [(i, i ^ bit) for i in range(size)])  187 us
    pallas_call x13, Pallas kernels, call(): pl.pallas_call(body, out_shape=out, in_specs=specs, out_specs=jax.tree.ma...  126 us
    all_to_all x4, waiting for transfers between devices, exchange(): return lax.all_to_all(blocks, axis, 0, 0, tiled=True)  106 us
    pallas_call x1, Pallas kernels, experts_pass(): pl.pallas_call(functools.partial(expert_body, groups, chunk), grid=(total...  59.2 us
    ppermute x52, starting transfers between devices, swap(): return lax.ppermute(value, axis, [(i, i ^ bit) for i in range(size)])  51.1 us
    dot_general x6, matrix products, dot_tn(): lax.dot_general(a, b, (((0,), (0,)), ((), ())), preferred_element_type=F32)  45.6 us
    all_to_all x4, starting transfers between devices, exchange(): return lax.all_to_all(blocks, axis, 0, 0, tiled=True)  18.7 us
  transfers between devices with their start and end apart: 56, of which 24 were waited for; matrix products, arithmetic and copies ran while one was open for 13% of the time, Pallas kernels for 17%

profile of v1, /device:TPU:0, one launch (start us, length us, event | category | flops | bytes accessed | tf_op | source)
XLA Modules:
  0.0 649.5 jit_solution(1009576731428694067)
XLA Ops:
  0.7 3.0 collective-permute-start.1
  3.7 34.7 %collective-permute-done.1.w_ref = bf16[3,1024,256]{2,1,0:T(8,128)(2,1)} collective-permute-done((bf16[3,1024,256]{2,1,0:T(8,128)(2,1)}, bf16[3,1024,256]{2,1,0:T(8,128)(2,1)}, u32[]{:S(2)}, u32[]{:S(2)}) %collective-permute-start.1) | collective-permute-done | bytes 1572896 | tf_op jit(solution)/shard_map/ppermute | solution.py:650
  38.4 1.7 collective-permute-start.4
  40.4 12.7 %collective-permute-done.4.refs_6_ = bf16[1024,256]{1,0:T(8,128)(2,1)} collective-permute-done((bf16[1024,256]{1,0:T(8,128)(2,1)}, bf16[1024,256]{1,0:T(8,128)(2,1)}, u32[]{:S(2)}, u32[]{:S(2)}) %collective-permute-start.4) | collective-permute-done | bytes 524320 | tf_op jit(solution)/shard_map/ppermute | solution.py:650
  53.1 4.5 route.1
  58.9 1.7 convolution_bitcast_fusion.diag_ref.refs_3_
  60.6 8.1 %attend.4 = (bf16[3,512,256]{2,1,0:T(8,128)(2,1)}, bf16[512,256]{1,0:T(8,128)(2,1)}) custom-call(s32[2]{0:T(128)} %pad_add_fusion.where_ref.refs_0_, bf16[512,1024]{1,0:T(8,128)(2,1)} %x_ref.17, f32[2,1024]{1,0:T(2,128)} %gain_ref.19, f32[16,1024]{1,0:T(8,128)} %convolution_bitcast_fusion.diag_ref.refs_3_, bf16[3,1024,256]{2,1,0:T(8,128)(2,1)} %w_ref.3), custom_call_target="tpu_custom_call" | custom-call | flops 1024 | bytes 1024 | tf_op jit(solution)/shard_map/attend/pallas_call | solution.py:48
  69.8 7.9 %attend.5 = (bf16[3,512,256]{2,1,0:T(8,128)(2,1)}, bf16[512,256]{1,0:T(8,128)(2,1)}) custom-call(s32[2]{0:T(128)} %pad_add_fusion.where_ref.refs_0_, bf16[512,1024]{1,0:T(8,128)(2,1)} %x_ref.17, f32[2,1024]{1,0:T(2,128)} %gain_ref.19, f32[16,1024]{1,0:T(8,128)} %convolution_bitcast_fusion.diag_ref.refs_3_, bf16[3,1024,256]{2,1,0:T(8,128)(2,1)} %copy-done.6), custom_call_target="tpu_custom_call" | custom-call | flops 1024 | bytes 1024 | tf_op jit(solution)/shard_map/attend/pallas_call | solution.py:48
  77.7 7.9 %attend.6 = (bf16[3,512,256]{2,1,0:T(8,128)(2,1)}, bf16[512,256]{1,0:T(8,128)(2,1)}) custom-call(s32[2]{0:T(128)} %pad_add_fusion.where_ref.refs_0_, bf16[512,1024]{1,0:T(8,128)(2,1)} %x_ref.17, f32[2,1024]{1,0:T(2,128)} %gain_ref.19, f32[16,1024]{1,0:T(8,128)} %convolution_bitcast_fusion.diag_ref.refs_3_, bf16[3,1024,256]{2,1,0:T(8,128)(2,1)} %collective-permute-done.1.w_ref), custom_call_target="tpu_custom_call" | custom-call | flops 1024 | bytes 1024 | tf_op jit(solution)/shard_map/attend/pallas_call | solution.py:48
  86.7 8.3 %attend.7 = (bf16[3,512,256]{2,1,0:T(8,128)(2,1)}, bf16[512,256]{1,0:T(8,128)(2,1)}) custom-call(s32[2]{0:T(128)} %pad_add_fusion.where_ref.refs_0_, bf16[512,1024]{1,0:T(8,128)(2,1)} %x_ref.17, f32[2,1024]{1,0:T(2,128)} %gain_ref.19, f32[16,1024]{1,0:T(8,128)} %convolution_bitcast_fusion.diag_ref.refs_3_, bf16[3,1024,256]{2,1,0:T(8,128)(2,1)} %copy-done.5), custom_call_target="tpu_custom_call" | custom-call | flops 1024 | bytes 1024 | tf_op jit(solution)/shard_map/attend/pallas_call | solution.py:48
  95.0 9.2 %dispatch.1 = (f32[512,1024]{1,0:T(8,128)}, bf16[512,1024]{1,0:T(8,128)(2,1)}, f32[512,2]{1,0:T(8,128)}, bf16[1344,1024]{1,0:T(8,128)(2,1)}) custom-call(s32[2]{0:T(128)} %pad_add_fusion.where_ref.refs_0_, bf16[512,1024]{1,0:T(8,128)(2,1)} %x_ref.17, f32[2,1024]{1,0:T(2,128)} %gain_ref.19, bf16[8,1024]{1,0:T(8,128)(2,1)} %bitcast.107, ...), custom_call_target="tpu_custom_call" | custom-call | flops 1024 | bytes 1024 | tf_op jit(solution)/shard_map/dispatch/pallas_call | solution.py:48
  104.2 6.0 all-to-all-start
  111.7 61.4 %all-to-all-done = bf16[8,168,1024]{2,1,0:T(8,128)(2,1)S(1)} async-done(((bf16[8,168,1024]{2,1,0:T(8,128)(2,1)}), bf16[8,168,1024]{2,1,0:T(8,128)(2,1)S(1)}, u32[]{:S(2)}, u32[]{:S(2)}) %all-to-all-start) | async-done | bytes 2752544 | tf_op jit(solution)/shard_map/all_to_all | solution.py:723
  173.1 4.4 all-to-all-start.1
  179.7 32.2 %collective-permute-done.9.refs_5_ = bf16[704,1024]{1,0:T(8,128)(2,1)} collective-permute-done((bf16[704,1024]{1,0:T(8,128)(2,1)}, bf16[704,1024]{1,0:T(8,128)(2,1)}, u32[]{:S(2)}, u32[]{:S(2)}) %collective-permute-start.9) | collective-permute-done | bytes 1441824 | tf_op jit(solution)/shard_map/ppermute | solution.py:650
  213.3 1.8 slice.158
  215.1 21.8 %all-to-all-done.1 = bf16[8,160,1024]{2,1,0:T(8,128)(2,1)} async-done(((bf16[8,160,1024]{2,1,0:T(8,128)(2,1)}), bf16[8,160,1024]{2,1,0:T(8,128)(2,1)}, u32[]{:S(2)}, u32[]{:S(2)}) %all-to-all-start.1) | async-done | bytes 2621472 | tf_op jit(solution)/shard_map/all_to_all | solution.py:723
  236.8 59.2 %experts.1 = (bf16[1280,1024]{1,0:T(8,128)(2,1)}, bf16[1280,1024]{1,0:T(8,128)(2,1)}, bf16[1280,1024]{1,0:T(8,128)(2,1)}, f32[1280,1]{1,0:T(8,128)}, bf16[1280,2...) custom-call(bf16[1280,1024]{1,0:T(8,128)(2,1)} %bitcast.88, bf16[1280,1024]{1,0:T(8,128)(2,1)} %bitcast.7.outer_ref, ...), custom_call_target="tpu_custom_call" | custom-call | flops 1024 | bytes 1024 | tf_op jit(solution)/shard_map/experts/pallas_call | solution.py:626
  296.1 8.5 %convolution_convert_fusion = bf16[1408,1024]{1,0:T(8,128)(2,1)} fusion(bf16[1280,1024]{1,0:T(8,128)(2,1)} %get-tuple-element.120, bf16[1280,2816]{1,0:T(8,128)(2,1)} %get-tuple-element.119), kind=kOutput, calls=%fused_computation.6 | convolution fusion | flops 3692429312 | bytes 9109504 | tf_op jit(solution)/shard_map/dot_general | solution.py:36
  304.6 7.5 %convolution_convert_fusion.2 = bf16[1408,1024]{1,0:T(8,128)(2,1)} fusion(bf16[1280,1024]{1,0:T(8,128)(2,1)S(1)} %bitcast.90, bf16[2,1280,2816]{2,1,0:T(8,128)(2,1)} %get-tuple-element.118), kind=kOutput, calls=%fused_computation.8 | convolution fusion | flops 3692429312 | bytes 9109504 | tf_op jit(solution)/shard_map/dot_general | solution.py:36
  312.9 1.9 fusion.11
  314.8 3.6 all-to-all-start.2
  318.4 8.4 %convolution_convert_fusion.1 = bf16[1408,1024]{1,0:T(8,128)(2,1)} fusion(bf16[1280,1024]{1,0:T(8,128)(2,1)} %bitcast.89, bf16[2,1280,2816]{2,1,0:T(8,128)(2,1)} %get-tuple-element.118), kind=kOutput, calls=%fused_computation.7 | convolution fusion | flops 3692429312 | bytes 9109504 | tf_op jit(solution)/shard_map/dot_general | solution.py:36
  327.4 7.6 %add_convert_fusion = bf16[1408,1024]{1,0:T(8,128)(2,1)S(1)} fusion(bf16[1408,1024]{1,0:T(8,128)(2,1)} %collective-permute-done.50, bf16[1280,1024]{1,0:T(8,128)(2,1)} %get-tuple-element.120, bf16[1280,2816]{1,0:T(8,128)(2,1)} %get-tuple-element.119), kind=kOutput, calls=%fused_computation.1 | convolution fusion | flops 3695312896 | bytes 11993088 | tf_op jit(solution)/shard_map/dot_general | solution.py:36
  338.3 6.6 %add_convert_fusion.2 = bf16[1408,1024]{1,0:T(8,128)(2,1)S(1)} fusion(bf16[1408,1024]{1,0:T(8,128)(2,1)} %collective-permute-done.46, bf16[1280,1024]{1,0:T(8,128)(2,1)S(1)} %bitcast.91, bf16[2,1280,2816]{2,1,0:T(8,128)(2,1)} %get-tuple-element.118), kind=kOutput, calls=%fused_computation.3 | convolution fusion | flops 3695312896 | bytes 11993088 | tf_op jit(solution)/shard_map/dot_general | solution.py:36
  347.9 7.1 %add_convert_fusion.1 = bf16[1408,1024]{1,0:T(8,128)(2,1)S(1)} fusion(bf16[1408,1024]{1,0:T(8,128)(2,1)} %collective-permute-done.48, bf16[1280,1024]{1,0:T(8,128)(2,1)S(1)} %bitcast.92, bf16[2,1280,2816]{2,1,0:T(8,128)(2,1)} %get-tuple-element.118), kind=kOutput, calls=%fused_computation.2 | convolution fusion | flops 3695312896 | bytes 11993088 | tf_op jit(solution)/shard_map/dot_general | solution.py:36
  357.8 23.2 %all-to-all-done.2 = bf16[8,168,1024]{2,1,0:T(8,128)(2,1)S(1)} async-done(((bf16[8,168,1024]{2,1,0:T(8,128)(2,1)}), bf16[8,168,1024]{2,1,0:T(8,128)(2,1)S(1)}, u32[]{:S(2)}, u32[]{:S(2)}) %all-to-all-start.2) | async-done | bytes 2752544 | tf_op jit(solution)/shard_map/all_to_all | solution.py:723
  382.6 13.1 %undispatch.1 = (f32[512,1024]{1,0:T(8,128)}, bf16[512,1024]{1,0:T(8,128)(2,1)}, f32[8,1024]{1,0:T(8,128)}, f32[1,1024]{1,0:T(1,128)}, bf16[1024,256]{1,0:T(8,12...) custom-call(s32[2]{0:T(128)} %pad_add_fusion.where_ref.refs_0_, ...), custom_call_target="tpu_custom_call" | custom-call | flops 1024 | bytes 1024 | tf_op jit(solution)/shard_map/undispatch/pallas_call | solution.py:48
  395.7 13.5 %attend_back.4 = (bf16[3,1024,256]{2,1,0:T(8,128)(2,1)}, f32[512,1024]{1,0:T(8,128)}, f32[4,8,128]{2,1,0:T(8,128)}) custom-call(s32[2]{0:T(128)} %pad_add_fusion.where_ref.refs_0_, bf16[512,1024]{1,0:T(8,128)(2,1)} %x_ref.17, f32[2,1024]{1,0:T(2,128)} %gain_ref.19, f32[16,1024]{1,0:T(8,128)} %convolution_bitcast_fusion.diag_ref.refs_3_, ...), custom_call_target="tpu_custom_call" | custom-call | flops 1024 | bytes 1024 | tf_op jit(solution)/shard_map/attend_back/pallas_call | solution.py:48
  409.7 14.2 %attend_back.5 = (bf16[3,1024,256]{2,1,0:T(8,128)(2,1)}, f32[512,1024]{1,0:T(8,128)}, f32[4,8,128]{2,1,0:T(8,128)}) custom-call(s32[2]{0:T(128)} %pad_add_fusion.where_ref.refs_0_, bf16[512,1024]{1,0:T(8,128)(2,1)} %x_ref.17, f32[2,1024]{1,0:T(2,128)} %gain_ref.19, f32[16,1024]{1,0:T(8,128)} %convolution_bitcast_fusion.diag_ref.refs_3_, ...), custom_call_target="tpu_custom_call" | custom-call | flops 1024 | bytes 1024 | tf_op jit(solution)/shard_map/attend_back/pallas_call | solution.py:48
  423.9 14.4 %attend_back.6 = (bf16[3,1024,256]{2,1,0:T(8,128)(2,1)}, f32[512,1024]{1,0:T(8,128)}, f32[4,8,128]{2,1,0:T(8,128)}) custom-call(s32[2]{0:T(128)} %pad_add_fusion.where_ref.refs_0_, bf16[512,1024]{1,0:T(8,128)(2,1)} %x_ref.17, f32[2,1024]{1,0:T(2,128)} %gain_ref.19, f32[16,1024]{1,0:T(8,128)} %convolution_bitcast_fusion.diag_ref.refs_3_, ...), custom_call_target="tpu_custom_call" | custom-call | flops 1024 | bytes 1024 | tf_op jit(solution)/shard_map/attend_back/pallas_call | solution.py:48
  438.3 14.2 %attend_back.7 = (bf16[3,1024,256]{2,1,0:T(8,128)(2,1)}, f32[512,1024]{1,0:T(8,128)}, f32[4,8,128]{2,1,0:T(8,128)}) custom-call(s32[2]{0:T(128)} %pad_add_fusion.where_ref.refs_0_, bf16[512,1024]{1,0:T(8,128)(2,1)} %x_ref.17, f32[2,1024]{1,0:T(2,128)} %gain_ref.19, f32[16,1024]{1,0:T(8,128)} %convolution_bitcast_fusion.diag_ref.refs_3_, ...), custom_call_target="tpu_custom_call" | custom-call | flops 1024 | bytes 1024 | tf_op jit(solution)/shard_map/attend_back/pallas_call | solution.py:48
  452.5 4.7 finish.1
  462.7 3.6 add_bitcast_fusion
  466.7 1.7 collective-permute-start.13
  473.3 10.1 %collective-permute-done.39 = bf16[1024,256]{1,0:T(8,128)(2,1)S(1)} collective-permute-done((bf16[1024,256]{1,0:T(8,128)(2,1)S(1)}, bf16[1024,256]{1,0:T(8,128)(2,1)S(1)}, u32[]{:S(2)}, u32[]{:S(2)}) %collective-permute-start.39) | collective-permute-done | bytes 524320 | tf_op jit(solution)/shard_map/ppermute | solution.py:650
  485.6 3.0 add_convert_fusion.4
  488.7 1.8 collective-permute-done.40
  492.3 22.9 %collective-permute-done.18 = f32[72,128]{1,0:T(8,128)S(1)} collective-permute-done((f32[72,128]{1,0:T(8,128)S(1)}, f32[72,128]{1,0:T(8,128)S(1)}, u32[]{:S(2)}, u32[]{:S(2)}) %collective-permute-start.18) | collective-permute-done | bytes 36896 | tf_op jit(solution)/shard_map/ppermute | solution.py:650
  515.1 5.0 collective-permute-done.41
  524.5 1.8 add_bitcast_fusion.2
  526.4 4.7 all-to-all-start.3
  531.1 2.0 collective-permute-start.15
  533.3 2.9 collective-permute-start.43
  536.2 11.5 %collective-permute-done.24 = bf16[3,1024,256]{2,1,0:T(8,128)(2,1)} collective-permute-done((bf16[3,1024,256]{2,1,0:T(8,128)(2,1)}, bf16[3,1024,256]{2,1,0:T(8,128)(2,1)}, u32[]{:S(2)}, u32[]{:S(2)}) %collective-permute-start.24) | collective-permute-done | bytes 1572896 | tf_op jit(solution)/shard_map/ppermute | solution.py:650
  547.8 3.1 add_convert_fusion.3
  552.5 1.8 add_bitcast_fusion.1
  554.3 20.4 %collective-permute-done.15 = f32[12,128]{1,0:T(8,128)S(1)} collective-permute-done((f32[12,128]{1,0:T(8,128)S(1)}, f32[12,128]{1,0:T(8,128)S(1)}, u32[]{:S(2)}, u32[]{:S(2)}) %collective-permute-start.15) | collective-permute-done | bytes 6176 | tf_op jit(solution)/shard_map/ppermute | solution.py:650
  574.7 4.8 collective-permute-start.16
  580.9 11.0 %collective-permute-done.43 = bf16[128,256]{1,0:T(8,128)(2,1)S(1)} collective-permute-done((bf16[128,256]{1,0:T(8,128)(2,1)S(1)}, bf16[128,256]{1,0:T(8,128)(2,1)S(1)}, u32[]{:S(2)}, u32[]{:S(2)}) %collective-permute-start.43) | collective-permute-done | bytes 65568 | tf_op jit(solution)/shard_map/ppermute | solution.py:650
  592.5 2.1 collective-permute-start.26
  595.8 3.6 collective-permute-done.26
  600.9 1.7 collective-permute-start.33
  602.6 6.6 %collective-permute-done.27 = bf16[192,256]{1,0:T(8,128)(2,1)S(1)} collective-permute-done((bf16[192,256]{1,0:T(8,128)(2,1)S(1)}, bf16[192,256]{1,0:T(8,128)(2,1)S(1)}, u32[]{:S(2)}, u32[]{:S(2)}) %collective-permute-start.27) | collective-permute-done | bytes 98336 | tf_op jit(solution)/shard_map/ppermute | solution.py:650
  609.4 1.7 collective-permute-done.33
  612.4 4.2 collective-permute-done.28
  616.9 2.4 collective-permute-start.45
  620.0 2.0 collective-permute-start.35
  622.6 1.8 collective-permute-start.30
  624.3 3.0 maximum_bitcast_fusion
  628.9 1.8 collective-permute-done.35
  634.7 2.1 fusion.12
  640.8 1.9 convert.8
  642.7 6.5 %combine.1 = bf16[512,1024]{1,0:T(8,128)(2,1)} custom-call(f32[512,1024]{1,0:T(8,128)} %get-tuple-element.77.hidden_ref, f32[512,2]{1,0:T(8,128)} %get-tuple-element.103.gate_ref, s32[512,8]{1,0:T(8,128)} %get-tuple-element.75.col_ref, bf16[1280,1024]{1,0:T(8,128)(2,1)} %bitcast.14.rows_ref), custom_call_target="tpu_custom_call" | custom-call | flops 1024 | bytes 1024 | tf_op jit(solution)/shard_map/combine/pallas_call | solution.py:48
  (196 shorter events, 58.9 us)
Async XLA Ops:
  0.6 58.2 %copy-start = (f32[32,16]{0,1:T(8,128)S(1)}, f32[32,16]{0,1:T(8,128)}, u32[]{:S(2)}) copy-start(f32[32,16]{0,1:T(8,128)} %param.17) | copy-start | bytes 6148
  0.7 37.7 %collective-permute-start.1 = (bf16[3,1024,256]{2,1,0:T(8,128)(2,1)}, bf16[3,1024,256]{2,1,0:T(8,128)(2,1)}, u32[]{:S(2)}, u32[]{:S(2)}) collective-permute-start(bf16[3,1024,256]{2,1,0:T(8,128)(2,1)} %w_ref.3), channel_id=1, source_target_pairs={{0,2},{1,3},{2,0},{3,1},{4,6},{5,7},{6,4},{7,5},{8,10},{9,11},{10,... | collective-permute-start | bytes 4718600 | tf_op jit(solution)/shard_map/ppermute | solution.py:650
  3.7 64.9 %collective-permute-start = (bf16[3,1024,256]{2,1,0:T(8,128)(2,1)}, bf16[3,1024,256]{2,1,0:T(8,128)(2,1)S(1)}, u32[]{:S(2)}, u32[]{:S(2)}) collective-permute-start(bf16[3,1024,256]{2,1,0:T(8,128)(2,1)} %w_ref.3), channel_id=1, source_target_pairs={{0,1},{1,0},{2,3},{3,2},{4,5},{5,4},{6,7},{7,6},{8,9},{9,8},{10,11... | collective-permute-start | bytes 4718600 | tf_op jit(solution)/shard_map/ppermute | solution.py:650
  38.4 47.2 %collective-permute-start.2 = (bf16[3,1024,256]{2,1,0:T(8,128)(2,1)}, bf16[3,1024,256]{2,1,0:T(8,128)(2,1)S(1)}, u32[]{:S(2)}, u32[]{:S(2)}) collective-permute-start(bf16[3,1024,256]{2,1,0:T(8,128)(2,1)} %collective-permute-done.1.w_ref), channel_id=1, source_target_pairs={{0,1},{1,0},{2,3},{3,2},{4,5},{5,4},{6,7},{7,6},{8,9},{9,8},{10,11... | collective-permute-start | bytes 4718600 | tf_op jit(solution)/shard_map/ppermute | solution.py:650
  38.4 14.7 %collective-permute-start.4 = (bf16[1024,256]{1,0:T(8,128)(2,1)}, bf16[1024,256]{1,0:T(8,128)(2,1)}, u32[]{:S(2)}, u32[]{:S(2)}) collective-permute-start(bf16[1024,256]{1,0:T(8,128)(2,1)} %refs_4_.1), channel_id=1, source_target_pairs={{0,2},{1,3},{2,0},{3,1},{4,6},{5,7},{6,4},{7,5},{8,10},{9,11},{10,... | collective-permute-start | bytes 1572872 | tf_op jit(solution)/shard_map/ppermute | solution.py:650
  40.1 54.9 %collective-permute-start.3 = (bf16[1024,256]{1,0:T(8,128)(2,1)}, bf16[1024,256]{1,0:T(8,128)(2,1)}, u32[]{:S(2)}, u32[]{:S(2)}) collective-permute-start(bf16[1024,256]{1,0:T(8,128)(2,1)} %refs_4_.1), channel_id=1, source_target_pairs={{0,1},{1,0},{2,3},{3,2},{4,5},{5,4},{6,7},{7,6},{8,9},{9,8},{10,11... | collective-permute-start | bytes 1572872 | tf_op jit(solution)/shard_map/ppermute | solution.py:650
  53.1 42.0 %collective-permute-start.5 = (bf16[1024,256]{1,0:T(8,128)(2,1)}, bf16[1024,256]{1,0:T(8,128)(2,1)}, u32[]{:S(2)}, u32[]{:S(2)}) collective-permute-start(bf16[1024,256]{1,0:T(8,128)(2,1)} %collective-permute-done.4.refs_6_), channel_id=1, source_target_pairs={{0,1},{1,0},{2,3},{3,2},{4,5},{5,4},{6,7},{7,6},{8,9},{9,8},{10,11... | collective-permute-start | bytes 1572872 | tf_op jit(solution)/shard_map/ppermute | solution.py:650
  104.2 69.0 %all-to-all-start = ((bf16[8,168,1024]{2,1,0:T(8,128)(2,1)}), bf16[8,168,1024]{2,1,0:T(8,128)(2,1)S(1)}, u32[]{:S(2)}, u32[]{:S(2)}) async-start(bf16[8,168,1024]{2,1,0:T(8,128)(2,1)} %bitcast.97), calls=%async_computation | async-start | bytes 5505024 | tf_op jit(solution)/shard_map/all_to_all | solution.py:723
  110.2 67.4 %collective-permute-start.6 = (bf16[2,704,1024]{2,1,0:T(8,128)(2,1)}, bf16[2,704,1024]{2,1,0:T(8,128)(2,1)}, u32[]{:S(2)}, u32[]{:S(2)}) collective-permute-start(bf16[2,704,1024]{2,1,0:T(8,128)(2,1)} %bitcast.94), channel_id=1, source_target_pairs={{0,2},{1,3},{2,0},{3,1},{4,6},{5,7},{6,4},{7,5},{8,10},{9,11},{10,... | collective-permute-start | bytes 8650760 | tf_op jit(solution)/shard_map/ppermute | solution.py:650
  173.1 63.7 %all-to-all-start.1 = ((bf16[8,160,1024]{2,1,0:T(8,128)(2,1)}), bf16[8,160,1024]{2,1,0:T(8,128)(2,1)}, u32[]{:S(2)}, u32[]{:S(2)}) async-start(bf16[8,160,1024]{2,1,0:T(8,128)(2,1)} %bitcast.99), calls=%async_computation.1 | async-start | bytes 5242880 | tf_op jit(solution)/shard_map/all_to_all | solution.py:723
  177.5 59.3 %collective-permute-start.7 = (bf16[2,704,1024]{2,1,0:T(8,128)(2,1)}, bf16[2,704,1024]{2,1,0:T(8,128)(2,1)}, u32[]{:S(2)}, u32[]{:S(2)}) collective-permute-start(bf16[2,704,1024]{2,1,0:T(8,128)(2,1)} %bitcast.95), channel_id=1, source_target_pairs={{0,1},{1,0},{2,3},{3,2},{4,5},{5,4},{6,7},{7,6},{8,9},{9,8},{10,11... | collective-permute-start | bytes 8650760 | tf_op jit(solution)/shard_map/ppermute | solution.py:650
  177.6 34.3 %collective-permute-start.9 = (bf16[704,1024]{1,0:T(8,128)(2,1)}, bf16[704,1024]{1,0:T(8,128)(2,1)}, u32[]{:S(2)}, u32[]{:S(2)}) collective-permute-start(bf16[704,1024]{1,0:T(8,128)(2,1)} %bitcast.101), channel_id=1, source_target_pairs={{0,2},{1,3},{2,0},{3,1},{4,6},{5,7},{6,4},{7,5},{8,10},{9,11},{10,... | collective-permute-start | bytes 4325384 | tf_op jit(solution)/shard_map/ppermute | solution.py:650
  179.2 57.6 %collective-permute-start.8 = (bf16[2,704,1024]{2,1,0:T(8,128)(2,1)}, bf16[2,704,1024]{2,1,0:T(8,128)(2,1)}, u32[]{:S(2)}, u32[]{:S(2)}) collective-permute-start(bf16[2,704,1024]{2,1,0:T(8,128)(2,1)} %collective-permute-done.6.refs_1_), channel_id=1, source_target_pairs={{0,1},{1,0},{2,3},{3,2},{4,5},{5,4},{6,7},{7,6},{8,9},{9,8},{10,11... | collective-permute-start | bytes 8650760 | tf_op jit(solution)/shard_map/ppermute | solution.py:650
  179.4 57.4 %collective-permute-start.10 = (bf16[704,1024]{1,0:T(8,128)(2,1)}, bf16[704,1024]{1,0:T(8,128)(2,1)}, u32[]{:S(2)}, u32[]{:S(2)}) collective-permute-start(bf16[704,1024]{1,0:T(8,128)(2,1)} %bitcast.102), channel_id=1, source_target_pairs={{0,1},{1,0},{2,3},{3,2},{4,5},{5,4},{6,7},{7,6},{8,9},{9,8},{10,11... | collective-permute-start | bytes 4325384 | tf_op jit(solution)/shard_map/ppermute | solution.py:650
  211.9 24.9 %collective-permute-start.11 = (bf16[704,1024]{1,0:T(8,128)(2,1)}, bf16[704,1024]{1,0:T(8,128)(2,1)}, u32[]{:S(2)}, u32[]{:S(2)}) collective-permute-start(bf16[704,1024]{1,0:T(8,128)(2,1)} %collective-permute-done.9.refs_5_), channel_id=1, source_target_pairs={{0,1},{1,0},{2,3},{3,2},{4,5},{5,4},{6,7},{7,6},{8,9},{9,8},{10,11... | collective-permute-start | bytes 4325384 | tf_op jit(solution)/shard_map/ppermute | solution.py:650
  296.0 8.5 %copy-start.3 = (bf16[8,160,1024]{2,1,0:T(8,128)(2,1)S(1)}, bf16[8,160,1024]{2,1,0:T(8,128)(2,1)}, u32[]{:S(2)}) copy-start(bf16[8,160,1024]{2,1,0:T(8,128)(2,1)} %slice.158) | copy-start | bytes 7864324
  304.6 22.9 %collective-permute-start.50 = (bf16[1408,1024]{1,0:T(8,128)(2,1)}, bf16[1408,1024]{1,0:T(8,128)(2,1)}, u32[]{:S(2)}, u32[]{:S(2)}) collective-permute-start(bf16[1408,1024]{1,0:T(8,128)(2,1)} %convolution_convert_fusion), channel_id=1, source_target_pairs={{0,1},{1,0},{2,3},{3,2},{4,5},{5,4},{6,7},{7,6},{8,9},{9,8},{10,11... | collective-permute-start | bytes 8650760 | tf_op jit(solution)/shard_map/ppermute | solution.py:650
  304.6 8.3 %copy-start.13 = (bf16[1280,1024]{1,0:T(8,128)(2,1)S(1)}, bf16[1280,1024]{1,0:T(8,128)(2,1)}, u32[]{:S(2)}) copy-start(bf16[1280,1024]{1,0:T(8,128)(2,1)} %get-tuple-element.84) | copy-start | bytes 7864324
  312.0 25.9 %collective-permute-start.46 = (bf16[1408,1024]{1,0:T(8,128)(2,1)}, bf16[1408,1024]{1,0:T(8,128)(2,1)}, u32[]{:S(2)}, u32[]{:S(2)}) collective-permute-start(bf16[1408,1024]{1,0:T(8,128)(2,1)} %convolution_convert_fusion.2), channel_id=1, source_target_pairs={{0,1},{1,0},{2,3},{3,2},{4,5},{5,4},{6,7},{7,6},{8,9},{9,8},{10,11... | collective-permute-start | bytes 8650760 | tf_op jit(solution)/shard_map/ppermute | solution.py:650
  314.8 66.3 %all-to-all-start.2 = ((bf16[8,168,1024]{2,1,0:T(8,128)(2,1)}), bf16[8,168,1024]{2,1,0:T(8,128)(2,1)S(1)}, u32[]{:S(2)}, u32[]{:S(2)}) async-start(bf16[8,168,1024]{2,1,0:T(8,128)(2,1)} %fusion.11), calls=%async_computation.2 | async-start | bytes 5505024 | tf_op jit(solution)/shard_map/all_to_all | solution.py:723
  318.4 8.4 %copy-start.19 = (bf16[1024,8]{0,1:T(8,128)(2,1)S(1)}, bf16[1024,8]{0,1:T(8,128)(2,1)}, u32[]{:S(2)}) copy-start(bf16[1024,8]{0,1:T(8,128)(2,1)} %param.18) | copy-start | bytes 49156
  326.8 21.1 %collective-permute-start.48 = (bf16[1408,1024]{1,0:T(8,128)(2,1)}, bf16[1408,1024]{1,0:T(8,128)(2,1)}, u32[]{:S(2)}, u32[]{:S(2)}) collective-permute-start(bf16[1408,1024]{1,0:T(8,128)(2,1)} %convolution_convert_fusion.1), channel_id=1, source_target_pairs={{0,1},{1,0},{2,3},{3,2},{4,5},{5,4},{6,7},{7,6},{8,9},{9,8},{10,11... | collective-permute-start | bytes 8650760 | tf_op jit(solution)/shard_map/ppermute | solution.py:650
  336.3 126.4 %collective-permute-start.51 = (bf16[704,1024]{1,0:T(8,128)(2,1)}, bf16[704,1024]{1,0:T(8,128)(2,1)}, u32[]{:S(2)}, u32[]{:S(2)}) collective-permute-start(bf16[704,1024]{1,0:T(8,128)(2,1)} %slice.188), channel_id=1, source_target_pairs={{0,2},{1,3},{2,0},{3,1},{4,6},{5,7},{6,4},{7,5},{8,10},{9,11},{10,... | collective-permute-start | bytes 4325384 | tf_op jit(solution)/shard_map/ppermute | solution.py:650
  346.3 175.3 %collective-permute-start.47 = (bf16[704,1024]{1,0:T(8,128)(2,1)}, bf16[704,1024]{1,0:T(8,128)(2,1)}, u32[]{:S(2)}, u32[]{:S(2)}) collective-permute-start(bf16[704,1024]{1,0:T(8,128)(2,1)} %slice.184), channel_id=1, source_target_pairs={{0,2},{1,3},{2,0},{3,1},{4,6},{5,7},{6,4},{7,5},{8,10},{9,11},{10,... | collective-permute-start | bytes 4325384 | tf_op jit(solution)/shard_map/ppermute | solution.py:650
  395.7 72.7 %collective-permute-start.38 = (bf16[1024,256]{1,0:T(8,128)(2,1)}, bf16[1024,256]{1,0:T(8,128)(2,1)S(1)}, u32[]{:S(2)}, u32[]{:S(2)}) collective-permute-start(bf16[1024,256]{1,0:T(8,128)(2,1)} %get-tuple-element.117), channel_id=1, source_target_pairs={{0,1},{1,0},{2,3},{3,2},{4,5},{5,4},{6,7},{7,6},{8,9},{9,8},{10,11... | collective-permute-start | bytes 1572872 | tf_op jit(solution)/shard_map/ppermute | solution.py:650
  409.2 74.9 %collective-permute-start.23 = (bf16[3,1024,256]{2,1,0:T(8,128)(2,1)}, bf16[3,1024,256]{2,1,0:T(8,128)(2,1)}, u32[]{:S(2)}, u32[]{:S(2)}) collective-permute-start(bf16[3,1024,256]{2,1,0:T(8,128)(2,1)} %get-tuple-element.113), channel_id=1, source_target_pairs={{0,1},{1,0},{2,3},{3,2},{4,5},{5,4},{6,7},{7,6},{8,9},{9,8},{10,11... | collective-permute-start | bytes 4718600 | tf_op jit(solution)/shard_map/ppermute | solution.py:650
  452.5 10.2 %copy-start.12 = (bf16[1408,1024]{1,0:T(8,128)(2,1)S(1)}, bf16[1408,1024]{1,0:T(8,128)(2,1)}, u32[]{:S(2)}) copy-start(bf16[1408,1024]{1,0:T(8,128)(2,1)} %copy-done.11) | copy-start | bytes 8650756
  462.6 21.3 %copy-start.18 = (bf16[1024,256]{1,0:T(8,128)(2,1)S(1)}, bf16[1024,256]{1,0:T(8,128)(2,1)}, u32[]{:S(2)}) copy-start(bf16[1024,256]{1,0:T(8,128)(2,1)} %get-tuple-element.114) | copy-start | bytes 1572868
  462.6 4.1 collective-permute-start.12
  466.3 19.3 %copy-start.14 = (bf16[3,1024,256]{2,1,0:T(8,128)(2,1)S(1)}, bf16[3,1024,256]{2,1,0:T(8,128)(2,1)}, u32[]{:S(2)}) copy-start(bf16[3,1024,256]{2,1,0:T(8,128)(2,1)} %get-tuple-element.112) | copy-start | bytes 4718596
  466.3 6.9 %collective-permute-start.37 = (bf16[1024,256]{1,0:T(8,128)(2,1)S(1)}, bf16[1024,256]{1,0:T(8,128)(2,1)S(1)}, u32[]{:S(2)}, u32[]{:S(2)}) collective-permute-start(bf16[1024,256]{1,0:T(8,128)(2,1)S(1)} %copy-done.23), channel_id=1, source_target_pairs={{0,1},{1,0},{2,3},{3,2},{4,5},{5,4},{6,7},{7,6},{8,9},{9,8},{10,11... | collective-permute-start | bytes 1572872 | tf_op jit(solution)/shard_map/ppermute | solution.py:650
  466.7 3.7 collective-permute-start.13
  468.5 14.9 %collective-permute-start.39 = (bf16[1024,256]{1,0:T(8,128)(2,1)S(1)}, bf16[1024,256]{1,0:T(8,128)(2,1)S(1)}, u32[]{:S(2)}, u32[]{:S(2)}) collective-permute-start(bf16[1024,256]{1,0:T(8,128)(2,1)S(1)} %add_convert_fusion.7), channel_id=1, source_target_pairs={{0,2},{1,3},{2,0},{3,1},{4,6},{5,7},{6,4},{7,5},{8,10},{9,11},{10,... | collective-permute-start | bytes 1572872 | tf_op jit(solution)/shard_map/ppermute | solution.py:650
  470.4 1.2 collective-permute-start.17
  471.6 80.9 %collective-permute-start.49 = (bf16[704,1024]{1,0:T(8,128)(2,1)}, bf16[704,1024]{1,0:T(8,128)(2,1)}, u32[]{:S(2)}, u32[]{:S(2)}) collective-permute-start(bf16[704,1024]{1,0:T(8,128)(2,1)} %slice.186), channel_id=1, source_target_pairs={{0,2},{1,3},{2,0},{3,1},{4,6},{5,7},{6,4},{7,5},{8,10},{9,11},{10,... | collective-permute-start | bytes 4325384 | tf_op jit(solution)/shard_map/ppermute | solution.py:650
  473.3 60.0 %collective-permute-start.22 = (bf16[3,1024,256]{2,1,0:T(8,128)(2,1)}, bf16[3,1024,256]{2,1,0:T(8,128)(2,1)}, u32[]{:S(2)}, u32[]{:S(2)}) collective-permute-start(bf16[3,1024,256]{2,1,0:T(8,128)(2,1)} %get-tuple-element.111), channel_id=1, source_target_pairs={{0,1},{1,0},{2,3},{3,2},{4,5},{5,4},{6,7},{7,6},{8,9},{9,8},{10,11... | collective-permute-start | bytes 4718600 | tf_op jit(solution)/shard_map/ppermute | solution.py:650
  483.4 31.7 %collective-permute-start.18 = (f32[72,128]{1,0:T(8,128)S(1)}, f32[72,128]{1,0:T(8,128)S(1)}, u32[]{:S(2)}, u32[]{:S(2)}) collective-permute-start(f32[72,128]{1,0:T(8,128)S(1)} %fusion.15), channel_id=1, source_target_pairs={{0,2},{1,3},{2,0},{3,1},{4,6},{5,7},{6,4},{7,5},{8,10},{9,11},{10,... | collective-permute-start | bytes 110600 | tf_op jit(solution)/shard_map/ppermute | solution.py:650
  484.1 6.4 collective-permute-start.40
  485.6 38.9 %copy-start.10 = (bf16[1408,1024]{1,0:T(8,128)(2,1)S(1)}, bf16[1408,1024]{1,0:T(8,128)(2,1)}, u32[]{:S(2)}) copy-start(bf16[1408,1024]{1,0:T(8,128)(2,1)} %copy-done.9) | copy-start | bytes 8650756
  490.5 57.3 %collective-permute-start.24 = (bf16[3,1024,256]{2,1,0:T(8,128)(2,1)}, bf16[3,1024,256]{2,1,0:T(8,128)(2,1)}, u32[]{:S(2)}, u32[]{:S(2)}) collective-permute-start(bf16[3,1024,256]{2,1,0:T(8,128)(2,1)} %add_convert_fusion.4), channel_id=1, source_target_pairs={{0,2},{1,3},{2,0},{3,1},{4,6},{5,7},{6,4},{7,5},{8,10},{9,11},{10,... | collective-permute-start | bytes 4718600 | tf_op jit(solution)/shard_map/ppermute | solution.py:650
  515.1 5.0 collective-permute-start.41
  520.1 3.7 collective-permute-start.14
  521.6 9.4 %collective-permute-start.19 = (f32[72,128]{1,0:T(8,128)S(1)}, f32[72,128]{1,0:T(8,128)S(1)}, u32[]{:S(2)}, u32[]{:S(2)}) collective-permute-start(f32[72,128]{1,0:T(8,128)S(1)} %fusion.29), channel_id=1, source_target_pairs={{0,4},{4,0},{8,12},{12,8},{16,20},{20,16},{24,28},{28,24},{1,5},{5... | collective-permute-start | bytes 110600 | tf_op jit(solution)/shard_map/ppermute | solution.py:650
  523.7 9.4 %collective-permute-start.42 = (bf16[128,256]{1,0:T(8,128)(2,1)S(1)}, bf16[128,256]{1,0:T(8,128)(2,1)S(1)}, u32[]{:S(2)}, u32[]{:S(2)}) collective-permute-start(bf16[128,256]{1,0:T(8,128)(2,1)S(1)} %broadcast_select_fusion.8), channel_id=1, source_target_pairs={{0,16},{4,20},{8,24},{12,28},{16,0},{20,4},{24,8},{28,12},{1,17},{... | collective-permute-start | bytes 196616 | tf_op jit(solution)/shard_map/ppermute | solution.py:650
  526.4 116.3 %all-to-all-start.3 = ((bf16[8,160,1024]{2,1,0:T(8,128)(2,1)}), bf16[8,160,1024]{2,1,0:T(8,128)(2,1)}, u32[]{:S(2)}, u32[]{:S(2)}) async-start(bf16[8,160,1024]{2,1,0:T(8,128)(2,1)} %bitcast.98), calls=%async_computation.3 | async-start | bytes 5242880 | tf_op jit(solution)/shard_map/all_to_all | solution.py:723
  531.1 43.6 %collective-permute-start.15 = (f32[12,128]{1,0:T(8,128)S(1)}, f32[12,128]{1,0:T(8,128)S(1)}, u32[]{:S(2)}, u32[]{:S(2)}) collective-permute-start(f32[12,128]{1,0:T(8,128)S(1)} %add.141), channel_id=1, source_target_pairs={{0,8},{4,12},{8,0},{12,4},{16,24},{20,28},{24,16},{28,20},{1,9},{5... | collective-permute-start | bytes 18440 | tf_op jit(solution)/shard_map/ppermute | solution.py:650
  533.1 46.4 %collective-permute-start.20 = (f32[72,128]{1,0:T(8,128)S(1)}, f32[72,128]{1,0:T(8,128)S(1)}, u32[]{:S(2)}, u32[]{:S(2)}) collective-permute-start(f32[72,128]{1,0:T(8,128)S(1)} %add.146), channel_id=1, source_target_pairs={{0,8},{4,12},{8,0},{12,4},{16,24},{20,28},{24,16},{28,20},{1,9},{5... | collective-permute-start | bytes 110600 | tf_op jit(solution)/shard_map/ppermute | solution.py:650
  533.3 58.6 %collective-permute-start.43 = (bf16[128,256]{1,0:T(8,128)(2,1)S(1)}, bf16[128,256]{1,0:T(8,128)(2,1)S(1)}, u32[]{:S(2)}, u32[]{:S(2)}) collective-permute-start(bf16[128,256]{1,0:T(8,128)(2,1)S(1)} %add_convert_fusion.17), channel_id=1, source_target_pairs={{0,16},{4,20},{8,24},{12,28},{16,0},{20,4},{24,8},{28,12},{1,17},{... | collective-permute-start | bytes 196616 | tf_op jit(solution)/shard_map/ppermute | solution.py:650
  551.0 41.1 %collective-permute-start.25 = (bf16[768,256]{1,0:T(8,128)(2,1)S(1)}, bf16[768,256]{1,0:T(8,128)(2,1)S(1)}, u32[]{:S(2)}, u32[]{:S(2)}) collective-permute-start(bf16[768,256]{1,0:T(8,128)(2,1)S(1)} %get-tuple-element.132), channel_id=1, source_target_pairs={{0,4},{4,0},{8,12},{12,8},{16,20},{20,16},{24,28},{28,24},{1,5},{5... | collective-permute-start | bytes 1179656 | tf_op jit(solution)/shard_map/ppermute | solution.py:650
  552.5 39.6 %collective-permute-start.31 = (bf16[768,256]{1,0:T(8,128)(2,1)S(1)}, bf16[768,256]{1,0:T(8,128)(2,1)S(1)}, u32[]{:S(2)}, u32[]{:S(2)}) collective-permute-start(bf16[768,256]{1,0:T(8,128)(2,1)S(1)} %get-tuple-element.133), channel_id=1, source_target_pairs={{0,8},{4,12},{8,0},{12,4},{16,24},{20,28},{24,16},{28,20},{1,9},{5... | collective-permute-start | bytes 1179656 | tf_op jit(solution)/shard_map/ppermute | solution.py:650
  574.7 52.6 %collective-permute-start.16 = (f32[12,128]{1,0:T(8,128)S(1)}, f32[12,128]{1,0:T(8,128)S(1)}, u32[]{:S(2)}, u32[]{:S(2)}) collective-permute-start(f32[12,128]{1,0:T(8,128)S(1)} %add.142), channel_id=1, source_target_pairs={{0,16},{4,20},{8,24},{12,28},{16,0},{20,4},{24,8},{28,12},{1,17},{... | collective-permute-start | bytes 18440 | tf_op jit(solution)/shard_map/ppermute | solution.py:650
  580.1 48.0 %collective-permute-start.21 = (f32[72,128]{1,0:T(8,128)}, f32[72,128]{1,0:T(8,128)}, u32[]{:S(2)}, u32[]{:S(2)}) collective-permute-start(f32[72,128]{1,0:T(8,128)} %add.147), channel_id=1, source_target_pairs={{0,16},{4,20},{8,24},{12,28},{16,0},{20,4},{24,8},{28,12},{1,17},{... | collective-permute-start | bytes 110600 | tf_op jit(solution)/shard_map/ppermute | solution.py:650
  592.0 24.8 %collective-permute-start.44 = (bf16[256,256]{1,0:T(8,128)(2,1)S(1)}, bf16[256,256]{1,0:T(8,128)(2,1)S(1)}, u32[]{:S(2)}, u32[]{:S(2)}) collective-permute-start(bf16[256,256]{1,0:T(8,128)(2,1)S(1)} %maximum_select_fusion.8), channel_id=1, source_target_pairs={{0,8},{4,12},{8,0},{12,4},{16,24},{20,28},{24,16},{28,20},{1,9},{5... | collective-permute-start | bytes 393224 | tf_op jit(solution)/shard_map/ppermute | solution.py:650
  592.5 6.9 %collective-permute-start.26 = (bf16[384,256]{1,0:T(8,128)(2,1)S(1)}, bf16[384,256]{1,0:T(8,128)(2,1)S(1)}, u32[]{:S(2)}, u32[]{:S(2)}) collective-permute-start(bf16[384,256]{1,0:T(8,128)(2,1)S(1)} %broadcast_select_fusion.4), channel_id=1, source_target_pairs={{0,8},{4,12},{8,0},{12,4},{16,24},{20,28},{24,16},{28,20},{1,9},{5... | collective-permute-start | bytes 589832 | tf_op jit(solution)/shard_map/ppermute | solution.py:650
  594.5 6.3 collective-permute-start.32
  599.4 9.8 %collective-permute-start.27 = (bf16[192,256]{1,0:T(8,128)(2,1)S(1)}, bf16[192,256]{1,0:T(8,128)(2,1)S(1)}, u32[]{:S(2)}, u32[]{:S(2)}) collective-permute-start(bf16[192,256]{1,0:T(8,128)(2,1)S(1)} %broadcast_select_fusion.7), channel_id=1, source_target_pairs={{0,16},{4,20},{8,24},{12,28},{16,0},{20,4},{24,8},{28,12},{1,17},{... | collective-permute-start | bytes 294920 | tf_op jit(solution)/shard_map/ppermute | solution.py:650
  600.9 10.2 %collective-permute-start.33 = (bf16[192,256]{1,0:T(8,128)(2,1)S(1)}, bf16[192,256]{1,0:T(8,128)(2,1)S(1)}, u32[]{:S(2)}, u32[]{:S(2)}) collective-permute-start(bf16[192,256]{1,0:T(8,128)(2,1)S(1)} %broadcast_select_fusion.6), channel_id=1, source_target_pairs={{0,16},{4,20},{8,24},{12,28},{16,0},{20,4},{24,8},{28,12},{1,17},{... | collective-permute-start | bytes 294920 | tf_op jit(solution)/shard_map/ppermute | solution.py:650
  609.3 7.3 %collective-permute-start.28 = (bf16[192,256]{1,0:T(8,128)(2,1)S(1)}, bf16[192,256]{1,0:T(8,128)(2,1)S(1)}, u32[]{:S(2)}, u32[]{:S(2)}) collective-permute-start(bf16[192,256]{1,0:T(8,128)(2,1)S(1)} %add_convert_fusion.16), channel_id=1, source_target_pairs={{0,16},{4,20},{8,24},{12,28},{16,0},{20,4},{24,8},{28,12},{1,17},{... | collective-permute-start | bytes 294920 | tf_op jit(solution)/shard_map/ppermute | solution.py:650
  611.1 8.1 %collective-permute-start.34 = (bf16[192,256]{1,0:T(8,128)(2,1)S(1)}, bf16[192,256]{1,0:T(8,128)(2,1)S(1)}, u32[]{:S(2)}, u32[]{:S(2)}) collective-permute-start(bf16[192,256]{1,0:T(8,128)(2,1)S(1)} %add_convert_fusion.15), channel_id=1, source_target_pairs={{0,16},{4,20},{8,24},{12,28},{16,0},{20,4},{24,8},{28,12},{1,17},{... | collective-permute-start | bytes 294920 | tf_op jit(solution)/shard_map/ppermute | solution.py:650
  616.7 5.7 collective-permute-start.29
  616.9 17.9 %collective-permute-start.45 = (bf16[512,256]{1,0:T(8,128)(2,1)S(1)}, bf16[512,256]{1,0:T(8,128)(2,1)}, u32[]{:S(2)}, u32[]{:S(2)}) collective-permute-start(bf16[512,256]{1,0:T(8,128)(2,1)S(1)} %maximum_select_fusion.5), channel_id=1, source_target_pairs={{0,4},{4,0},{8,12},{12,8},{16,20},{20,16},{24,28},{28,24},{1,5},{5... | collective-permute-start | bytes 786440 | tf_op jit(solution)/shard_map/ppermute | solution.py:650
  620.0 10.8 %collective-permute-start.35 = (bf16[384,256]{1,0:T(8,128)(2,1)}, bf16[384,256]{1,0:T(8,128)(2,1)}, u32[]{:S(2)}, u32[]{:S(2)}) collective-permute-start(bf16[384,256]{1,0:T(8,128)(2,1)} %maximum_select_fusion.7), channel_id=1, source_target_pairs={{0,4},{4,0},{8,12},{12,8},{16,20},{20,16},{24,28},{28,24},{1,5},{5... | collective-permute-start | bytes 589832 | tf_op jit(solution)/shard_map/ppermute | solution.py:650
  622.6 15.2 %collective-permute-start.30 = (bf16[768,256]{1,0:T(8,128)(2,1)S(1)}, bf16[768,256]{1,0:T(8,128)(2,1)}, u32[]{:S(2)}, u32[]{:S(2)}) collective-permute-start(bf16[768,256]{1,0:T(8,128)(2,1)S(1)} %maximum_select_fusion.3), channel_id=1, source_target_pairs={{0,4},{4,0},{8,12},{12,8},{16,20},{20,16},{24,28},{28,24},{1,5},{5... | collective-permute-start | bytes 1179656 | tf_op jit(solution)/shard_map/ppermute | solution.py:650
  632.1 8.3 %collective-permute-start.36 = (bf16[768,256]{1,0:T(8,128)(2,1)S(1)}, bf16[768,256]{1,0:T(8,128)(2,1)S(1)}, u32[]{:S(2)}, u32[]{:S(2)}) collective-permute-start(bf16[768,256]{1,0:T(8,128)(2,1)S(1)} %maximum_select_fusion.4), channel_id=1, source_target_pairs={{0,8},{4,12},{8,0},{12,4},{16,24},{20,28},{24,16},{28,20},{1,9},{5... | collective-permute-start | bytes 1179656 | tf_op jit(solution)/shard_map/ppermute | solution.py:650
  (16 other events, 65.8 us)

commit v2 on v1

--- a/solution.py
+++ b/solution.py
@@ -106,8 +106,7 @@
     for k in range(2):
         own = jnp.sum(jnp.where(routes[k : k + 1] == label, before, 0.0), 0, keepdims=True)
         slots.append(own.astype(I32) + routes[k : k + 1] * capacity)
-    slots += [slots[k] + routes[k : k + 1] * EXTRA for k in range(2)]
-    slots = jnp.concatenate(slots + slots, 0)
+    slots = jnp.concatenate(slots * 4, 0)
     row_ref[...] = slots
     col_ref[...] = slots.astype(F32).T.astype(I32)
     place_rows(slots, cot_ref[...], out_ref)
@@ -378,7 +377,7 @@
     groups, experts, where_ref, x_ref, gain_ref, router_ref, row_ref, col_ref, *refs
 ):
     mix_refs, out_refs = refs[:groups], refs[groups : 2 * groups]
-    hidden_ref, norm_ref, gate_ref, sent_ref, mixed_ref = refs[2 * groups :]
+    hidden_ref, norm_ref, gate_ref, sent_ref, sent_gate_ref, mixed_ref = refs[2 * groups :]
     place = where_ref[0]
     gather_lanes(mix_refs, place, mixed_ref)
     for group in range(groups):
@@ -388,10 +387,9 @@
         hidden_ref[:, lanes] = x_ref[:, lanes].astype(F32) + branch
     unit, _ = unit_norm(hidden_ref[...])
     norm_ref[...] = (unit * gain_ref[1:2, :]).astype(BF16)
-    place_rows(row_ref[2:4, :], norm_ref[...], sent_ref)
+    place_rows(row_ref[...], norm_ref[...], sent_ref)
     logits = dot_nt(norm_ref[...], router_ref[...])
-    stride = sent_ref.shape[0] // experts
-    capacity = stride - EXTRA
+    capacity = sent_ref.shape[0] // experts
     slots = [col_ref[:, k : k + 1] for k in range(2)]
     lane = iota(logits.shape, 1)
     chosen = []
@@ -403,20 +401,14 @@
     gates = [power / (powers[0] + powers[1]) for power in powers]
     for k in range(2):
         gate_ref[:, k : k + 1] = gates[k]
-    span = -(-capacity // TILE) * TILE
-    lane = iota((slots[0].shape[0], span), 1)
-    below = iota((EXTRA, span), 0)
+    lane = iota((slots[0].shape[0], sent_gate_ref.shape[2]), 1)
     for expert in range(experts):
         label = jnp.where(lane < capacity, lane + expert * capacity, -1)
         part = 0.0
         for k in range(2):
             part = part + jnp.where(label == slots[k], gates[k], 0.0)
-        high, middle, low = split_three(jnp.sum(part, 0, keepdims=True))
-        block = jnp.where(
-            below == 0, high, jnp.where(below == 1, middle, jnp.where(below == 2, low, 0.0))
-        )
-        first = expert * stride + capacity
-        sent_ref[first : first + EXTRA, :span] = block.astype(BF16)
+        line = jnp.sum(part, 0, keepdims=True)
+        sent_gate_ref[expert] = jnp.broadcast_to(line, sent_gate_ref.shape[1:])
 
 
 def dispatch(where, tokens, gains, router_t, slots_row, slots_col, mixed, out_weights, capacity):
@@ -429,7 +421,8 @@
             shape_of((count, width), F32),
             shape_of((count, width), BF16),
             shape_of((count, 2), F32),
-            shape_of((experts * (capacity + EXTRA), width), BF16),
+            shape_of((experts * capacity, width), BF16),
+            shape_of((experts, EXTRA, -(-capacity // TILE) * TILE), F32),
         ),
         (where, tokens, gains, router_t, slots_row, slots_col, *mixed, *out_weights),
         [SMEM] + [VMEM] * (5 + 2 * groups),
@@ -472,16 +465,15 @@
     mixed_ref, branch_ref = refs[3 * groups + 4 :]
     place = where_ref[0]
     total = rows_ref.shape[0]
-    capacity = total // experts - EXTRA
+    capacity = total // experts
     gates = [gate_ref[:, k : k + 1] for k in range(2)]
     slots = [col_ref[:, k : k + 1] for k in range(2)]
     gate_grads = []
     hits = None
     for k in range(2):
-        hit = onehot_columns(slots[k], 0, gate_grad_ref.shape[1])
+        hit = onehot_columns(slots[k], 0, total)
         picked = jnp.where(hit, gate_grad_ref[...], 0.0)
         gate_grads.append(jnp.sum(picked, -1, keepdims=True))
-        hit = onehot_columns(col_ref[:, 2 + k : 3 + k], 0, total)
         hits = hit if hits is None else hits | hit
     hits = hits.astype(F32).astype(BF16)
     mean = gates[0] * gate_grads[0] + gates[1] * gate_grads[1]
@@ -560,6 +552,295 @@
         [VMEM] * 4,
         name="finish",
     )
+
+
+def flip(value, change, size):
+    result = 0
+    bit = 1
+    while bit < size:
+        one, two = lax.rem(lax.div(value, bit), 2), lax.rem(lax.div(change, bit), 2)
+        result = result + bit * (one + two - 2 * one * two)
+        bit *= 2
+    return result
+
+
+def column_of(row, size):
+    spot = iota((size, row.shape[1]), 0) == iota((size, row.shape[1]), 1)
+    return jnp.sum(jnp.where(spot, row, 0.0), 1, keepdims=True)
+
+
+def row_of(column, lanes):
+    spot = iota((column.shape[0], lanes), 0) == iota((column.shape[0], lanes), 1)
+    return jnp.sum(jnp.where(spot, column, 0.0), 0, keepdims=True)
+
+
+def moe_body(size, groups, chunk, sent_ref, gates_ref, outer_ref, *refs):
+    in_refs, down_refs = refs[:groups], refs[groups : 2 * groups]
+    refs = refs[2 * groups :]
+    back_out, extra_out, made_out = refs[:3]
+    grad_outs = refs[3 : 3 + groups]
+    (
+        buf, rows, gates, outer, low_outer, made_sum, back_sum, act, low, stage, extra_stage,
+        made, grad_stage, weight_sems, send_sems, recv_sems, give_sems, take_sems, own_sems,
+        save_sems, grad_sems,
+    ) = refs[3 + groups :]
+    share = down_refs[0].shape[0]
+    part_size = share * groups // 2
+    capacity, width = outer.shape[1:]
+    both = 2 * capacity
+    me = lax.axis_index("dp")
+    pairs = size // 2
+    my_pair = lax.div(me, 2)
+    mesh_id = pl.DeviceIdType.MESH
+
+    barrier = pltpu.get_barrier_semaphore()
+    for step in range(1, size):
+        peer = flip(me, step, size)
+        pl.semaphore_signal(barrier, inc=1, device_id={"dp": peer}, device_id_type=mesh_id)
+    pl.semaphore_wait(barrier, size - 1)
+
+    def remote(source, target, sent, got, peer):
+        return pltpu.make_async_remote_copy(
+            src_ref=source, dst_ref=target, send_sem=sent, recv_sem=got,
+            device_id={"dp": peer}, device_id_type=mesh_id,
+        )
+
+    def forth(source, target, peer):
+        return (
+            remote(sent_ref.at[source], rows.at[target], send_sems.at[source, 0],
+                   recv_sems.at[target, 0], peer),
+            remote(gates_ref.at[source], gates.at[target], send_sems.at[source, 1],
+                   recv_sems.at[target, 1], peer),
+        )
+
+    def back_copies(source, target, peer):
+        return (
+            remote(stage.at[source], back_out.at[target], give_sems.at[source, 0],
+                   take_sems.at[target, 0], peer),
+            remote(extra_stage.at[source], extra_out.at[target], give_sems.at[source, 1],
+                   take_sems.at[target, 1], peer),
+        )
+
+    own = (
+        pltpu.make_async_copy(sent_ref.at[me], rows.at[me], own_sems.at[0]),
+        pltpu.make_async_copy(gates_ref.at[me], gates.at[me], own_sems.at[1]),
+        pltpu.make_async_copy(outer_ref, outer, own_sems.at[2]),
+    )
+    own_back = (
+        pltpu.make_async_copy(stage.at[me], back_out.at[me], own_sems.at[3]),
+        pltpu.make_async_copy(extra_stage.at[me], extra_out.at[me], own_sems.at[4]),
+    )
+    for copy in own:
+        copy.start()
+    for step in range(1, size):
+        peer = flip(me, step, size)
+        for copy in forth(peer, me, peer):
+            copy.start()
+
+    def weight_copies(group):
+        spot = pl.ds(group * share, share)
+        return (
+            pltpu.make_async_copy(in_refs[group], buf.at[0:2, spot], weight_sems.at[group, 0]),
+            pltpu.make_async_copy(down_refs[group], buf.at[2, spot], weight_sems.at[group, 1]),
+        )
+
+    for group in range(groups):
+        for copy in weight_copies(group):
+            copy.start()
+    for copy in own:
+        copy.wait()
+
+    def hidden_part(pair, base):
+        spot = pl.ds(pl.multiple_of(pair * both, both), both)
+        two = pl.ds(2 * pair, 2)
+        these = rows[two].reshape(both, width)
+        outers = low_outer[spot, :]
+        for first in range(0, part_size, chunk):
+            last = min(first + chunk, part_size)
+            part, lanes = slice(base + first, base + last), slice(first, last)
+            gate, up = dot_nt(these, buf[0, part, :]), dot_nt(these, buf[1, part, :])
+            act_grad = dot_nt(outers, buf[2, part, :])
+            square = gate * gate
+            inner = gate * (0.7978845608028654 + (0.7978845608028654 * 0.044715) * square)
+            rise = 0.5 + 0.5 * jnp.tanh(inner)
+            bent = gate * rise
+            act[spot, lanes] = (bent * up).astype(BF16)
+            slope = rise + bent * (1.0 - rise) * (
+                2 * 0.7978845608028654 + (6 * 0.7978845608028654 * 0.044715) * square
+            )
+            low[0, spot, lanes] = (act_grad * up * slope).astype(BF16)
+            low[1, spot, lanes] = (act_grad * bent).astype(BF16)
+        whole = slice(base, base + part_size)
+        result = dot_nn(act[spot, :], buf[2, whole, :])
+        back = dot_nn(low[0, spot, :], buf[0, whole, :]) + dot_nn(low[1, spot, :], buf[1, whole, :])
+        return spot, result, back
+
+    def near_step(step, carry):
+        pair = flip(my_pair, step, pairs)
+        first = 2 * pair
+
+        @pl.when(step == 0)
+        def _():
+            peer = flip(me, 1, size)
+            for copy in forth(me, peer, peer):
+                copy.wait_recv()
+
+        @pl.when(step > 0)
+        def _():
+            for which in range(2):
+                for copy in forth(me, first + which, first + which):
+                    copy.wait_recv()
+
+        for which in range(2):
+            gate = column_of(gates[first + which, 0:1, :], capacity)
+            spot = pl.ds(pl.multiple_of((first + which) * capacity, capacity), capacity)
+            low_outer[spot, :] = (outer[first + which].astype(F32) * gate).astype(BF16)
+        spot, result, back = hidden_part(pair, 0)
+        made_sum[spot, :] = result
+        back_sum[spot, :] = back
+        return carry
+
+    def weight_grads(half):
+        every = rows[...].reshape(size * capacity, width)
+        outers = low_outer[...]
+        count = 0
+        base = half * part_size
+        waiting = {}
+        for c in range(3):
+            source = act if c == 2 else low.at[c]
+            for first in range(0, part_size, 2 * chunk):
+                last = min(first + 2 * chunk, part_size)
+                slot = count % 2
+                for copy in waiting.pop(slot, ()):
+                    copy.wait()
+                piece = dot_tn(source[:, first:last], outers if c == 2 else every)
+                grad_stage[slot, : last - first, :] = piece.astype(BF16)
+                copies = []
+                begin = base + first
+                while begin < base + last:
+                    group = begin // share
+                    end = min(base + last, (group + 1) * share)
+                    copies.append(
+                        pltpu.make_async_copy(
+                            grad_stage.at[slot, pl.ds(begin - base - first, end - begin)],
+                            grad_outs[group].at[c, pl.ds(begin - group * share, end - begin)],
+                            grad_sems.at[slot, len(copies)],
+                        )
+                    )
+                    begin = end
+                for copy in copies:
+                    copy.start()
+                waiting[slot] = copies
+                count += 1
+        for copies in waiting.values():
+            for copy in copies:
+                copy.wait()
+
+    for group in range(groups // 2):
+        for copy in weight_copies(group):
+            copy.wait()
+    lax.fori_loop(0, pairs, near_step, 0)
+    weight_grads(0)
+
+    def far_step(step, carry):
+        pair = flip(my_pair, pairs - 1 - step, pairs)
+        first = 2 * pair
+        spot, result, back = hidden_part(pair, part_size)
+        result = (made_sum[spot, :] + result).astype(BF16)
+        back = (back_sum[spot, :] + back).astype(BF16)
+        two = pl.ds(first, 2)
+        made[two] = result.reshape(2, capacity, width)
+        stage[two] = back.reshape(2, capacity, width)
+        for which in range(2):
+            grads = outer[first + which].astype(F32) * made[first + which].astype(F32)
+            line = row_of(jnp.sum(grads, -1, keepdims=True), extra_stage.shape[2])
+            extra_stage[first + which] = jnp.broadcast_to(line, extra_stage.shape[1:])
+        pltpu.make_async_copy(made.at[two], made_out.at[two], save_sems.at[step]).start()
+
+        @pl.when(step < pairs - 1)
+        def _():
+            for which in range(2):
+                for copy in back_copies(first + which, me, first + which):
+                    copy.start()
+
+        @pl.when(step == pairs - 1)
+        def _():
+            peer = flip(me, 1, size)
+            for copy in back_copies(peer, me, peer):
+                copy.start()
+            for copy in own_back:
+                copy.start()
+
+        return carry
+
+    for group in range(groups // 2, groups):
+        for copy in weight_copies(group):
+            copy.wait()
+    lax.fori_loop(0, pairs, far_step, 0)
+    weight_grads(1)
+    for copy in own_back:
+        copy.wait()
+    for step in range(pairs):
+        two = pl.ds(2 * flip(my_pair, pairs - 1 - step, pairs), 2)
+        pltpu.make_async_copy(made.at[two], made_out.at[two], save_sems.at[step]).wait()
+    for step in range(1, size):
+        peer = flip(me, step, size)
+        for copy in forth(peer, me, peer):
+            copy.wait_send()
+        for copy in back_copies(peer, me, peer):
+            copy.wait_send()
+        for copy in back_copies(me, peer, peer):
+            copy.wait_recv()
+
+
+def moe(sent, gates, outer, in_weights, down_weights, chunk=256):
+    size, capacity, width = sent.shape
+    groups = len(in_weights)
+    share = down_weights[0].shape[0]
+    part = share * groups // 2
+    total = size * capacity
+    extra = gates.shape[1:]
+    dma = pltpu.SemaphoreType.DMA
+    result = pl.pallas_call(
+        functools.partial(moe_body, size, groups, chunk),
+        out_shape=(
+            shape_of((size, capacity, width), BF16),
+            shape_of((size, *extra), F32),
+            shape_of((size, capacity, width), BF16),
+        )
+        + (shape_of((3, share, width), BF16),) * groups,
+        in_specs=[ANY] * (3 + 2 * groups),
+        out_specs=(ANY,) * (3 + groups),
+        scratch_shapes=[
+            pltpu.VMEM((3, share * groups, width), BF16),
+            pltpu.VMEM((size, capacity, width), BF16),
+            pltpu.VMEM((size, *extra), F32),
+            pltpu.VMEM((size, capacity, width), BF16),
+            pltpu.VMEM((total, width), BF16),
+            pltpu.VMEM((total, width), F32),
+            pltpu.VMEM((total, width), F32),
+            pltpu.VMEM((total, part), BF16),
+            pltpu.VMEM((2, total, part), BF16),
+            pltpu.VMEM((size, capacity, width), BF16),
+            pltpu.VMEM((size, *extra), F32),
+            pltpu.VMEM((size, capacity, width), BF16),
+            pltpu.VMEM((2, 2 * chunk, width), BF16),
+            dma((groups, 2)),
+            dma((size, 2)),
+            dma((size, 2)),
+            dma((size, 2)),
+            dma((size, 2)),
+            dma((5,)),
+            dma((size // 2,)),
+            dma((2, 3)),
+        ],
+        cost_estimate=pl.CostEstimate(flops=LIGHT, bytes_accessed=LIGHT, transcendentals=0),
+        compiler_params=pltpu.CompilerParams(
+            collective_id=0, has_side_effects=True, vmem_limit_bytes=66_000_000
+        ),
+        name="experts",
+    )(sent, gates, outer, *in_weights, *down_weights)
+    return result[:3], list(result[3:])
 
 
 def expert_body(groups, chunk, rows_ref, outer_ref, gate_ref, *refs):
@@ -645,6 +926,26 @@
     )(rows, outer, gate_column, *in_weights, *down_weights)
 
 
+def moe_plain(sent, gates, outer, in_weights, down_weights):
+    size, capacity, width = sent.shape
+    total = size * capacity
+    rows = exchange(sent.reshape(total, width), "dp").reshape(total, width)
+    gate_column = lax.all_to_all(gates, "dp", 0, 0, tiled=True)[:, 0, :capacity].reshape(total, 1)
+    made, back, outer_low, gate_grads, act, low = experts_pass(
+        rows, outer.reshape(total, width), gate_column, in_weights, down_weights
+    )
+    extra = jnp.pad(gate_grads.reshape(size, 1, capacity), ((0, 0), (0, EXTRA - 1), (0, 0)))
+    extra = lax.all_to_all(extra, "dp", 0, 0, tiled=True)
+    share = down_weights[0].shape[0]
+    grads = []
+    for group in range(len(in_weights)):
+        part = slice(group * share, (group + 1) * share)
+        pieces = [dot_tn(low[c, :, part], rows) for c in range(2)]
+        grads.append(jnp.stack(pieces + [dot_tn(act[:, part], outer_low)]).astype(BF16))
+    shape = (size, capacity, width)
+    return (exchange(back, "dp"), extra, made.reshape(shape)), grads
+
+
 def swap(value, axis, bit):
     size = lax.axis_size(axis)
     return lax.ppermute(value, axis, [(i, i ^ bit) for i in range(size)])
@@ -753,7 +1054,7 @@
 
     qkv_far = gather_far(attn_qkv, "wshard")
     slots_row, slots_col, outer_sent = route(routes, cotangent, experts, capacity)
-    outer_rows = exchange(outer_sent, "dp").reshape(total, model_width)
+    outer_rows = exchange(outer_sent, "dp")
     qkv_all = gather_near(qkv_far, "wshard")
     out_far = gather_far(after(attn_out, qkv_far[2]), "wshard")
     out_all = gather_near(out_far, "wshard")
@@ -770,45 +1071,25 @@
         qkv.append(one[0])
         mixed.append(one[1])
         turn = after(where, one[1])
-    hidden, normed_two, gates, sent = dispatch(
+    hidden, normed_two, gates, sent, sent_gates = dispatch(
         turn, tokens, norm_gains, router_t, slots_row, slots_col, mixed, out_all, capacity
     )
-    arrived = exchange(sent, "dp")
-    rows = arrived[:, :capacity].reshape(total, model_width)
-    gate_column = jnp.sum(arrived[:, capacity : capacity + 3, :capacity].astype(F32), 1)
-    gate_column = gate_column.reshape(total, 1)
-
-    order = [g for g in range(groups) if g % 2 == 0] + [g for g in range(groups) if g % 2]
-    made, back, outer_low, gate_grads, act, low = experts_pass(
-        rows, outer_rows, gate_column, [in_all[g] for g in order], [down_all[g] for g in order]
-    )
-    owners = total // capacity
-    extra = jnp.stack(split_three(gate_grads.reshape(owners, capacity)), 1).astype(BF16)
-    extra = jnp.pad(extra, ((0, 0), (0, EXTRA - 3), (0, model_width - capacity)))
-    message = jnp.concatenate([back.reshape(owners, capacity, model_width), extra], 1)
-    back_rows = exchange(message.reshape(-1, model_width), "dp")
-    gate_grad_row = jnp.sum(back_rows[:, capacity : capacity + 3, :capacity].astype(F32), 1)
-    gate_grad_row = gate_grad_row.reshape(1, total)
-    back_rows = back_rows.reshape(-1, model_width)
-
-    half = act.shape[1] // 2
-    far_part = [low[0, :, half:], low[1, :, half:], act[:, half:]]
-    near_part = [low[0, :, :half], low[1, :, :half], act[:, :half]]
-    right = [rows, rows, outer_low]
-    sums = []
-    for far_one, near_one, rows_one in zip(far_part, near_part, right):
-        got = swap(dot_tn(far_one, rows_one).astype(BF16), "wshard", 1)
-        sums.append((dot_tn(near_one, rows_one) + got.astype(F32)).astype(BF16))
-    share = half // 2
-    sums = [s[:share].astype(F32) + swap(s[share:], "wshard", 2).astype(F32) for s in sums]
-    grad_expert_in = jnp.swapaxes(jnp.stack(sums[:2]), 1, 2)[None]
-    grad_expert_down = sums[2][None]
+
+    through = moe if capacity % 16 == 0 else moe_plain
+    (back_rows, back_extra, made), expert_grads = through(
+        sent.reshape(-1, capacity, model_width), sent_gates, outer_rows, in_all, down_all
+    )
+    gate_grad_row = back_extra[:, 0, :capacity].reshape(1, total)
+    back_rows = back_rows.reshape(total, model_width)
+    expert_sum = scatter_sum(expert_grads, "wshard")
+    grad_expert_in = jnp.swapaxes(expert_sum[:2], 1, 2)[None]
+    grad_expert_down = expert_sum[2][None]
 
     (grad_hidden, mixed_grad, router_grad, gain_two), out_grads = undispatch(
         where, norm_gains, jnp.concatenate([router_t] * 3, 0), slots_col, gates, gate_grad_row,
         hidden, normed_two, cotangent, back_rows, mixed, out_all,
     )
-    made_rows = exchange(after(made, back_rows), "dp").reshape(total, model_width)
+    made_rows = exchange(made.reshape(total, model_width), "dp").reshape(total, model_width)
     bits = bits_of("dp")
     other_bits = [bits[1], bits[0]] + bits[2:]
     out_sum = scatter_sum(out_grads, "wshard").astype(BF16)

time: 654 us -> 648 us (level)
  Pallas kernels: 186 us -> 270 us
  waiting for transfers between devices: 293 us -> 241 us
  matrix products: 48.2 us -> 1.07 us
    all_to_all x4 -> x2, waiting for transfers between devices: 106 us -> 0.01 us  [exchange(): return lax.all_to_all(blocks, axis, 0, 0, tiled=True)]
    pallas_call x1, Pallas kernels: 59.2 us -> 144 us  [moe(): pl.pallas_call(functools.partial(moe_body, size, groups, chunk), out_shap...]
    ppermute x52 -> x49, waiting for transfers between devices: 187 us -> 241 us  [swap(): return lax.ppermute(value, axis, [(i, i ^ bit) for i in range(size)])]
    dot_general x6 -> x0, matrix products: 45.6 us -> none  [dot_tn(): lax.dot_general(a, b, (((0,), (0,)), ((), ())), preferred_element_type=F32)]
    ppermute x52 -> x49, starting transfers between devices: 51.1 us -> 62.3 us  [swap(): return lax.ppermute(value, axis, [(i, i ^ bit) for i in range(size)])]
    add x0 -> x1, other arithmetic: none -> 7.89 us  [scatter_sum(): held[place].astype(F32) + piece.astype(F32)]
    convert_element_type x2 -> x3, other arithmetic: 3.2 us -> 10.5 us  [scatter_sum(): (held[place].astype(F32) + piece.astype(F32)).astype(F32 if last else BF16)]
    all_to_all x4 -> x2, starting transfers between devices: 18.7 us -> 11.8 us  [exchange(): return lax.all_to_all(blocks, axis, 0, 0, tiled=True)]
  transfers between devices with their start and end apart: 56 -> 51, of which waited for: 24 -> 21; matrix products, arithmetic and copies ran while one was open for 13% -> 5% of each run, Pallas kernels for 17% -> 20%
where the time goes in v2:
time: 648 us; the launch traced here: 638 us
  Pallas kernels  270 us (42%)
  waiting for transfers between devices  241 us (37%)
  starting transfers between devices  74.1 us (11%)
  other arithmetic  36.6 us (6%)
  local copies, waits for them, and re-layouts  13.1 us (2%)
    ppermute x49, waiting for transfers between devices, swap(): return lax.ppermute(value, axis, [(i, i ^ bit) for i in range(size)])  241 us
    pallas_call x1, Pallas kernels, moe(): pl.pallas_call(functools.partial(moe_body, size, groups, chunk), out_shap...  144 us
    pallas_call x13, Pallas kernels, call(): pl.pallas_call(body, out_shape=out, in_specs=specs, out_specs=jax.tree.ma...  126 us
    ppermute x49, starting transfers between devices, swap(): return lax.ppermute(value, axis, [(i, i ^ bit) for i in range(size)])  62.3 us
  transfers between devices with their start and end apart: 51, of which 21 were waited for; matrix products, arithmetic and copies ran while one was open for 5% of the time, Pallas kernels for 20%

profile of v2, /device:TPU:0, one launch (start us, length us, event | category | flops | bytes accessed | tf_op | source)
XLA Modules:
  0.0 638.2 jit_solution(6522572034960951108)
XLA Ops:
  0.7 3.0 collective-permute-start.1
  3.7 34.7 %collective-permute-done.1.w_ref = bf16[3,1024,256]{2,1,0:T(8,128)(2,1)} collective-permute-done((bf16[3,1024,256]{2,1,0:T(8,128)(2,1)}, bf16[3,1024,256]{2,1,0:T(8,128)(2,1)}, u32[]{:S(2)}, u32[]{:S(2)}) %collective-permute-start.1) | collective-permute-done | bytes 1572896 | tf_op jit(solution)/shard_map/ppermute | solution.py:951
  38.4 1.7 collective-permute-start.4
  40.1 11.6 %collective-permute-done.4.refs_6_ = bf16[1024,256]{1,0:T(8,128)(2,1)S(1)} collective-permute-done((bf16[1024,256]{1,0:T(8,128)(2,1)}, bf16[1024,256]{1,0:T(8,128)(2,1)S(1)}, u32[]{:S(2)}, u32[]{:S(2)}) %collective-permute-start.4) | collective-permute-done | bytes 524320 | tf_op jit(solution)/shard_map/ppermute | solution.py:951
  53.1 4.5 route.1
  57.6 5.9 all-to-all-start
  64.1 50.7 %collective-permute-done.7.refs_2_ = bf16[2,704,1024]{2,1,0:T(8,128)(2,1)} collective-permute-done((bf16[2,704,1024]{2,1,0:T(8,128)(2,1)}, bf16[2,704,1024]{2,1,0:T(8,128)(2,1)}, u32[]{:S(2)}, u32[]{:S(2)}) %collective-permute-start.7) | collective-permute-done | bytes 2883616 | tf_op jit(solution)/shard_map/ppermute | solution.py:951
  116.5 6.6 %collective-permute-done.3.refs_5_ = bf16[1024,256]{1,0:T(8,128)(2,1)S(1)} collective-permute-done((bf16[1024,256]{1,0:T(8,128)(2,1)S(1)}, bf16[1024,256]{1,0:T(8,128)(2,1)S(1)}, u32[]{:S(2)}, u32[]{:S(2)}) %collective-permute-start.3) | collective-permute-done | bytes 524320 | tf_op jit(solution)/shard_map/ppermute | solution.py:951
  123.2 22.8 %collective-permute-done.10.refs_6_ = bf16[704,1024]{1,0:T(8,128)(2,1)} collective-permute-done((bf16[704,1024]{1,0:T(8,128)(2,1)}, bf16[704,1024]{1,0:T(8,128)(2,1)}, u32[]{:S(2)}, u32[]{:S(2)}) %collective-permute-start.10) | collective-permute-done | bytes 1441824 | tf_op jit(solution)/shard_map/ppermute | solution.py:951
  148.7 7.9 %attend.4 = (bf16[3,512,256]{2,1,0:T(8,128)(2,1)}, bf16[512,256]{1,0:T(8,128)(2,1)}) custom-call(s32[2]{0:T(128)} %pad_add_fusion.where_ref.refs_0_, bf16[512,1024]{1,0:T(8,128)(2,1)} %x_ref.17, f32[2,1024]{1,0:T(2,128)} %gain_ref.19, f32[16,1024]{1,0:T(8,128)} %convolution_bitcast_fusion.diag_ref.refs_3_, bf16[3,1024,256]{2,1,0:T(8,128)(2,1)} %w_ref.3), custom_call_target="tpu_custom_call" | custom-call | flops 1024 | bytes 1024 | tf_op jit(solution)/shard_map/attend/pallas_call | solution.py:48
  157.2 7.9 %attend.5 = (bf16[3,512,256]{2,1,0:T(8,128)(2,1)}, bf16[512,256]{1,0:T(8,128)(2,1)}) custom-call(s32[2]{0:T(128)} %pad_add_fusion.where_ref.refs_0_, bf16[512,1024]{1,0:T(8,128)(2,1)} %x_ref.17, f32[2,1024]{1,0:T(2,128)} %gain_ref.19, f32[16,1024]{1,0:T(8,128)} %convolution_bitcast_fusion.diag_ref.refs_3_, bf16[3,1024,256]{2,1,0:T(8,128)(2,1)} %copy-done.4), custom_call_target="tpu_custom_call" | custom-call | flops 1024 | bytes 1024 | tf_op jit(solution)/shard_map/attend/pallas_call | solution.py:48
  165.1 7.9 %attend.6 = (bf16[3,512,256]{2,1,0:T(8,128)(2,1)}, bf16[512,256]{1,0:T(8,128)(2,1)}) custom-call(s32[2]{0:T(128)} %pad_add_fusion.where_ref.refs_0_, bf16[512,1024]{1,0:T(8,128)(2,1)} %x_ref.17, f32[2,1024]{1,0:T(2,128)} %gain_ref.19, f32[16,1024]{1,0:T(8,128)} %convolution_bitcast_fusion.diag_ref.refs_3_, bf16[3,1024,256]{2,1,0:T(8,128)(2,1)} %collective-permute-done.1.w_ref), custom_call_target="tpu_custom_call" | custom-call | flops 1024 | bytes 1024 | tf_op jit(solution)/shard_map/attend/pallas_call | solution.py:48
  173.0 8.1 %attend.7 = (bf16[3,512,256]{2,1,0:T(8,128)(2,1)}, bf16[512,256]{1,0:T(8,128)(2,1)}) custom-call(s32[2]{0:T(128)} %pad_add_fusion.where_ref.refs_0_, bf16[512,1024]{1,0:T(8,128)(2,1)} %x_ref.17, f32[2,1024]{1,0:T(2,128)} %gain_ref.19, f32[16,1024]{1,0:T(8,128)} %convolution_bitcast_fusion.diag_ref.refs_3_, bf16[3,1024,256]{2,1,0:T(8,128)(2,1)} %copy-done.3), custom_call_target="tpu_custom_call" | custom-call | flops 1024 | bytes 1024 | tf_op jit(solution)/shard_map/attend/pallas_call | solution.py:48
  181.9 8.6 %dispatch.1 = (f32[512,1024]{1,0:T(8,128)}, bf16[512,1024]{1,0:T(8,128)(2,1)}, f32[512,2]{1,0:T(8,128)}, bf16[1280,1024]{1,0:T(8,128)(2,1)}, f32[8,8,256]{2,1,0:T(8,128)}) custom-call(s32[2]{0:T(128)} %pad_add_fusion.where_ref.refs_0_, bf16[512,1024]{1,0:T(8,128)(2,1)} %x_ref.17, f32[2,1024]{1,0:T(2,128)} %gain_ref.19, bf16[8,1024]{1,0:T(8,128)(2,1)} %bitcast.67, ...), custom_call_target="tpu_custom_call" | custom-call | flops 1024 | bytes 1024 | tf_op jit(solution)/shard_map/dispatch/pallas_call | solution.py:48
  190.6 144.2 %experts.1 = (bf16[8,160,1024]{2,1,0:T(8,128)(2,1)}, f32[8,8,256]{2,1,0:T(8,128)}, bf16[8,160,1024]{2,1,0:T(8,128)(2,1)}, bf16[3,704,1024]{2,1,0:T(8,128)(2,1)},...) custom-call(bf16[8,160,1024]{2,1,0:T(8,128)(2,1)} %bitcast.63, ...), custom_call_target="tpu_custom_call" | custom-call | flops 1024 | bytes 1024 | tf_op jit(solution)/shard_map/experts/pallas_call | solution.py:804
  336.4 13.4 %undispatch.1 = (f32[512,1024]{1,0:T(8,128)}, bf16[512,1024]{1,0:T(8,128)(2,1)}, f32[8,1024]{1,0:T(8,128)}, f32[1,1024]{1,0:T(1,128)}, bf16[1024,256]{1,0:T(8,12...) custom-call(s32[2]{0:T(128)} %pad_add_fusion.where_ref.refs_0_, ...), custom_call_target="tpu_custom_call" | custom-call | flops 1024 | bytes 1024 | tf_op jit(solution)/shard_map/undispatch/pallas_call | solution.py:48
  350.4 13.3 %attend_back.4 = (bf16[3,1024,256]{2,1,0:T(8,128)(2,1)}, f32[512,1024]{1,0:T(8,128)}, f32[4,8,128]{2,1,0:T(8,128)}) custom-call(s32[2]{0:T(128)} %pad_add_fusion.where_ref.refs_0_, bf16[512,1024]{1,0:T(8,128)(2,1)} %x_ref.17, f32[2,1024]{1,0:T(2,128)} %gain_ref.19, f32[16,1024]{1,0:T(8,128)} %convolution_bitcast_fusion.diag_ref.refs_3_, ...), custom_call_target="tpu_custom_call" | custom-call | flops 1024 | bytes 1024 | tf_op jit(solution)/shard_map/attend_back/pallas_call | solution.py:48
  364.8 14.4 %attend_back.5 = (bf16[3,1024,256]{2,1,0:T(8,128)(2,1)}, f32[512,1024]{1,0:T(8,128)}, f32[4,8,128]{2,1,0:T(8,128)}) custom-call(s32[2]{0:T(128)} %pad_add_fusion.where_ref.refs_0_, bf16[512,1024]{1,0:T(8,128)(2,1)} %x_ref.17, f32[2,1024]{1,0:T(2,128)} %gain_ref.19, f32[16,1024]{1,0:T(8,128)} %convolution_bitcast_fusion.diag_ref.refs_3_, ...), custom_call_target="tpu_custom_call" | custom-call | flops 1024 | bytes 1024 | tf_op jit(solution)/shard_map/attend_back/pallas_call | solution.py:48
  380.0 14.3 %attend_back.6 = (bf16[3,1024,256]{2,1,0:T(8,128)(2,1)}, f32[512,1024]{1,0:T(8,128)}, f32[4,8,128]{2,1,0:T(8,128)}) custom-call(s32[2]{0:T(128)} %pad_add_fusion.where_ref.refs_0_, bf16[512,1024]{1,0:T(8,128)(2,1)} %x_ref.17, f32[2,1024]{1,0:T(2,128)} %gain_ref.19, f32[16,1024]{1,0:T(8,128)} %convolution_bitcast_fusion.diag_ref.refs_3_, ...), custom_call_target="tpu_custom_call" | custom-call | flops 1024 | bytes 1024 | tf_op jit(solution)/shard_map/attend_back/pallas_call | solution.py:48
  394.2 14.5 %attend_back.7 = (bf16[3,1024,256]{2,1,0:T(8,128)(2,1)}, f32[512,1024]{1,0:T(8,128)}, f32[4,8,128]{2,1,0:T(8,128)}) custom-call(s32[2]{0:T(128)} %pad_add_fusion.where_ref.refs_0_, bf16[512,1024]{1,0:T(8,128)(2,1)} %x_ref.17, f32[2,1024]{1,0:T(2,128)} %gain_ref.19, f32[16,1024]{1,0:T(8,128)} %convolution_bitcast_fusion.diag_ref.refs_3_, ...), custom_call_target="tpu_custom_call" | custom-call | flops 1024 | bytes 1024 | tf_op jit(solution)/shard_map/attend_back/pallas_call | solution.py:48
  410.4 1.6 collective-permute-start.39
  412.3 4.5 finish.1
  420.1 4.6 collective-permute-done.39
  424.7 1.5 collective-permute-start.13
  426.3 1.5 add_convert_fusion.5
  427.9 8.6 %collective-permute-start.40 = (bf16[512,256]{1,0:T(8,128)(2,1)S(1)}, bf16[512,256]{1,0:T(8,128)(2,1)S(1)}, u32[]{:S(2)}, u32[]{:S(2)}) collective-permute-start(bf16[512,256]{1,0:T(8,128)(2,1)S(1)} %broadcast_select_fusion.2), channel_id=1, source_target_pairs={{0,4},{4,0},{8,12},{12,8},{16,20},{20,16},{24,28},{28,24},{1,5},{5... | collective-permute-start | bytes 786440 | tf_op jit(solution)/shard_map/ppermute | solution.py:951
  436.5 1.6 add_convert_fusion.3
  438.7 3.3 collective-permute-done.40
  442.7 31.4 %collective-permute-done.18 = f32[72,128]{1,0:T(8,128)S(1)} collective-permute-done((f32[72,128]{1,0:T(8,128)S(1)}, f32[72,128]{1,0:T(8,128)S(1)}, u32[]{:S(2)}, u32[]{:S(2)}) %collective-permute-start.18) | collective-permute-done | bytes 36896 | tf_op jit(solution)/shard_map/ppermute | solution.py:951
  474.6 5.9 all-to-all-start.1
  480.6 2.1 collective-permute-start.15
  482.9 2.9 collective-permute-start.42
  485.8 2.9 add_convert_fusion.2
  488.8 8.0 %add_convert_fusion = bf16[3,704,1024]{2,1,0:T(8,128)(2,1)} fusion(bf16[3,704,1024]{2,1,0:T(8,128)(2,1)} %collective-permute-done.47, bf16[3,704,1024]{2,1,0:T(8,128)(2,1)} %get-tuple-element.121), kind=kLoop, calls=%fused_computation.1 | loop fusion | flops 8650752 | bytes 12976128 | tf_op jit(solution)/shard_map/convert_element_type | solution.py:983
  498.3 23.1 %collective-permute-done.15 = f32[12,128]{1,0:T(8,128)S(1)} collective-permute-done((f32[12,128]{1,0:T(8,128)S(1)}, f32[12,128]{1,0:T(8,128)S(1)}, u32[]{:S(2)}, u32[]{:S(2)}) %collective-permute-start.15) | collective-permute-done | bytes 6176 | tf_op jit(solution)/shard_map/ppermute | solution.py:951
  521.4 1.8 collective-permute-start.25
  523.2 17.2 %collective-permute-done.42 = bf16[128,256]{1,0:T(8,128)(2,1)S(1)} collective-permute-done((bf16[128,256]{1,0:T(8,128)(2,1)S(1)}, bf16[128,256]{1,0:T(8,128)(2,1)S(1)}, u32[]{:S(2)}, u32[]{:S(2)}) %collective-permute-start.42) | collective-permute-done | bytes 65568 | tf_op jit(solution)/shard_map/ppermute | solution.py:951
  540.4 1.5 collective-permute-start.43
  541.9 6.0 collective-permute-done.43
  547.9 3.4 collective-permute-start.16
  553.9 5.2 collective-permute-done.26
  559.1 3.1 collective-permute-start.32
  562.3 3.5 collective-permute-done.32
  565.8 2.9 collective-permute-start.27
  568.8 3.6 collective-permute-done.27
  572.4 1.9 collective-permute-start.33
  574.3 3.6 collective-permute-done.33
  577.9 2.1 collective-permute-start.28
  580.1 3.3 collective-permute-done.28
  583.4 2.7 collective-permute-start.34
  586.2 2.8 collective-permute-done.34
  589.0 4.5 collective-permute-start.29
  593.5 2.3 collective-permute-start.35
  596.6 2.3 collective-permute-start.21
  599.5 2.2 collective-permute-done.21
  605.5 1.9 collective-permute-done.45
  607.4 2.3 fusion
  609.7 2.0 collective-permute-done.30
  614.5 1.9 convert.2
  616.4 1.5 copy-done.2
  617.9 6.5 %combine.1 = bf16[512,1024]{1,0:T(8,128)(2,1)} custom-call(f32[512,1024]{1,0:T(8,128)} %get-tuple-element.78.hidden_ref, f32[512,2]{1,0:T(8,128)} %get-tuple-element.105.gate_ref, s32[512,8]{1,0:T(8,128)} %get-tuple-element.76.col_ref, bf16[1280,1024]{1,0:T(8,128)(2,1)} %bitcast.59), custom_call_target="tpu_custom_call" | custom-call | flops 1024 | bytes 1024 | tf_op jit(solution)/shard_map/combine/pallas_call | solution.py:48
  624.4 7.9 %convert_add_fusion = f32[3,704,1024]{2,1,0:T(8,128)S(1)} fusion(bf16[3,704,1024]{2,1,0:T(8,128)(2,1)} %collective-permute-done.48, bf16[3,704,1024]{2,1,0:T(8,128)(2,1)} %collective-permute-done.46, bf16[3,704,1024]{2,1,0:T(8,128)(2,1)} %get-tuple-element.119), kind=kLoop, calls=%fused_computation | loop fusion | flops 15138816 | bytes 21626880 | tf_op jit(solution)/shard_map/add | solution.py:983
  632.3 3.5 slice_bitcast_fusion
  635.8 1.9 slice.133
  (156 shorter events, 31.2 us)
Async XLA Ops:
  0.6 147.2 %copy-start = (f32[32,16]{0,1:T(8,128)S(1)}, f32[32,16]{0,1:T(8,128)}, u32[]{:S(2)}) copy-start(f32[32,16]{0,1:T(8,128)} %param.17) | copy-start | bytes 6148
  0.7 37.7 %collective-permute-start.1 = (bf16[3,1024,256]{2,1,0:T(8,128)(2,1)}, bf16[3,1024,256]{2,1,0:T(8,128)(2,1)}, u32[]{:S(2)}, u32[]{:S(2)}) collective-permute-start(bf16[3,1024,256]{2,1,0:T(8,128)(2,1)} %w_ref.3), channel_id=1, source_target_pairs={{0,2},{1,3},{2,0},{3,1},{4,6},{5,7},{6,4},{7,5},{8,10},{9,11},{10,... | collective-permute-start | bytes 4718600 | tf_op jit(solution)/shard_map/ppermute | solution.py:951
  38.4 13.3 %collective-permute-start.4 = (bf16[1024,256]{1,0:T(8,128)(2,1)}, bf16[1024,256]{1,0:T(8,128)(2,1)S(1)}, u32[]{:S(2)}, u32[]{:S(2)}) collective-permute-start(bf16[1024,256]{1,0:T(8,128)(2,1)} %refs_4_.1), channel_id=1, source_target_pairs={{0,2},{1,3},{2,0},{3,1},{4,6},{5,7},{6,4},{7,5},{8,10},{9,11},{10,... | collective-permute-start | bytes 1572872 | tf_op jit(solution)/shard_map/ppermute | solution.py:951
  51.7 94.3 %copy-start.6 = (bf16[1024,256]{1,0:T(8,128)(2,1)}, bf16[1024,256]{1,0:T(8,128)(2,1)S(1)}, u32[]{:S(2)}) copy-start(bf16[1024,256]{1,0:T(8,128)(2,1)S(1)} %collective-permute-done.4.refs_6_) | copy-start | bytes 1572868
  51.7 63.1 %collective-permute-start.7 = (bf16[2,704,1024]{2,1,0:T(8,128)(2,1)}, bf16[2,704,1024]{2,1,0:T(8,128)(2,1)}, u32[]{:S(2)}, u32[]{:S(2)}) collective-permute-start(bf16[2,704,1024]{2,1,0:T(8,128)(2,1)} %bitcast.7.refs_0_), channel_id=1, source_target_pairs={{0,2},{1,3},{2,0},{3,1},{4,6},{5,7},{6,4},{7,5},{8,10},{9,11},{10,... | collective-permute-start | bytes 8650760 | tf_op jit(solution)/shard_map/ppermute | solution.py:951
  57.6 58.8 %copy-start.5 = (bf16[1024,256]{1,0:T(8,128)(2,1)S(1)}, bf16[1024,256]{1,0:T(8,128)(2,1)}, u32[]{:S(2)}) copy-start(bf16[1024,256]{1,0:T(8,128)(2,1)} %refs_4_.1) | copy-start | bytes 1572868
  57.6 90.3 %copy-start.12 = (f32[32,1024]{1,0:T(8,128)S(1)}, f32[32,1024]{1,0:T(8,128)}, u32[]{:S(2)}) copy-start(f32[32,1024]{1,0:T(8,128)} %constant.129.clone) | copy-start | bytes 393220
  57.6 132.9 %all-to-all-start = ((bf16[8,160,1024]{2,1,0:T(8,128)(2,1)}), bf16[8,160,1024]{2,1,0:T(8,128)(2,1)}, u32[]{:S(2)}, u32[]{:S(2)}) async-start(bf16[8,160,1024]{2,1,0:T(8,128)(2,1)} %bitcast.61), calls=%async_computation | async-start | bytes 5242880 | tf_op jit(solution)/shard_map/all_to_all | solution.py:1024
  63.5 93.0 %copy-start.13 = (bf16[1024,8]{0,1:T(8,128)(2,1)S(1)}, bf16[1024,8]{0,1:T(8,128)(2,1)}, u32[]{:S(2)}) copy-start(bf16[1024,8]{0,1:T(8,128)(2,1)} %param.18) | copy-start | bytes 49156
  63.5 52.9 %collective-permute-start = (bf16[3,1024,256]{2,1,0:T(8,128)(2,1)}, bf16[3,1024,256]{2,1,0:T(8,128)(2,1)S(1)}, u32[]{:S(2)}, u32[]{:S(2)}) collective-permute-start(bf16[3,1024,256]{2,1,0:T(8,128)(2,1)} %w_ref.3), channel_id=1, source_target_pairs={{0,1},{1,0},{2,3},{3,2},{4,5},{5,4},{6,7},{7,6},{8,9},{9,8},{10,11... | collective-permute-start | bytes 4718600 | tf_op jit(solution)/shard_map/ppermute | solution.py:951
  63.6 126.9 %collective-permute-start.6 = (bf16[2,704,1024]{2,1,0:T(8,128)(2,1)}, bf16[2,704,1024]{2,1,0:T(8,128)(2,1)}, u32[]{:S(2)}, u32[]{:S(2)}) collective-permute-start(bf16[2,704,1024]{2,1,0:T(8,128)(2,1)} %bitcast.7.refs_0_), channel_id=1, source_target_pairs={{0,1},{1,0},{2,3},{3,2},{4,5},{5,4},{6,7},{7,6},{8,9},{9,8},{10,11... | collective-permute-start | bytes 8650760 | tf_op jit(solution)/shard_map/ppermute | solution.py:951
  114.8 31.2 %collective-permute-start.10 = (bf16[704,1024]{1,0:T(8,128)(2,1)}, bf16[704,1024]{1,0:T(8,128)(2,1)}, u32[]{:S(2)}, u32[]{:S(2)}) collective-permute-start(bf16[704,1024]{1,0:T(8,128)(2,1)} %bitcast.8.refs_4_), channel_id=1, source_target_pairs={{0,2},{1,3},{2,0},{3,1},{4,6},{5,7},{6,4},{7,5},{8,10},{9,11},{10,... | collective-permute-start | bytes 4325384 | tf_op jit(solution)/shard_map/ppermute | solution.py:951
  115.9 74.7 %collective-permute-start.8 = (bf16[2,704,1024]{2,1,0:T(8,128)(2,1)}, bf16[2,704,1024]{2,1,0:T(8,128)(2,1)}, u32[]{:S(2)}, u32[]{:S(2)}) collective-permute-start(bf16[2,704,1024]{2,1,0:T(8,128)(2,1)} %collective-permute-done.7.refs_2_), channel_id=1, source_target_pairs={{0,1},{1,0},{2,3},{3,2},{4,5},{5,4},{6,7},{7,6},{8,9},{9,8},{10,11... | collective-permute-start | bytes 8650760 | tf_op jit(solution)/shard_map/ppermute | solution.py:951
  115.9 30.1 %collective-permute-start.2 = (bf16[3,1024,256]{2,1,0:T(8,128)(2,1)}, bf16[3,1024,256]{2,1,0:T(8,128)(2,1)S(1)}, u32[]{:S(2)}, u32[]{:S(2)}) collective-permute-start(bf16[3,1024,256]{2,1,0:T(8,128)(2,1)} %collective-permute-done.1.w_ref), channel_id=1, source_target_pairs={{0,1},{1,0},{2,3},{3,2},{4,5},{5,4},{6,7},{7,6},{8,9},{9,8},{10,11... | collective-permute-start | bytes 4718600 | tf_op jit(solution)/shard_map/ppermute | solution.py:951
  116.4 29.6 %copy-start.4 = (bf16[3,1024,256]{2,1,0:T(8,128)(2,1)}, bf16[3,1024,256]{2,1,0:T(8,128)(2,1)S(1)}, u32[]{:S(2)}) copy-start(bf16[3,1024,256]{2,1,0:T(8,128)(2,1)S(1)} %collective-permute-done.w_ref) | copy-start | bytes 4718596
  116.4 6.7 %collective-permute-start.3 = (bf16[1024,256]{1,0:T(8,128)(2,1)S(1)}, bf16[1024,256]{1,0:T(8,128)(2,1)S(1)}, u32[]{:S(2)}, u32[]{:S(2)}) collective-permute-start(bf16[1024,256]{1,0:T(8,128)(2,1)S(1)} %copy-done.5), channel_id=1, source_target_pairs={{0,1},{1,0},{2,3},{3,2},{4,5},{5,4},{6,7},{7,6},{8,9},{9,8},{10,11... | collective-permute-start | bytes 1572872 | tf_op jit(solution)/shard_map/ppermute | solution.py:951
  123.1 23.6 %copy-start.7 = (bf16[1024,256]{1,0:T(8,128)(2,1)}, bf16[1024,256]{1,0:T(8,128)(2,1)S(1)}, u32[]{:S(2)}) copy-start(bf16[1024,256]{1,0:T(8,128)(2,1)S(1)} %collective-permute-done.3.refs_5_) | copy-start | bytes 1572868
  123.1 67.4 %collective-permute-start.9 = (bf16[704,1024]{1,0:T(8,128)(2,1)}, bf16[704,1024]{1,0:T(8,128)(2,1)}, u32[]{:S(2)}, u32[]{:S(2)}) collective-permute-start(bf16[704,1024]{1,0:T(8,128)(2,1)} %bitcast.8.refs_4_), channel_id=1, source_target_pairs={{0,1},{1,0},{2,3},{3,2},{4,5},{5,4},{6,7},{7,6},{8,9},{9,8},{10,11... | collective-permute-start | bytes 4325384 | tf_op jit(solution)/shard_map/ppermute | solution.py:951
  146.0 44.5 %collective-permute-start.11 = (bf16[704,1024]{1,0:T(8,128)(2,1)}, bf16[704,1024]{1,0:T(8,128)(2,1)}, u32[]{:S(2)}, u32[]{:S(2)}) collective-permute-start(bf16[704,1024]{1,0:T(8,128)(2,1)} %collective-permute-done.10.refs_6_), channel_id=1, source_target_pairs={{0,1},{1,0},{2,3},{3,2},{4,5},{5,4},{6,7},{7,6},{8,9},{9,8},{10,11... | collective-permute-start | bytes 4325384 | tf_op jit(solution)/shard_map/ppermute | solution.py:951
  146.1 19.0 %copy-start.3 = (bf16[3,1024,256]{2,1,0:T(8,128)(2,1)}, bf16[3,1024,256]{2,1,0:T(8,128)(2,1)S(1)}, u32[]{:S(2)}) copy-start(bf16[3,1024,256]{2,1,0:T(8,128)(2,1)S(1)} %collective-permute-done.2.w_ref.refs_4_) | copy-start | bytes 4718596
  146.1 35.0 %collective-permute-start.5 = (bf16[1024,256]{1,0:T(8,128)(2,1)S(1)}, bf16[1024,256]{1,0:T(8,128)(2,1)S(1)}, u32[]{:S(2)}, u32[]{:S(2)}) collective-permute-start(bf16[1024,256]{1,0:T(8,128)(2,1)S(1)} %collective-permute-done.4.refs_6_), channel_id=1, source_target_pairs={{0,1},{1,0},{2,3},{3,2},{4,5},{5,4},{6,7},{7,6},{8,9},{9,8},{10,11... | collective-permute-start | bytes 1572872 | tf_op jit(solution)/shard_map/ppermute | solution.py:951
  334.8 154.0 %collective-permute-start.47 = (bf16[3,704,1024]{2,1,0:T(8,128)(2,1)}, bf16[3,704,1024]{2,1,0:T(8,128)(2,1)}, u32[]{:S(2)}, u32[]{:S(2)}) collective-permute-start(bf16[3,704,1024]{2,1,0:T(8,128)(2,1)} %get-tuple-element.122), channel_id=1, source_target_pairs={{0,1},{1,0},{2,3},{3,2},{4,5},{5,4},{6,7},{7,6},{8,9},{9,8},{10,11... | collective-permute-start | bytes 12976136 | tf_op jit(solution)/shard_map/ppermute | solution.py:951
  349.8 59.7 %collective-permute-start.38 = (bf16[1024,256]{1,0:T(8,128)(2,1)}, bf16[1024,256]{1,0:T(8,128)(2,1)S(1)}, u32[]{:S(2)}, u32[]{:S(2)}) collective-permute-start(bf16[1024,256]{1,0:T(8,128)(2,1)} %get-tuple-element.118), channel_id=1, source_target_pairs={{0,1},{1,0},{2,3},{3,2},{4,5},{5,4},{6,7},{7,6},{8,9},{9,8},{10,11... | collective-permute-start | bytes 1572872 | tf_op jit(solution)/shard_map/ppermute | solution.py:951
  350.3 69.5 %collective-permute-start.37 = (bf16[1024,256]{1,0:T(8,128)(2,1)}, bf16[1024,256]{1,0:T(8,128)(2,1)}, u32[]{:S(2)}, u32[]{:S(2)}) collective-permute-start(bf16[1024,256]{1,0:T(8,128)(2,1)} %get-tuple-element.116), channel_id=1, source_target_pairs={{0,1},{1,0},{2,3},{3,2},{4,5},{5,4},{6,7},{7,6},{8,9},{9,8},{10,11... | collective-permute-start | bytes 1572872 | tf_op jit(solution)/shard_map/ppermute | solution.py:951
  363.7 64.2 %collective-permute-start.23 = (bf16[3,1024,256]{2,1,0:T(8,128)(2,1)}, bf16[3,1024,256]{2,1,0:T(8,128)(2,1)S(1)}, u32[]{:S(2)}, u32[]{:S(2)}) collective-permute-start(bf16[3,1024,256]{2,1,0:T(8,128)(2,1)} %get-tuple-element.114), channel_id=1, source_target_pairs={{0,1},{1,0},{2,3},{3,2},{4,5},{5,4},{6,7},{7,6},{8,9},{9,8},{10,11... | collective-permute-start | bytes 4718600 | tf_op jit(solution)/shard_map/ppermute | solution.py:951
  394.2 14.5 %copy-start.17 = (f32[4,8,128]{2,1,0:T(8,128)S(1)}, f32[4,8,128]{2,1,0:T(8,128)}, u32[]{:S(2)}) copy-start(f32[4,8,128]{2,1,0:T(8,128)} %get-tuple-element.98) | copy-start | bytes 49156
  394.2 15.3 %copy-start.11 = (bf16[1024,256]{1,0:T(8,128)(2,1)S(1)}, bf16[1024,256]{1,0:T(8,128)(2,1)}, u32[]{:S(2)}) copy-start(bf16[1024,256]{1,0:T(8,128)(2,1)} %get-tuple-element.117) | copy-start | bytes 1572868
  410.4 14.3 %collective-permute-start.39 = (bf16[1024,256]{1,0:T(8,128)(2,1)}, bf16[1024,256]{1,0:T(8,128)(2,1)}, u32[]{:S(2)}, u32[]{:S(2)}) collective-permute-start(bf16[1024,256]{1,0:T(8,128)(2,1)} %add_convert_fusion.6), channel_id=1, source_target_pairs={{0,2},{1,3},{2,0},{3,1},{4,6},{5,7},{6,4},{7,5},{8,10},{9,11},{10,... | collective-permute-start | bytes 1572872 | tf_op jit(solution)/shard_map/ppermute | solution.py:951
  416.8 19.7 %copy-start.9 = (bf16[3,1024,256]{2,1,0:T(8,128)(2,1)S(1)}, bf16[3,1024,256]{2,1,0:T(8,128)(2,1)}, u32[]{:S(2)}) copy-start(bf16[3,1024,256]{2,1,0:T(8,128)(2,1)} %get-tuple-element.113) | copy-start | bytes 4718596
  417.7 1.2 collective-permute-start.12
  418.9 63.9 %collective-permute-start.22 = (bf16[3,1024,256]{2,1,0:T(8,128)(2,1)}, bf16[3,1024,256]{2,1,0:T(8,128)(2,1)}, u32[]{:S(2)}, u32[]{:S(2)}) collective-permute-start(bf16[3,1024,256]{2,1,0:T(8,128)(2,1)} %get-tuple-element.112), channel_id=1, source_target_pairs={{0,1},{1,0},{2,3},{3,2},{4,5},{5,4},{6,7},{7,6},{8,9},{9,8},{10,11... | collective-permute-start | bytes 4718600 | tf_op jit(solution)/shard_map/ppermute | solution.py:951
  419.7 18.9 %collective-permute-start.17 = (f32[72,128]{1,0:T(8,128)S(1)}, f32[72,128]{1,0:T(8,128)S(1)}, u32[]{:S(2)}, u32[]{:S(2)}) collective-permute-start(f32[72,128]{1,0:T(8,128)S(1)} %maximum_bitcast_fusion), channel_id=1, source_target_pairs={{0,1},{1,0},{2,3},{3,2},{4,5},{5,4},{6,7},{7,6},{8,9},{9,8},{10,11... | collective-permute-start | bytes 110600 | tf_op jit(solution)/shard_map/ppermute | solution.py:951
  424.7 13.4 %collective-permute-start.13 = (f32[12,128]{1,0:T(8,128)S(1)}, f32[12,128]{1,0:T(8,128)S(1)}, u32[]{:S(2)}, u32[]{:S(2)}) collective-permute-start(f32[12,128]{1,0:T(8,128)S(1)} %fusion.1), channel_id=1, source_target_pairs={{0,2},{1,3},{2,0},{3,1},{4,6},{5,7},{6,4},{7,5},{8,10},{9,11},{10,... | collective-permute-start | bytes 18440 | tf_op jit(solution)/shard_map/ppermute | solution.py:951
  427.8 10.8 %copy-start.15 = (f32[1,1024]{1,0:T(1,128)S(1)}, f32[1,1024]{1,0:T(1,128)}, u32[]{:S(2)}) copy-start(f32[1,1024]{1,0:T(1,128)} %get-tuple-element.107) | copy-start | bytes 12292
  427.9 14.1 %collective-permute-start.40 = (bf16[512,256]{1,0:T(8,128)(2,1)S(1)}, bf16[512,256]{1,0:T(8,128)(2,1)S(1)}, u32[]{:S(2)}, u32[]{:S(2)}) collective-permute-start(bf16[512,256]{1,0:T(8,128)(2,1)S(1)} %broadcast_select_fusion.2), channel_id=1, source_target_pairs={{0,4},{4,0},{8,12},{12,8},{16,20},{20,16},{24,28},{28,24},{1,5},{5... | collective-permute-start | bytes 786440 | tf_op jit(solution)/shard_map/ppermute | solution.py:951
  438.1 44.8 %collective-permute-start.24 = (bf16[3,1024,256]{2,1,0:T(8,128)(2,1)}, bf16[3,1024,256]{2,1,0:T(8,128)(2,1)}, u32[]{:S(2)}, u32[]{:S(2)}) collective-permute-start(bf16[3,1024,256]{2,1,0:T(8,128)(2,1)} %add_convert_fusion.3), channel_id=1, source_target_pairs={{0,2},{1,3},{2,0},{3,1},{4,6},{5,7},{6,4},{7,5},{8,10},{9,11},{10,... | collective-permute-start | bytes 4718600 | tf_op jit(solution)/shard_map/ppermute | solution.py:951
  438.6 35.5 %collective-permute-start.14 = (f32[12,128]{1,0:T(8,128)S(1)}, f32[12,128]{1,0:T(8,128)S(1)}, u32[]{:S(2)}, u32[]{:S(2)}) collective-permute-start(f32[12,128]{1,0:T(8,128)S(1)} %fusion.8), channel_id=1, source_target_pairs={{0,4},{4,0},{8,12},{12,8},{16,20},{20,16},{24,28},{28,24},{1,5},{5... | collective-permute-start | bytes 18440 | tf_op jit(solution)/shard_map/ppermute | solution.py:951
  442.0 32.1 %collective-permute-start.18 = (f32[72,128]{1,0:T(8,128)S(1)}, f32[72,128]{1,0:T(8,128)S(1)}, u32[]{:S(2)}, u32[]{:S(2)}) collective-permute-start(f32[72,128]{1,0:T(8,128)S(1)} %fusion.2), channel_id=1, source_target_pairs={{0,2},{1,3},{2,0},{3,1},{4,6},{5,7},{6,4},{7,5},{8,10},{9,11},{10,... | collective-permute-start | bytes 110600 | tf_op jit(solution)/shard_map/ppermute | solution.py:951
  474.1 6.6 %collective-permute-start.41 = (bf16[256,256]{1,0:T(8,128)(2,1)S(1)}, bf16[256,256]{1,0:T(8,128)(2,1)S(1)}, u32[]{:S(2)}, u32[]{:S(2)}) collective-permute-start(bf16[256,256]{1,0:T(8,128)(2,1)S(1)} %broadcast_select_fusion.5), channel_id=1, source_target_pairs={{0,8},{4,12},{8,0},{12,4},{16,24},{20,28},{24,16},{28,20},{1,9},{5... | collective-permute-start | bytes 393224 | tf_op jit(solution)/shard_map/ppermute | solution.py:951
  474.1 6.4 %collective-permute-start.19 = (f32[72,128]{1,0:T(8,128)S(1)}, f32[72,128]{1,0:T(8,128)S(1)}, u32[]{:S(2)}, u32[]{:S(2)}) collective-permute-start(f32[72,128]{1,0:T(8,128)S(1)} %fusion.9), channel_id=1, source_target_pairs={{0,4},{4,0},{8,12},{12,8},{16,20},{20,16},{24,28},{28,24},{1,5},{5... | collective-permute-start | bytes 110600 | tf_op jit(solution)/shard_map/ppermute | solution.py:951
  474.6 141.8 %all-to-all-start.1 = ((bf16[8,160,1024]{2,1,0:T(8,128)(2,1)}), bf16[8,160,1024]{2,1,0:T(8,128)(2,1)S(1)}, u32[]{:S(2)}, u32[]{:S(2)}) async-start(bf16[8,160,1024]{2,1,0:T(8,128)(2,1)} %get-tuple-element.106), calls=%async_computation.1 | async-start | bytes 5242880 | tf_op jit(solution)/shard_map/all_to_all | solution.py:1024
  480.5 143.9 %collective-permute-start.46 = (bf16[3,704,1024]{2,1,0:T(8,128)(2,1)}, bf16[3,704,1024]{2,1,0:T(8,128)(2,1)}, u32[]{:S(2)}, u32[]{:S(2)}) collective-permute-start(bf16[3,704,1024]{2,1,0:T(8,128)(2,1)} %get-tuple-element.120), channel_id=1, source_target_pairs={{0,1},{1,0},{2,3},{3,2},{4,5},{5,4},{6,7},{7,6},{8,9},{9,8},{10,11... | collective-permute-start | bytes 12976136 | tf_op jit(solution)/shard_map/ppermute | solution.py:951
  480.6 40.7 %collective-permute-start.15 = (f32[12,128]{1,0:T(8,128)S(1)}, f32[12,128]{1,0:T(8,128)S(1)}, u32[]{:S(2)}, u32[]{:S(2)}) collective-permute-start(f32[12,128]{1,0:T(8,128)S(1)} %add.130), channel_id=1, source_target_pairs={{0,8},{4,12},{8,0},{12,4},{16,24},{20,28},{24,16},{28,20},{1,9},{5... | collective-permute-start | bytes 18440 | tf_op jit(solution)/shard_map/ppermute | solution.py:951
  482.8 57.6 %collective-permute-start.20 = (f32[72,128]{1,0:T(8,128)S(1)}, f32[72,128]{1,0:T(8,128)S(1)}, u32[]{:S(2)}, u32[]{:S(2)}) collective-permute-start(f32[72,128]{1,0:T(8,128)S(1)} %add.135), channel_id=1, source_target_pairs={{0,8},{4,12},{8,0},{12,4},{16,24},{20,28},{24,16},{28,20},{1,9},{5... | collective-permute-start | bytes 110600 | tf_op jit(solution)/shard_map/ppermute | solution.py:951
  482.9 57.4 %collective-permute-start.42 = (bf16[128,256]{1,0:T(8,128)(2,1)S(1)}, bf16[128,256]{1,0:T(8,128)(2,1)S(1)}, u32[]{:S(2)}, u32[]{:S(2)}) collective-permute-start(bf16[128,256]{1,0:T(8,128)(2,1)S(1)} %broadcast_select_fusion.8), channel_id=1, source_target_pairs={{0,16},{4,20},{8,24},{12,28},{16,0},{20,4},{24,8},{28,12},{1,17},{... | collective-permute-start | bytes 196616 | tf_op jit(solution)/shard_map/ppermute | solution.py:951
  496.7 127.7 %collective-permute-start.48 = (bf16[3,704,1024]{2,1,0:T(8,128)(2,1)}, bf16[3,704,1024]{2,1,0:T(8,128)(2,1)}, u32[]{:S(2)}, u32[]{:S(2)}) collective-permute-start(bf16[3,704,1024]{2,1,0:T(8,128)(2,1)} %add_convert_fusion), channel_id=1, source_target_pairs={{0,2},{1,3},{2,0},{3,1},{4,6},{5,7},{6,4},{7,5},{8,10},{9,11},{10,... | collective-permute-start | bytes 12976136 | tf_op jit(solution)/shard_map/ppermute | solution.py:951
  521.4 30.0 %collective-permute-start.25 = (bf16[768,256]{1,0:T(8,128)(2,1)S(1)}, bf16[768,256]{1,0:T(8,128)(2,1)S(1)}, u32[]{:S(2)}, u32[]{:S(2)}) collective-permute-start(bf16[768,256]{1,0:T(8,128)(2,1)S(1)} %get-tuple-element.134), channel_id=1, source_target_pairs={{0,4},{4,0},{8,12},{12,8},{16,20},{20,16},{24,28},{28,24},{1,5},{5... | collective-permute-start | bytes 1179656 | tf_op jit(solution)/shard_map/ppermute | solution.py:951
  540.3 11.8 %collective-permute-start.31 = (bf16[768,256]{1,0:T(8,128)(2,1)S(1)}, bf16[768,256]{1,0:T(8,128)(2,1)S(1)}, u32[]{:S(2)}, u32[]{:S(2)}) collective-permute-start(bf16[768,256]{1,0:T(8,128)(2,1)S(1)} %get-tuple-element.135), channel_id=1, source_target_pairs={{0,8},{4,12},{8,0},{12,4},{16,24},{20,28},{24,16},{28,20},{1,9},{5... | collective-permute-start | bytes 1179656 | tf_op jit(solution)/shard_map/ppermute | solution.py:951
  540.4 7.5 %collective-permute-start.43 = (bf16[128,256]{1,0:T(8,128)(2,1)S(1)}, bf16[128,256]{1,0:T(8,128)(2,1)S(1)}, u32[]{:S(2)}, u32[]{:S(2)}) collective-permute-start(bf16[128,256]{1,0:T(8,128)(2,1)S(1)} %add_convert_fusion.16), channel_id=1, source_target_pairs={{0,16},{4,20},{8,24},{12,28},{16,0},{20,4},{24,8},{28,12},{1,17},{... | collective-permute-start | bytes 196616 | tf_op jit(solution)/shard_map/ppermute | solution.py:951
  547.9 48.8 %collective-permute-start.16 = (f32[12,128]{1,0:T(8,128)S(1)}, f32[12,128]{1,0:T(8,128)S(1)}, u32[]{:S(2)}, u32[]{:S(2)}) collective-permute-start(f32[12,128]{1,0:T(8,128)S(1)} %add.131), channel_id=1, source_target_pairs={{0,16},{4,20},{8,24},{12,28},{16,0},{20,4},{24,8},{28,12},{1,17},{... | collective-permute-start | bytes 18440 | tf_op jit(solution)/shard_map/ppermute | solution.py:951
  551.4 42.2 %collective-permute-start.44 = (bf16[256,256]{1,0:T(8,128)(2,1)S(1)}, bf16[256,256]{1,0:T(8,128)(2,1)S(1)}, u32[]{:S(2)}, u32[]{:S(2)}) collective-permute-start(bf16[256,256]{1,0:T(8,128)(2,1)S(1)} %maximum_select_fusion.8), channel_id=1, source_target_pairs={{0,8},{4,12},{8,0},{12,4},{16,24},{20,28},{24,16},{28,20},{1,9},{5... | collective-permute-start | bytes 393224 | tf_op jit(solution)/shard_map/ppermute | solution.py:951
  552.5 6.6 %collective-permute-start.26 = (bf16[384,256]{1,0:T(8,128)(2,1)S(1)}, bf16[384,256]{1,0:T(8,128)(2,1)S(1)}, u32[]{:S(2)}, u32[]{:S(2)}) collective-permute-start(bf16[384,256]{1,0:T(8,128)(2,1)S(1)} %broadcast_select_fusion.4), channel_id=1, source_target_pairs={{0,8},{4,12},{8,0},{12,4},{16,24},{20,28},{24,16},{28,20},{1,9},{5... | collective-permute-start | bytes 589832 | tf_op jit(solution)/shard_map/ppermute | solution.py:951
  559.1 6.7 %collective-permute-start.32 = (bf16[384,256]{1,0:T(8,128)(2,1)S(1)}, bf16[384,256]{1,0:T(8,128)(2,1)S(1)}, u32[]{:S(2)}, u32[]{:S(2)}) collective-permute-start(bf16[384,256]{1,0:T(8,128)(2,1)S(1)} %broadcast_select_fusion.3), channel_id=1, source_target_pairs={{0,4},{4,0},{8,12},{12,8},{16,20},{20,16},{24,28},{28,24},{1,5},{5... | collective-permute-start | bytes 589832 | tf_op jit(solution)/shard_map/ppermute | solution.py:951
  565.8 6.6 %collective-permute-start.27 = (bf16[192,256]{1,0:T(8,128)(2,1)S(1)}, bf16[192,256]{1,0:T(8,128)(2,1)S(1)}, u32[]{:S(2)}, u32[]{:S(2)}) collective-permute-start(bf16[192,256]{1,0:T(8,128)(2,1)S(1)} %broadcast_select_fusion.7), channel_id=1, source_target_pairs={{0,16},{4,20},{8,24},{12,28},{16,0},{20,4},{24,8},{28,12},{1,17},{... | collective-permute-start | bytes 294920 | tf_op jit(solution)/shard_map/ppermute | solution.py:951
  572.4 5.5 collective-permute-start.33
  577.9 5.5 collective-permute-start.28
  583.4 5.6 collective-permute-start.34
  589.0 10.0 %collective-permute-start.29 = (bf16[384,256]{1,0:T(8,128)(2,1)S(1)}, bf16[384,256]{1,0:T(8,128)(2,1)S(1)}, u32[]{:S(2)}, u32[]{:S(2)}) collective-permute-start(bf16[384,256]{1,0:T(8,128)(2,1)S(1)} %maximum_select_fusion.6), channel_id=1, source_target_pairs={{0,8},{4,12},{8,0},{12,4},{16,24},{20,28},{24,16},{28,20},{1,9},{5... | collective-permute-start | bytes 589832 | tf_op jit(solution)/shard_map/ppermute | solution.py:951
  593.5 9.3 %copy-start.10 = (bf16[384,256]{1,0:T(8,128)(2,1)}, bf16[384,256]{1,0:T(8,128)(2,1)S(1)}, u32[]{:S(2)}) copy-start(bf16[384,256]{1,0:T(8,128)(2,1)S(1)} %maximum_select_fusion.7) | copy-start | bytes 589828
  593.5 9.3 %collective-permute-start.35 = (bf16[384,256]{1,0:T(8,128)(2,1)S(1)}, bf16[384,256]{1,0:T(8,128)(2,1)}, u32[]{:S(2)}, u32[]{:S(2)}) collective-permute-start(bf16[384,256]{1,0:T(8,128)(2,1)S(1)} %maximum_select_fusion.7), channel_id=1, source_target_pairs={{0,4},{4,0},{8,12},{12,8},{16,20},{20,16},{24,28},{28,24},{1,5},{5... | collective-permute-start | bytes 589832 | tf_op jit(solution)/shard_map/ppermute | solution.py:951
  596.6 5.0 collective-permute-start.21
  599.0 8.4 %collective-permute-start.45 = (bf16[512,256]{1,0:T(8,128)(2,1)}, bf16[512,256]{1,0:T(8,128)(2,1)}, u32[]{:S(2)}, u32[]{:S(2)}) collective-permute-start(bf16[512,256]{1,0:T(8,128)(2,1)} %maximum_select_fusion.5), channel_id=1, source_target_pairs={{0,4},{4,0},{8,12},{12,8},{16,20},{20,16},{24,28},{28,24},{1,5},{5... | collective-permute-start | bytes 786440 | tf_op jit(solution)/shard_map/ppermute | solution.py:951
  601.7 9.9 %collective-permute-start.30 = (bf16[768,256]{1,0:T(8,128)(2,1)S(1)}, bf16[768,256]{1,0:T(8,128)(2,1)}, u32[]{:S(2)}, u32[]{:S(2)}) collective-permute-start(bf16[768,256]{1,0:T(8,128)(2,1)S(1)} %maximum_select_fusion.3), channel_id=1, source_target_pairs={{0,4},{4,0},{8,12},{12,8},{16,20},{20,16},{24,28},{28,24},{1,5},{5... | collective-permute-start | bytes 1179656 | tf_op jit(solution)/shard_map/ppermute | solution.py:951
  604.1 8.8 %collective-permute-start.36 = (bf16[768,256]{1,0:T(8,128)(2,1)S(1)}, bf16[768,256]{1,0:T(8,128)(2,1)}, u32[]{:S(2)}, u32[]{:S(2)}) collective-permute-start(bf16[768,256]{1,0:T(8,128)(2,1)S(1)} %maximum_select_fusion.4), channel_id=1, source_target_pairs={{0,8},{4,12},{8,0},{12,4},{16,24},{20,28},{24,16},{28,20},{1,9},{5... | collective-permute-start | bytes 1179656 | tf_op jit(solution)/shard_map/ppermute | solution.py:951
  (5 other events, 18.7 us)

commit v3 on v2

v3 whole, which is shorter than its diff:
```python
import functools

import jax
import jax.numpy as jnp
import numpy as np
from jax import lax
from jax.experimental import pallas as pl
from jax.experimental.pallas import tpu as pltpu
from jax.sharding import PartitionSpec as P

PIC = 256
PRECISE = lax.Precision.HIGHEST
EPSILON = 1e-06
MASKED_SCORE = -1e30
BUCKET_EDGES = (8, 11, 16, 23, 32, 45, 64, 91)
TILE = 128
F32 = jnp.float32
BF16 = jnp.bfloat16
I32 = jnp.int32
VMEM = pl.BlockSpec(memory_space=pltpu.VMEM)
SMEM = pl.BlockSpec(memory_space=pltpu.SMEM)
ANY = pl.BlockSpec(memory_space=pl.ANY)
LIGHT = 1024
EXTRA = 8


def dot_nn(a, b):
    return lax.dot_general(a, b, (((1,), (0,)), ((), ())), preferred_element_type=F32)


def dot_nt(a, b):
    return lax.dot_general(a, b, (((1,), (1,)), ((), ())), preferred_element_type=F32)


def dot_tn(a, b):
    return lax.dot_general(a, b, (((0,), (0,)), ((), ())), preferred_element_type=F32)


def iota(shape, axis):
    return lax.broadcasted_iota(I32, shape, axis)


def shape_of(shape, dtype):
    return jax.ShapeDtypeStruct(shape, dtype)


def call(body, out, args, specs, scratch=(), name=None):
    return pl.pallas_call(
        body,
        out_shape=out,
        in_specs=specs,
        out_specs=jax.tree.map(lambda _: VMEM, out),
        scratch_shapes=list(scratch),
        cost_estimate=pl.CostEstimate(flops=LIGHT, bytes_accessed=LIGHT, transcendentals=0),
        name=name,
    )(*args)


def bucket_of(offset):
    magnitude = np.abs(offset)
    coarse = 7 + sum((magnitude >= bound).astype(np.int32) for bound in BUCKET_EDGES)
    return np.where(magnitude < 8, magnitude, coarse) + 16 * (offset < 0)


def diagonal_ones(bucket_count):
    column = np.arange(2 * TILE)
    signed = np.where(column < TILE, column, column - 2 * TILE)
    offsets = np.concatenate([TILE * step - signed for step in (-1, 0, 1)])
    used = np.tile(column != TILE, 3)
    hit = bucket_of(offsets)[None, :] == np.arange(bucket_count)[:, None]
    near = (hit & used[None, :]).astype(np.float32)
    far = np.zeros((bucket_count, 2 * TILE), np.float32)
    far[bucket_of(np.array(TILE)), :TILE] = 1
    far[bucket_of(np.array(-TILE)), TILE:] = 1
    return np.concatenate([near, far], 1)


def onehot_rows(first, count, slots_row):
    index = iota((count, slots_row.shape[1]), 0) + first
    hit = (index == slots_row[0:1, :]) | (index == slots_row[1:2, :])
    return hit.astype(F32).astype(BF16)


def onehot_columns(slots_column, first, count):
    index = iota((slots_column.shape[0], count), 1) + first
    return index == slots_column


def route_slots(experts, capacity, routes):
    tokens = routes.shape[1]
    label = iota((experts, tokens), 0)
    hits = ((routes[0:1] == label) | (routes[1:2] == label)).astype(F32).astype(BF16)
    earlier = iota((tokens, tokens), 0) < iota((tokens, tokens), 1)
    before = dot_nn(hits, earlier.astype(F32).astype(BF16))
    slots = []
    for k in range(2):
        own = jnp.sum(jnp.where(routes[k : k + 1] == label, before, 0.0), 0, keepdims=True)
        slots.append(own.astype(I32) + routes[k : k + 1] * capacity)
    return jnp.concatenate(slots * 4, 0)


def unit_norm(values):
    recip = lax.rsqrt(jnp.mean(values * values, -1, keepdims=True) + EPSILON)
    return values * recip, recip


def fill_mask(mask_ref, span_start):
    size = mask_ref.shape[0]
    i, j = iota((size, size), 0), iota((size, size), 1)

    def inside(p):
        return (p >= span_start) & (p < span_start + PIC)

    visible = (j <= i) | (inside(i) & inside(j))
    mask_ref[...] = jnp.where(visible, 0.0, MASKED_SCORE)


def head_lanes(which, size):
    lane = iota((1, 2 * size), 1)
    return ((lane >= size) == (which == 1)).astype(F32).astype(BF16)


def bias_tiles(diag_row):
    tiles = []
    for step in range(3):
        row = diag_row[:, 2 * TILE * step : 2 * TILE * (step + 1)]
        wide = jnp.broadcast_to(row, (TILE, 2 * TILE))
        tiles.append(pltpu.roll(wide, 0, 1, stride=1, stride_axis=0)[:, :TILE])
    return tiles, (diag_row[:, 6 * TILE : 7 * TILE], diag_row[:, 7 * TILE :])


def score_tiles(block, query, keys, tiles, far, mask_ref):
    raw = dot_nt(query, keys)
    rows = slice(block * TILE, (block + 1) * TILE)
    result = []
    for other in range(keys.shape[0] // TILE):
        piece = raw[:, other * TILE : (other + 1) * TILE]
        step = block - other
        piece = piece + (far[0] if step >= 2 else far[1] if step <= -2 else tiles[step + 1])
        if step <= 0:
            piece = piece + mask_ref[rows, other * TILE : (other + 1) * TILE]
        result.append(piece)
    return result


def softmax_tiles(pieces):
    top = functools.reduce(jnp.maximum, pieces)
    top = jnp.max(top, -1, keepdims=True)
    powers = [jnp.exp(piece - top) for piece in pieces]
    total = jnp.sum(functools.reduce(jnp.add, powers), -1, keepdims=True)
    scale = 1.0 / total
    return [power * scale for power in powers]


def split_three(value):
    high = value.astype(BF16).astype(F32)
    middle = (value - high).astype(BF16).astype(F32)
    return high, middle, value - high - middle


def remote_copy(source, target, sent, got, axis, peer):
    return pltpu.make_async_remote_copy(
        src_ref=source,
        dst_ref=target,
        send_sem=sent,
        recv_sem=got,
        device_id={axis: peer},
        device_id_type=pl.DeviceIdType.MESH,
    )


def greet(peers):
    barrier = pltpu.get_barrier_semaphore()
    for axis, peer in peers:
        pl.semaphore_signal(
            barrier, inc=1, device_id={axis: peer}, device_id_type=pl.DeviceIdType.MESH
        )
    pl.semaphore_wait(barrier, len(peers))


def project_and_attend(place, group, groups, head_size, norm, diag_ref, w_ref, qkv_ref, mix_ref, mask):
    count = norm.shape[0]
    cols = w_ref.shape[-1]
    width = 2 * head_size
    owner = flip(place, group, groups)
    for c in range(3):
        qkv_ref[group, c] = dot_nn(norm[...], w_ref[group, c]).astype(BF16)

    def pair(p, carry):
        offset = pl.multiple_of(p * width, width)
        lanes = pl.ds(offset, width)
        query, keys, value = (qkv_ref[group, c, :, lanes] for c in range(3))
        mixed = [None] * (count // TILE)
        for which in range(2):
            head = owner * (cols // head_size) + 2 * p + which
            own = head_lanes(which, head_size)
            own_query, own_value = query * (own * 0.125), value * own
            tiles, far = bias_tiles(diag_ref[pl.ds(head, 1), :])
            for block in range(count // TILE):
                rows = slice(block * TILE, (block + 1) * TILE)
                pieces = score_tiles(block, own_query[rows], keys, tiles, far, mask)
                probs = jnp.concatenate([t.astype(BF16) for t in softmax_tiles(pieces)], 1)
                part = dot_nn(probs, own_value)
                mixed[block] = part if which == 0 else mixed[block] + part
        target = pl.ds(pl.multiple_of(owner * cols + offset, width), width)
        for block in range(count // TILE):
            rows = slice(block * TILE, (block + 1) * TILE)
            mix_ref[rows, target] = mixed[block].astype(BF16)
        return carry

    lax.fori_loop(0, cols // width, pair, 0)


def front_body(
    size, groups, head_size, span_ref, routes_ref, gain_ref, diag_ref, router_ref, tok_hbm, cot_hbm,
    qkv_shard, out_shard, in_shard, down_shard,
    col_ref, gate_ref, sent_gate_ref, qkvw_out, outw_out, qkv_out, mixed_out, hidden_out, norm_out,
    sent_out, outer_out, in_out, down_out,
    tok, cot, qkvw, outw, qkv, mixed, hidden, norm, sent, outer, mask, row, load_sems, save_sems,
    shard_sems, outer_send, outer_got,
):
    me, place = lax.axis_index("dp"), lax.axis_index("wshard")
    near, far = flip(place, 1, groups), flip(place, 2, groups)
    peers = [("dp", flip(me, step, size)) for step in range(1, size)]
    greet(peers + [("wshard", near), ("wshard", far)])

    sources = (qkv_shard, out_shard, in_shard, down_shard)

    def held(item, group):
        if item == 0:
            return qkvw.at[group]
        if item == 1:
            return outw.at[group]
        return (in_out if item == 2 else down_out).at[group - 1]

    def shard_copy(kind, item):
        source = held(item, 2) if kind == 2 else sources[item]
        return remote_copy(
            source, held(item, (1, 2, 3)[kind]), shard_sems.at[kind, item, 0],
            shard_sems.at[kind, item, 1], "wshard", far if kind == 1 else near,
        )

    for item in range(2):
        shard_copy(1, item).start()
        shard_copy(0, item).start()
    loads = [
        pltpu.make_async_copy(source, target, load_sems.at[i])
        for i, (source, target) in enumerate(
            ((cot_hbm, cot), (tok_hbm, tok), (qkv_shard, qkvw.at[0]), (out_shard, outw.at[0]))
        )
    ]
    for copy in loads:
        copy.start()
    for item in range(2, 4):
        shard_copy(1, item).start()
        shard_copy(0, item).start()

    experts, capacity = size, sent.shape[1]
    count = tok.shape[0]
    slots = route_slots(experts, capacity, routes_ref[...])
    row[...] = slots
    col_ref[...] = slots.astype(F32).T.astype(I32)
    loads[0].wait()

    def place_outer(expert, carry):
        outer[expert] = dot_nn(onehot_rows(expert * capacity, capacity, row[...]), cot[...]).astype(BF16)
        return carry

    lax.fori_loop(0, experts, place_outer, 0)
    fill_mask(mask, span_ref[0])
    loads[1].wait()
    unit, _ = unit_norm(tok[...].astype(F32))
    norm[...] = (unit * gain_ref[0:1, :]).astype(BF16)
    loads[2].wait()

    def outer_copy(source, target, peer):
        return remote_copy(
            outer.at[source], outer_out.at[target], outer_send.at[source], outer_got.at[target],
            "dp", peer,
        )

    own_outer = pltpu.make_async_copy(outer.at[me], outer_out.at[me], load_sems.at[4])
    own_outer.start()
    for _, peer in peers:
        outer_copy(peer, me, peer).start()

    def one_group(group, carry):
        @pl.when(group == 1)
        def _():
            shard_copy(0, 0).wait_recv()

        @pl.when(group == 2)
        def _():
            shard_copy(1, 0).wait_recv()
            shard_copy(2, 0).start()

        @pl.when(group == 3)
        def _():
            shard_copy(2, 0).wait_recv()

        project_and_attend(
            place, group, groups, head_size, norm, diag_ref, qkvw, qkv, mixed, mask
        )
        return carry

    lax.fori_loop(0, groups, one_group, 0)
    saves = [
        pltpu.make_async_copy(source, target, save_sems.at[i])
        for i, (source, target) in enumerate(
            (
                (qkvw, qkvw_out), (qkv, qkv_out), (mixed, mixed_out), (outw, outw_out),
                (hidden, hidden_out), (norm, norm_out), (sent, sent_out),
            )
        )
    ]
    for copy in saves[:3]:
        copy.start()
    loads[3].wait()
    shard_copy(0, 1).wait_recv()
    shard_copy(1, 1).wait_recv()
    shard_copy(2, 1).start()

    shard_copy(2, 1).wait_recv()
    saves[3].start()
    for group in range(groups):
        cols = outw.shape[2]
        lanes = pl.ds(pl.multiple_of(flip(place, group, groups) * cols, cols), cols)
        hidden[:, lanes] = tok[:, lanes].astype(F32) + dot_nn(mixed[...], outw[group])
    saves[4].start()
    unit, _ = unit_norm(hidden[...])
    norm[...] = (unit * gain_ref[1:2, :]).astype(BF16)
    saves[5].start()

    def place_sent(expert, carry):
        sent[expert] = dot_nn(onehot_rows(expert * capacity, capacity, row[...]), norm[...]).astype(BF16)
        return carry

    lax.fori_loop(0, experts, place_sent, 0)
    saves[6].start()
    logits = dot_nt(norm[...], router_ref[...])
    slots = [col_ref[:, k : k + 1] for k in range(2)]
    lane = iota(logits.shape, 1)
    chosen = []
    for k in range(2):
        own = (lane * capacity <= slots[k]) & (slots[k] < (lane + 1) * capacity)
        chosen.append(jnp.sum(jnp.where(own, logits, 0.0), -1, keepdims=True))
    top = jnp.maximum(chosen[0], chosen[1])
    powers = [jnp.exp(c - top) for c in chosen]
    gates = [power / (powers[0] + powers[1]) for power in powers]
    for k in range(2):
        gate_ref[:, k : k + 1] = gates[k]
    lane = iota((count, sent_gate_ref.shape[2]), 1)
    for expert in range(experts):
        label = jnp.where(lane < capacity, lane + expert * capacity, -1)
        part = 0.0
        for k in range(2):
            part = part + jnp.where(label == slots[k], gates[k], 0.0)
        line = jnp.sum(part, 0, keepdims=True)
        sent_gate_ref[expert] = jnp.broadcast_to(line, sent_gate_ref.shape[1:])

    for item in range(2, 4):
        shard_copy(1, item).wait_recv()
        shard_copy(2, item).start()
    own_outer.wait()
    for copy in saves:
        copy.wait()
    for _, peer in peers:
        outer_copy(peer, me, peer).wait_send()
        outer_copy(me, peer, peer).wait_recv()
    for item in range(4):
        for kind in range(3):
            shard_copy(kind, item).wait_send()
    for item in range(2, 4):
        shard_copy(0, item).wait_recv()
        shard_copy(2, item).wait_recv()


def front(span, routes, gains, diag, router_t, tokens, cotangent, shards, head_size, capacity):
    count, width = tokens.shape
    size, groups = lax.axis_size("dp"), lax.axis_size("wshard")
    qkv_shard, out_shard, in_shard, down_shard = shards
    cols = out_shard.shape[1]
    lanes = -(-capacity // TILE) * TILE
    dma = pltpu.SemaphoreType.DMA
    block = (size, capacity, width)
    return pl.pallas_call(
        functools.partial(front_body, size, groups, head_size),
        out_shape=(
            shape_of((count, 8), I32),
            shape_of((count, 2), F32),
            shape_of((size, EXTRA, lanes), F32),
            shape_of((groups, *qkv_shard.shape), BF16),
            shape_of((groups, *out_shard.shape), BF16),
            shape_of((groups, 3, count, cols), BF16),
            shape_of((count, width), BF16),
            shape_of((count, width), F32),
            shape_of((count, width), BF16),
            shape_of(block, BF16),
            shape_of(block, BF16),
            shape_of((groups - 1, *in_shard.shape), BF16),
            shape_of((groups - 1, *down_shard.shape), BF16),
        ),
        in_specs=[SMEM] + [VMEM] * 4 + [ANY] * 6,
        out_specs=(VMEM,) * 3 + (ANY,) * 10,
        scratch_shapes=[
            pltpu.VMEM((count, width), BF16),
            pltpu.VMEM((count, width), BF16),
            pltpu.VMEM((groups, *qkv_shard.shape), BF16),
            pltpu.VMEM((groups, *out_shard.shape), BF16),
            pltpu.VMEM((groups, 3, count, cols), BF16),
            pltpu.VMEM((count, width), BF16),
            pltpu.VMEM((count, width), F32),
            pltpu.VMEM((count, width), BF16),
            pltpu.VMEM(block, BF16),
            pltpu.VMEM(block, BF16),
            pltpu.VMEM((count, count), F32),
            pltpu.VMEM((8, count), I32),
            dma((5,)),
            dma((7,)),
            dma((3, 4, 2)),
            dma((size,)),
            dma((size,)),
        ],
        cost_estimate=pl.CostEstimate(flops=LIGHT, bytes_accessed=LIGHT, transcendentals=0),
        compiler_params=pltpu.CompilerParams(
            collective_id=1, has_side_effects=True, vmem_limit_bytes=60_000_000
        ),
        name="front",
    )(span, routes.T, gains, diag, router_t, tokens, cotangent, *shards)


def flip(value, change, size):
    result = 0
    bit = 1
    while bit < size:
        one, two = lax.rem(lax.div(value, bit), 2), lax.rem(lax.div(change, bit), 2)
        result = result + bit * (one + two - 2 * one * two)
        bit *= 2
    return result


def column_of(row, size):
    spot = iota((size, row.shape[1]), 0) == iota((size, row.shape[1]), 1)
    return jnp.sum(jnp.where(spot, row, 0.0), 1, keepdims=True)


def row_of(column, lanes):
    spot = iota((column.shape[0], lanes), 0) == iota((column.shape[0], lanes), 1)
    return jnp.sum(jnp.where(spot, column, 0.0), 0, keepdims=True)


def moe_body(
    size, groups, chunk, sent_ref, gates_ref, outer_ref, own_in, own_down, other_in, other_down, *refs
):
    in_refs = [own_in] + [other_in.at[g] for g in range(groups - 1)]
    down_refs = [own_down] + [other_down.at[g] for g in range(groups - 1)]
    back_out, extra_out, made_out, grad_out, moved_out = refs[:5]
    (
        buf, rows, gates, outer, low_outer, made_sum, back_sum, act, low, stage, extra_stage,
        made, grad_stage, weight_sems, send_sems, recv_sems, give_sems, take_sems, own_sems,
        save_sems, grad_sems, moved_sem,
    ) = refs[5:]
    share = down_refs[0].shape[0]
    part_size = share * groups // 2
    capacity, width = outer.shape[1:]
    both = 2 * capacity
    me = lax.axis_index("dp")
    pairs = size // 2
    my_pair = lax.div(me, 2)
    mesh_id = pl.DeviceIdType.MESH

    place = lax.axis_index("wshard")
    near = flip(place, 1, groups)
    greet([("dp", flip(me, step, size)) for step in range(1, size)] + [("wshard", near)])

    def remote(source, target, sent, got, peer):
        return pltpu.make_async_remote_copy(
            src_ref=source, dst_ref=target, send_sem=sent, recv_sem=got,
            device_id={"dp": peer}, device_id_type=mesh_id,
        )

    def forth(source, target, peer):
        return (
            remote(sent_ref.at[source], rows.at[target], send_sems.at[source, 0],
                   recv_sems.at[target, 0], peer),
            remote(gates_ref.at[source], gates.at[target], send_sems.at[source, 1],
                   recv_sems.at[target, 1], peer),
        )

    def back_copies(source, target, peer):
        return (
            remote(stage.at[source], back_out.at[target], give_sems.at[source, 0],
                   take_sems.at[target, 0], peer),
            remote(extra_stage.at[source], extra_out.at[target], give_sems.at[source, 1],
                   take_sems.at[target, 1], peer),
        )

    own = (
        pltpu.make_async_copy(sent_ref.at[me], rows.at[me], own_sems.at[0]),
        pltpu.make_async_copy(gates_ref.at[me], gates.at[me], own_sems.at[1]),
        pltpu.make_async_copy(outer_ref, outer, own_sems.at[2]),
    )
    own_back = (
        pltpu.make_async_copy(stage.at[me], back_out.at[me], own_sems.at[3]),
        pltpu.make_async_copy(extra_stage.at[me], extra_out.at[me], own_sems.at[4]),
    )
    for copy in own:
        copy.start()
    for step in range(1, size):
        peer = flip(me, step, size)
        for copy in forth(peer, me, peer):
            copy.start()

    def weight_copies(group):
        spot = pl.ds(group * share, share)
        return (
            pltpu.make_async_copy(in_refs[group], buf.at[0:2, spot], weight_sems.at[group, 0]),
            pltpu.make_async_copy(down_refs[group], buf.at[2, spot], weight_sems.at[group, 1]),
        )

    for group in range(groups):
        for copy in weight_copies(group):
            copy.start()
    for copy in own:
        copy.wait()

    def hidden_part(pair, base):
        spot = pl.ds(pl.multiple_of(pair * both, both), both)
        two = pl.ds(2 * pair, 2)
        these = rows[two].reshape(both, width)
        outers = low_outer[spot, :]
        for first in range(0, part_size, chunk):
            last = min(first + chunk, part_size)
            part, lanes = slice(base + first, base + last), slice(first, last)
            gate, up = dot_nt(these, buf[0, part, :]), dot_nt(these, buf[1, part, :])
            act_grad = dot_nt(outers, buf[2, part, :])
            square = gate * gate
            inner = gate * (0.7978845608028654 + (0.7978845608028654 * 0.044715) * square)
            rise = 0.5 + 0.5 * jnp.tanh(inner)
            bent = gate * rise
            act[spot, lanes] = (bent * up).astype(BF16)
            slope = rise + bent * (1.0 - rise) * (
                2 * 0.7978845608028654 + (6 * 0.7978845608028654 * 0.044715) * square
            )
            low[0, spot, lanes] = (act_grad * up * slope).astype(BF16)
            low[1, spot, lanes] = (act_grad * bent).astype(BF16)
        whole = slice(base, base + part_size)
        result = dot_nn(act[spot, :], buf[2, whole, :])
        back = dot_nn(low[0, spot, :], buf[0, whole, :]) + dot_nn(low[1, spot, :], buf[1, whole, :])
        return spot, result, back

    def near_step(step, carry):
        pair = flip(my_pair, step, pairs)
        first = 2 * pair

        @pl.when(step == 0)
        def _():
            peer = flip(me, 1, size)
            for copy in forth(me, peer, peer):
                copy.wait_recv()

        @pl.when(step > 0)
        def _():
            for which in range(2):
                for copy in forth(me, first + which, first + which):
                    copy.wait_recv()

        for which in range(2):
            gate = column_of(gates[first + which, 0:1, :], capacity)
            spot = pl.ds(pl.multiple_of((first + which) * capacity, capacity), capacity)
            low_outer[spot, :] = (outer[first + which].astype(F32) * gate).astype(BF16)
        spot, result, back = hidden_part(pair, 0)
        made_sum[spot, :] = result
        back_sum[spot, :] = back
        return carry

    def sent_all(copies):
        for remote_one, copy in copies:
            if remote_one:
                copy.wait_send()
            else:
                copy.wait()

    def weight_grads(half):
        every = rows[...].reshape(size * capacity, width)
        outers = low_outer[...]
        count = 0
        base = half * part_size
        waiting = {}
        for c in range(3):
            left = act if c == 2 else low.at[c]
            for first in range(0, part_size, 2 * chunk):
                last = min(first + 2 * chunk, part_size)
                slot = count % 2
                sent_all(waiting.pop(slot, ()))
                piece = dot_tn(left[:, first:last], outers if c == 2 else every)
                grad_stage[slot, : last - first, :] = piece.astype(BF16)
                copies = []
                begin = base + first
                while begin < base + last:
                    group = begin // share
                    end = min(base + last, (group + 1) * share)
                    source = grad_stage.at[slot, pl.ds(begin - base - first, end - begin)]
                    spot = pl.ds(begin - group * share, end - begin)
                    sem = grad_sems.at[slot, len(copies)]
                    if group % 2:
                        target = moved_out.at[group // 2, c, spot]
                        copies.append((True, remote_copy(source, target, sem, moved_sem, "wshard", near)))
                    else:
                        target = grad_out.at[group // 2, c, spot]
                        copies.append((False, pltpu.make_async_copy(source, target, sem)))
                    begin = end
                for _, copy in copies:
                    copy.start()
                waiting[slot] = copies
                count += 1
        for copies in waiting.values():
            sent_all(copies)

    for group in range(groups // 2):
        for copy in weight_copies(group):
            copy.wait()
    lax.fori_loop(0, pairs, near_step, 0)
    weight_grads(0)

    def far_step(step, carry):
        pair = flip(my_pair, pairs - 1 - step, pairs)
        first = 2 * pair
        spot, result, back = hidden_part(pair, part_size)
        result = (made_sum[spot, :] + result).astype(BF16)
        back = (back_sum[spot, :] + back).astype(BF16)
        two = pl.ds(first, 2)
        made[two] = result.reshape(2, capacity, width)
        stage[two] = back.reshape(2, capacity, width)
        for which in range(2):
            grads = outer[first + which].astype(F32) * made[first + which].astype(F32)
            line = row_of(jnp.sum(grads, -1, keepdims=True), extra_stage.shape[2])
            extra_stage[first + which] = jnp.broadcast_to(line, extra_stage.shape[1:])
        pltpu.make_async_copy(made.at[two], made_out.at[two], save_sems.at[step]).start()

        @pl.when(step < pairs - 1)
        def _():
            for which in range(2):
                for copy in back_copies(first + which, me, first + which):
                    copy.start()

        @pl.when(step == pairs - 1)
        def _():
            peer = flip(me, 1, size)
            for copy in back_copies(peer, me, peer):
                copy.start()
            for copy in own_back:
                copy.start()

        return carry

    for group in range(groups // 2, groups):
        for copy in weight_copies(group):
            copy.wait()
    lax.fori_loop(0, pairs, far_step, 0)
    weight_grads(1)
    for copy in own_back:
        copy.wait()
    remote_copy(moved_out, moved_out, moved_sem, moved_sem, "wshard", near).wait_recv()
    for step in range(pairs):
        two = pl.ds(2 * flip(my_pair, pairs - 1 - step, pairs), 2)
        pltpu.make_async_copy(made.at[two], made_out.at[two], save_sems.at[step]).wait()
    for step in range(1, size):
        peer = flip(me, step, size)
        for copy in forth(peer, me, peer):
            copy.wait_send()
        for copy in back_copies(peer, me, peer):
            copy.wait_send()
        for copy in back_copies(me, peer, peer):
            copy.wait_recv()


def moe(sent, gates, outer, own_in, own_down, other_in, other_down, chunk=256):
    size, capacity, width = sent.shape
    groups = 1 + other_in.shape[0]
    share = own_down.shape[0]
    part = share * groups // 2
    total = size * capacity
    extra = gates.shape[1:]
    dma = pltpu.SemaphoreType.DMA
    result = pl.pallas_call(
        functools.partial(moe_body, size, groups, chunk),
        out_shape=(
            shape_of((size, capacity, width), BF16),
            shape_of((size, *extra), F32),
            shape_of((size, capacity, width), BF16),
        )
        + (shape_of((2, 3, share, width), BF16),) * 2,
        in_specs=[ANY] * 7,
        out_specs=(ANY,) * 5,
        scratch_shapes=[
            pltpu.VMEM((3, share * groups, width), BF16),
            pltpu.VMEM((size, capacity, width), BF16),
            pltpu.VMEM((size, *extra), F32),
            pltpu.VMEM((size, capacity, width), BF16),
            pltpu.VMEM((total, width), BF16),
            pltpu.VMEM((total, width), F32),
            pltpu.VMEM((total, width), F32),
            pltpu.VMEM((total, part), BF16),
            pltpu.VMEM((2, total, part), BF16),
            pltpu.VMEM((size, capacity, width), BF16),
            pltpu.VMEM((size, *extra), F32),
            pltpu.VMEM((size, capacity, width), BF16),
            pltpu.VMEM((2, 2 * chunk, width), BF16),
            dma((groups, 2)),
            dma((size, 2)),
            dma((size, 2)),
            dma((size, 2)),
            dma((size, 2)),
            dma((5,)),
            dma((size // 2,)),
            dma((2, 3)),
            dma,
        ],
        cost_estimate=pl.CostEstimate(flops=LIGHT, bytes_accessed=LIGHT, transcendentals=0),
        compiler_params=pltpu.CompilerParams(
            collective_id=0, has_side_effects=True, vmem_limit_bytes=66_000_000
        ),
        name="experts",
    )(sent, gates, outer, own_in, own_down, other_in, other_down)
    return result


def expert_body(groups, chunk, rows_ref, outer_ref, gate_ref, *refs):
    in_refs, down_refs = refs[:groups], refs[groups : 2 * groups]
    made_ref, back_ref, outer_out_ref, gate_grad_ref = refs[2 * groups : 2 * groups + 4]
    act_ref, low_ref, buf_ref, sems = refs[2 * groups + 4 :]
    share = down_refs[0].shape[0]
    hidden = share * groups

    def copies(group):
        spot = pl.ds(group * share, share)
        return (
            pltpu.make_async_copy(in_refs[group], buf_ref.at[0:2, spot], sems.at[2 * group]),
            pltpu.make_async_copy(down_refs[group], buf_ref.at[2, spot], sems.at[2 * group + 1]),
        )

    @pl.when(pl.program_id(0) == 0)
    def _():
        for group in range(groups):
            for copy in copies(group):
                copy.start()

    rows = rows_ref[...]
    low_outer = (outer_ref[...].astype(F32) * gate_ref[...]).astype(BF16)
    outer_out_ref[...] = low_outer

    @pl.when(pl.program_id(0) == 0)
    def _():
        for group in range(groups):
            for copy in copies(group):
                copy.wait()

    for first in range(0, hidden, chunk):
        part = slice(first, first + chunk)
        gate, up = dot_nt(rows, buf_ref[0, part, :]), dot_nt(rows, buf_ref[1, part, :])
        act_grad = dot_nt(low_outer, buf_ref[2, part, :])
        square = gate * gate
        inner = gate * (0.7978845608028654 + (0.7978845608028654 * 0.044715) * square)
        rise = 0.5 + 0.5 * jnp.tanh(inner)
        bent = gate * rise
        act_ref[:, part] = (bent * up).astype(BF16)
        slope = rise + bent * (1.0 - rise) * (
            2 * 0.7978845608028654 + (6 * 0.7978845608028654 * 0.044715) * square
        )
        low_ref[0, :, part] = (act_grad * up * slope).astype(BF16)
        low_ref[1, :, part] = (act_grad * bent).astype(BF16)
    made = dot_nn(act_ref[...], buf_ref[2]).astype(BF16)
    made_ref[...] = made
    back = dot_nn(low_ref[0], buf_ref[0]) + dot_nn(low_ref[1], buf_ref[1])
    back_ref[...] = back.astype(BF16)
    gate_grad_ref[...] = jnp.sum(
        outer_ref[...].astype(F32) * made.astype(F32), -1, keepdims=True
    )


def experts_pass(rows, outer, gate_column, in_weights, down_weights, block=320, chunk=256):
    total, width = rows.shape
    groups = len(in_weights)
    hidden = down_weights[0].shape[0] * groups
    row_spec = pl.BlockSpec((block, width), lambda i: (i, 0))
    column = pl.BlockSpec((block, 1), lambda i: (i, 0))
    wide = pl.BlockSpec((block, hidden), lambda i: (i, 0))
    both = pl.BlockSpec((2, block, hidden), lambda i: (0, i, 0))
    return pl.pallas_call(
        functools.partial(expert_body, groups, chunk),
        grid=(total // block,),
        out_shape=(
            shape_of((total, width), BF16),
            shape_of((total, width), BF16),
            shape_of((total, width), BF16),
            shape_of((total, 1), F32),
            shape_of((total, hidden), BF16),
            shape_of((2, total, hidden), BF16),
        ),
        in_specs=[row_spec, row_spec, column] + [ANY] * (2 * groups),
        out_specs=(row_spec, row_spec, row_spec, column, wide, both),
        scratch_shapes=[
            pltpu.VMEM((3, hidden, width), BF16),
            pltpu.SemaphoreType.DMA((2 * groups,)),
        ],
        cost_estimate=pl.CostEstimate(flops=LIGHT, bytes_accessed=LIGHT, transcendentals=0),
        name="experts",
    )(rows, outer, gate_column, *in_weights, *down_weights)


def moe_plain(sent, gates, outer, own_in, own_down, other_in, other_down):
    in_weights, down_weights = [own_in, *other_in], [own_down, *other_down]
    size, capacity, width = sent.shape
    total = size * capacity
    rows = exchange(sent.reshape(total, width), "dp").reshape(total, width)
    gate_column = lax.all_to_all(gates, "dp", 0, 0, tiled=True)[:, 0, :capacity].reshape(total, 1)
    made, back, outer_low, gate_grads, act, low = experts_pass(
        rows, outer.reshape(total, width), gate_column, in_weights, down_weights
    )
    extra = jnp.pad(gate_grads.reshape(size, 1, capacity), ((0, 0), (0, EXTRA - 1), (0, 0)))
    extra = lax.all_to_all(extra, "dp", 0, 0, tiled=True)
    share = down_weights[0].shape[0]
    grads = []
    for group in range(len(in_weights)):
        part = slice(group * share, (group + 1) * share)
        pieces = [dot_tn(low[c, :, part], rows) for c in range(2)]
        grads.append(jnp.stack(pieces + [dot_tn(act[:, part], outer_low)]).astype(BF16))
    shape = (size, capacity, width)
    moved = jnp.stack([swap(grads[g], "wshard", 1) for g in (1, 3)])
    return exchange(back, "dp"), extra, made.reshape(shape), jnp.stack(grads[::2]), moved


def rear_body(
    size, groups, head_size, remote_made, span_ref, gain_ref, diag_ref, ones_ref, router_ref, col_ref, gate_ref,
    extra_ref, tok_hbm, cot_hbm, hidden_hbm, norm_hbm, mixed_hbm, rows_hbm, made_hbm, outw_hbm,
    qkvw_hbm, qkv_hbm, far_hbm,
    output_ref, grad_ref, early_out, late_out, sum_out, far_out,
    tok, cot, hidden, norm, mixed, rows, made, outw, qkvw, qkv, norm_t, mask, grad_hidden,
    grads, probs_ref, scores_ref, diag_sums, wo, wo_got, wg, wg_got, total,
    total_got, sum_ref, early_ref, early_got, late_ref, late_got,
    load_sems, weight_sems, made_send, made_got, part_sems, total_sems, small_sems, far_sems,
):
    me, place = lax.axis_index("dp"), lax.axis_index("wshard")
    near, far = flip(place, 1, groups), flip(place, 2, groups)
    dp_bits, shard_bits = bits_below(size), bits_below(groups)
    peers = [("dp", flip(me, step, size)) for step in range(1, size)]
    greet(peers + [("wshard", near), ("wshard", far)])
    count, width = tok.shape
    blocks = count // TILE
    experts = size
    capacity = rows.shape[0] // experts
    cols = outw.shape[2]
    two_heads = 2 * head_size
    branch, mixgrad, norm_grad = cot, norm, hidden

    loads = [
        pltpu.make_async_copy(source, target, load_sems.at[i])
        for i, (source, target) in enumerate(
            (
                (rows_hbm, rows), (norm_hbm, norm), (hidden_hbm, hidden), (cot_hbm, cot),
                (mixed_hbm, mixed), (outw_hbm, outw), (tok_hbm, tok), (qkv_hbm, qkv),
                (made_hbm.at[me], made.at[me]) if remote_made else (made_hbm, rows),
            )
        )
    ]
    for copy in loads[: 9 if remote_made else 8]:
        copy.start()

    def far_copy(piece):
        return remote_copy(
            far_hbm.at[piece], far_out.at[piece], far_sems.at[piece, 0], far_sems.at[piece, 1],
            "wshard", far,
        )

    far_copy(0).start()

    def weight_load(step):
        slot = lax.rem(step, 2)
        return pltpu.make_async_copy(
            qkvw_hbm.at[groups - 1 - step], qkvw.at[slot], weight_sems.at[slot]
        )

    hidden_again = pltpu.make_async_copy(hidden_hbm, hidden, load_sems.at[9])

    def made_copy(source, target, peer):
        return remote_copy(
            made_hbm.at[source], made.at[target], made_send.at[source], made_got.at[target], "dp",
            peer,
        )

    if remote_made:
        for _, peer in peers:
            made_copy(peer, me, peer).start()

    exchanges = [("wshard", place, bit, groups) for bit in shard_bits]
    exchanges += [("dp", me, bit, size) for bit in dp_bits]

    def small_copy(kind, ref, got, step):
        axis, index, bit, length = exchanges[step]
        return remote_copy(
            ref, got.at[step], small_sems.at[kind, step, 0], small_sems.at[kind, step, 1], axis,
            flip(index, bit, length),
        )

    def small_step(kind, ref, got, step):
        now, before = step % 2, (step + 1) % 2
        if step > 0:
            small_copy(kind, ref.at[before], got, step - 1).wait()
            ref[now] = ref[before] + got[step - 1]
        if step < len(exchanges):
            small_copy(kind, ref.at[now], got, step).start()

    slots = [col_ref[:, k : k + 1] for k in range(2)]
    gates = [gate_ref[:, k : k + 1] for k in range(2)]
    lane = iota((count, extra_ref.shape[2]), 1)
    picked = [0.0, 0.0]
    for copy in loads[:1]:
        copy.wait()
    grads_in = 0.0
    for expert in range(experts):
        label = jnp.where(lane < capacity, lane + expert * capacity, -1)
        for k in range(2):
            picked[k] = picked[k] + jnp.where(label == slots[k], extra_ref[expert, 0:1, :], 0.0)
    gate_grads = [jnp.sum(p, -1, keepdims=True) for p in picked]
    mean = gates[0] * gate_grads[0] + gates[1] * gate_grads[1]
    lane = iota((count, 3 * experts), 1)
    part = (lane >= experts).astype(I32) + (lane >= 2 * experts).astype(I32)
    label = lane - part * experts
    logit_grads = 0.0
    for k in range(2):
        own = (label * capacity <= slots[k]) & (slots[k] < (label + 1) * capacity)
        logit_grads = logit_grads + jnp.where(own, gates[k] * (gate_grads[k] - mean), 0.0)
    high, middle, low = split_three(logit_grads)
    split = jnp.where(part == 0, high, jnp.where(part == 1, middle, low)).astype(BF16)
    hits = [onehot_columns(slots[k], 0, experts * capacity) for k in range(2)]
    hits = (hits[0] | hits[1]).astype(F32).astype(BF16)
    for copy in loads[1:4]:
        copy.wait()
    normed_grad = dot_nn(hits, rows[...])
    normed_grad = normed_grad + dot_nn(split, router_ref[...])
    router_grad = dot_tn(split, norm[...])
    early_ref[0, :experts, :] = (
        router_grad[:experts] + router_grad[experts : 2 * experts] + router_grad[2 * experts :]
    )
    unit, recip = unit_norm(hidden[...])
    early_ref[0, experts:, :] = jnp.broadcast_to(
        jnp.sum(normed_grad * unit, 0, keepdims=True), (EXTRA, width)
    )
    small_step(0, early_ref, early_got, 0)
    scaled = normed_grad * gain_ref[1:2, :]
    back = recip * (scaled - unit * jnp.mean(scaled * unit, -1, keepdims=True))
    grad_hidden[...] = cot[...].astype(F32) + back
    branch[...] = grad_hidden[...].astype(BF16)
    for copy in loads[4:6]:
        copy.wait()
    mixed_t = mixed[...].T
    result = 0.0

    def part_copy(item, source, target, kind, axis, peer):
        return remote_copy(
            source, target, part_sems.at[item, kind, 0], part_sems.at[item, kind, 1], axis, peer
        )

    def out_copy(kind):
        return part_copy(
            0, wo.at[(3, 1, 2)[kind]], wo_got.at[kind], kind, "wshard", far if kind == 2 else near
        )

    def qkv_copy(kind):
        return part_copy(
            1, wg.at[(2, 0, 1)[kind]], wg_got.at[kind], kind, "wshard", far if kind == 2 else near
        )

    for group in reversed(range(groups)):
        lanes = pl.ds(pl.multiple_of(flip(place, group, groups) * cols, cols), cols)
        piece = branch[:, lanes]
        result = result + dot_nt(piece, outw[group])
        wo[group] = dot_nn(mixed_t, piece).astype(BF16)
        if group == 3:
            out_copy(0).start()
        if group == 1:
            out_copy(1).start()
    mixgrad[...] = result.astype(BF16)
    for copy in loads[6:8]:
        copy.wait()
    weight_load(0).start()
    unit, _ = unit_norm(tok[...].astype(F32))
    norm_t[...] = (unit * gain_ref[0:1, :]).astype(BF16).T
    fill_mask(mask, span_ref[0])
    norm_grad[...] = jnp.zeros_like(norm_grad)

    def attend_group(step):
        group = groups - 1 - step
        slot = lax.rem(step, 2)
        weight_load(step).wait()

        @pl.when(step < groups - 1)
        def _():
            weight_load(step + 1).start()

        owner = flip(place, group, groups)
        heads = cols // head_size

        def pair(p, carry):
            offset = pl.multiple_of(p * two_heads, two_heads)
            lanes = pl.ds(offset, two_heads)
            query, keys, value = (qkv[group, c, :, lanes] for c in range(3))
            outer = mixgrad[:, pl.ds(pl.multiple_of(owner * cols + offset, two_heads), two_heads)]
            query_sum, key_sum, value_sum = [None] * blocks, None, None
            for which in range(2):
                head = owner * heads + 2 * p + which
                own = head_lanes(which, head_size)
                own_query, own_key, own_outer = query * own, keys * own, outer * own
                shrunk = own_query * 0.125
                tiles, far_bias = bias_tiles(diag_ref[pl.ds(head, 1), :])
                near_sums, far_sums = [None] * 3, [None] * 2
                for block in range(blocks):
                    piece = slice(block * TILE, (block + 1) * TILE)
                    probs = softmax_tiles(
                        score_tiles(block, shrunk[piece], keys, tiles, far_bias, mask)
                    )
                    prob_grads = dot_nt(own_outer[piece], value)
                    prob_grads = [prob_grads[:, j * TILE : (j + 1) * TILE] for j in range(blocks)]
                    delta = functools.reduce(jnp.add, [a * b for a, b in zip(probs, prob_grads)])
                    delta = jnp.sum(delta, -1, keepdims=True)
                    lows = [(a * (b - delta)).astype(BF16) for a, b in zip(probs, prob_grads)]
                    for other in range(blocks):
                        step = block - other
                        wide = lows[other].astype(F32)
                        if abs(step) >= 2:
                            side = 0 if step > 0 else 1
                            old = far_sums[side]
                            far_sums[side] = wide if old is None else old + wide
                        else:
                            old = near_sums[step + 1]
                            near_sums[step + 1] = wide if old is None else old + wide
                    probs_ref[which, piece, :] = jnp.concatenate([t.astype(BF16) for t in probs], 1)
                    lows = jnp.concatenate(lows, 1)
                    scores_ref[which, piece, :] = lows
                    more = dot_nn(lows, own_key)
                    query_sum[block] = more if which == 0 else query_sum[block] + more
                more = dot_tn(scores_ref[which], own_query)
                key_sum = more if which == 0 else key_sum + more
                more = dot_tn(probs_ref[which], own_outer)
                value_sum = more if which == 0 else value_sum + more
                for step in range(3):
                    wide = jnp.concatenate([near_sums[step], jnp.zeros((TILE, TILE), F32)], 1)
                    half = TILE // 2
                    while half:
                        turned = pltpu.roll(wide[half:], 2 * TILE - half, 1)
                        wide = wide[:half] + turned
                        half //= 2
                    for side in range(2):
                        spot = 2 * step + side
                        diag_sums[head, spot : spot + 1, :] = wide[:, TILE * side : TILE * (side + 1)]
                for side in range(2):
                    diag_sums[head, 6 + side : 7 + side, :] = jnp.sum(far_sums[side], 0, keepdims=True)
            for block in range(blocks):
                piece = slice(block * TILE, (block + 1) * TILE)
                grads[0, piece, lanes] = (query_sum[block] * 0.125).astype(BF16)
            grads[1, :, lanes] = (key_sum * 0.125).astype(BF16)
            grads[2, :, lanes] = value_sum.astype(BF16)
            return carry

        lax.fori_loop(0, cols // two_heads, pair, 0)
        for c in range(3):
            weight_grad = dot_nn(norm_t[...], grads[c]).astype(BF16)

            @pl.when(group > 0)
            def _():
                wg[group - 1, c] = weight_grad

            @pl.when(group == 0)
            def _():
                total[c * width : (c + 1) * width, :] = weight_grad

            norm_grad[...] += dot_nt(grads[c], qkvw[slot, c])

    def add_into(target, *others):
        for first in range(0, target.shape[0], 256):
            spot = slice(first, first + 256)
            value = target[spot].astype(F32)
            for other in others:
                value = value + other[spot].astype(F32)
            target[spot] = value.astype(BF16)

    def group_step(step, carry):
        attend_group(step)

        @pl.when(step == 0)
        def _():
            qkv_copy(0).start()
            small_step(0, early_ref, early_got, 1)
            out_copy(0).wait_recv()
            add_into(wo.at[2], wo_got.at[0])
            out_copy(2).start()

        @pl.when(step == 1)
        def _():
            qkv_copy(0).wait_recv()
            for c in range(3):
                add_into(wg.at[1, c], wg_got.at[0, c])
            qkv_copy(2).start()
            far_copy(1).start()
            far_copy(2).start()
            small_step(0, early_ref, early_got, 2)

        @pl.when(step == 2)
        def _():
            qkv_copy(1).start()
            small_step(0, early_ref, early_got, 3)

        return carry

    lax.fori_loop(0, groups, group_step, 0)

    small_step(0, early_ref, early_got, 4)
    unit, recip = unit_norm(tok[...].astype(F32))
    gain_grad = jnp.sum(norm_grad[...] * unit, 0, keepdims=True)
    table_grad = 0.0
    for k in range(8):
        for piece in split_three(diag_sums[:, k, :]):
            table_grad = table_grad + dot_nt(piece.astype(BF16), ones_ref[:, k * TILE : (k + 1) * TILE])
    late_ref[0] = jnp.zeros(late_ref.shape[1:], F32)
    for k in range(width // TILE):
        late_ref[0, k : k + 1, :] = gain_grad[:, k * TILE : (k + 1) * TILE]
    heads, buckets = table_grad.shape
    late_ref[0, 8 : 8 + heads, :buckets] = table_grad
    small_step(1, late_ref, late_got, 0)

    qkv_copy(1).wait_recv()
    out_copy(1).wait_recv()
    out_copy(2).wait_recv()
    qkv_copy(2).wait_recv()
    third = outw.shape[1]
    for c in range(3):
        add_into(total.at[c * third : (c + 1) * third], wg_got.at[1, c], wg_got.at[2, c])
    add_into(wo.at[0], wo_got.at[1], wo_got.at[2])
    total[3 * third :, :] = wo[0]
    parts = 2
    length = total.shape[0] // parts
    stages = len(dp_bits)

    def bit_of(step):
        return lax.rem(lax.div(me, dp_bits[step]), 2)

    def segment(part, step):
        first, size_of = part * length, length
        for s in range(step):
            size_of //= 2
            first = first + bit_of(s) * size_of
        return first, size_of

    def halving(part, step):
        first, size_of = segment(part, step)
        half = size_of // 2
        away = pl.multiple_of(first + (1 - bit_of(step)) * half, half)
        return remote_copy(
            total.at[pl.ds(away, half)],
            total_got.at[pl.ds(part * length + length - size_of, half)],
            total_sems.at[part, 0, step, 0], total_sems.at[part, 0, step, 1], "dp",
            flip(me, dp_bits[step], size),
        )

    def add_half(part, step):
        first, half = segment(part, step + 1)
        first = pl.multiple_of(first, half)
        got = part * length + length - 2 * half
        value = total[pl.ds(first, half), :].astype(F32) + total_got[got : got + half, :].astype(F32)
        total[pl.ds(first, half), :] = value.astype(BF16)
        if step == stages - 1:
            sum_ref[pl.ds(first, half), :] = value.astype(BF16)

    def doubling(part, step):
        first, size_of = segment(part, step + 1)
        spot = pl.ds(pl.multiple_of(first, size_of), size_of)
        return remote_copy(
            sum_ref.at[spot], sum_ref.at[spot],
            total_sems.at[part, 1, step, 0], total_sems.at[part, 1, step, 1], "dp",
            flip(me, dp_bits[step], size),
        )

    def sum_stage(part, stage):
        if 0 < stage <= stages:
            halving(part, stage - 1).wait()
            add_half(part, stage - 1)
        elif stage > stages:
            doubling(part, 2 * stages - stage).wait()
        if stage < stages:
            halving(part, stage).start()
        elif stage < 2 * stages:
            doubling(part, 2 * stages - 1 - stage).start()

    def finish_tokens():
        scaled = norm_grad[...] * gain_ref[0:1, :]
        back = recip * (scaled - unit * jnp.mean(scaled * unit, -1, keepdims=True))
        grad_ref[...] = (grad_hidden[...] + back).astype(BF16)
        hidden_again.start()
        if not remote_made:
            loads[8].start()

    def finish_output():
        loads[8].wait()
        hidden_again.wait()
        if remote_made:
            for _, peer in peers:
                made_copy(me, peer, peer).wait_recv()
        values = made[...].reshape(experts * capacity, width) if remote_made else rows[...]
        for first in range(0, count, 256):
            spot = slice(first, first + 256)
            value = hidden[spot, :]
            for k in range(2):
                hit = onehot_columns(slots[k][spot], 0, experts * capacity)
                value = value + gates[k][spot] * dot_nn(hit.astype(F32).astype(BF16), values)
            output_ref[spot, :] = value.astype(BF16)

    rest_early = list(range(groups + 1, len(exchanges) + 1))
    rest_late = list(range(1, len(exchanges) + 1))

    def next_small():
        if rest_early:
            small_step(0, early_ref, early_got, rest_early.pop(0))
        if rest_late:
            small_step(1, late_ref, late_got, rest_late.pop(0))

    sum_stage(0, 0)
    sum_stage(1, 0)
    finish_tokens()
    next_small()
    sum_stage(0, 1)
    finish_output()
    next_small()
    sum_stage(1, 1)
    for stage in range(2, 2 * stages + 1):
        next_small()
        for part in range(parts):
            sum_stage(part, stage)
    while rest_early or rest_late:
        next_small()
    early_out[...] = early_ref[len(exchanges) % 2]
    late_out[...] = late_ref[len(exchanges) % 2]
    save = pltpu.make_async_copy(sum_ref, sum_out, load_sems.at[10])
    save.start()
    save.wait()
    for piece in range(3):
        far_copy(piece).wait()
    if remote_made:
        for _, peer in peers:
            made_copy(peer, me, peer).wait_send()
    for kind in range(3):
        out_copy(kind).wait_send()
        qkv_copy(kind).wait_send()


def bits_below(size):
    return [1 << b for b in range(size.bit_length() - 1)]


def rear(
    span, gains, diag, ones, router_t3, slots_col, gates, extra, tokens, cotangent, hidden, normed,
    mixed, rows, made, out_weights, qkv_weights, qkv, far_sum, head_size,
):
    count, width = tokens.shape
    size, groups = lax.axis_size("dp"), lax.axis_size("wshard")
    heads, buckets = width // head_size, ones.shape[0]
    experts = router_t3.shape[0] // 3
    cols = out_weights.shape[2]
    exchanges = len(bits_below(size)) + len(bits_below(groups))
    dma = pltpu.SemaphoreType.DMA
    wide, small = (count, width), (experts + EXTRA, width)
    late = (8 + heads, TILE)
    total = (4 * width, cols)
    vmem = pltpu.VMEM
    return pl.pallas_call(
        functools.partial(rear_body, size, groups, head_size, made.ndim == 3),
        out_shape=(
            shape_of(wide, BF16),
            shape_of(wide, BF16),
            shape_of(small, F32),
            shape_of(late, F32),
            shape_of(total, BF16),
            shape_of(far_sum.shape, BF16),
        ),
        in_specs=[SMEM] + [VMEM] * 7 + [ANY] * 11,
        out_specs=(VMEM,) * 4 + (ANY,) * 2,
        scratch_shapes=[
            vmem(wide, BF16),
            vmem(wide, BF16),
            vmem(wide, F32),
            vmem(wide, BF16),
            vmem(wide, BF16),
            vmem(rows.shape, BF16),
            vmem(made.shape if made.ndim == 3 else (16, TILE), BF16),
            vmem(out_weights.shape, BF16),
            vmem((2, *qkv_weights.shape[1:]), BF16),
            vmem(qkv.shape, BF16),
            vmem((width, count), BF16),
            vmem((count, count), F32),
            vmem(wide, F32),
            vmem((3, count, cols), BF16),
            vmem((2, count, count), BF16),
            vmem((2, count, count), BF16),
            vmem((heads, 8, TILE), F32),
            vmem((groups, width, cols), BF16),
            vmem((3, width, cols), BF16),
            vmem((groups - 1, 3, width, cols), BF16),
            vmem((3, 3, width, cols), BF16),
            vmem(total, BF16),
            vmem(total, BF16),
            vmem(total, BF16),
            vmem((2, *small), F32),
            vmem((exchanges, *small), F32),
            vmem((2, *late), F32),
            vmem((exchanges, *late), F32),
            dma((11,)),
            dma((2,)),
            dma((size,)),
            dma((size,)),
            dma((2, 3, 2)),
            dma((2, 2, len(bits_below(size)), 2)),
            dma((2, exchanges, 2)),
            dma((3, 2)),
        ],
        cost_estimate=pl.CostEstimate(flops=LIGHT, bytes_accessed=LIGHT, transcendentals=0),
        compiler_params=pltpu.CompilerParams(
            collective_id=2, has_side_effects=True, vmem_limit_bytes=66_000_000
        ),
        name="rear",
    )(
        span, gains, diag, ones, router_t3, slots_col, gates, extra, tokens, cotangent, hidden,
        normed, mixed, rows, made, out_weights, qkv_weights, qkv, far_sum,
    )


def swap(value, axis, bit):
    size = lax.axis_size(axis)
    return lax.ppermute(value, axis, [(i, i ^ bit) for i in range(size)])


def bits_of(axis):
    size = lax.axis_size(axis)
    return [1 << b for b in range(size.bit_length() - 1)]


def after(value, *others):
    return lax.optimization_barrier((value, *others))[0]


def exchange(rows, axis):
    size = lax.axis_size(axis)
    total, width = rows.shape
    blocks = rows.reshape(size, total // size, width)
    return lax.all_to_all(blocks, axis, 0, 0, tiled=True)


def per_device(
    tokens,
    cotangent,
    span_starts,
    routes,
    norm_gains,
    bias_table,
    router,
    attn_qkv,
    attn_out,
    expert_in,
    expert_down,
):
    assert span_starts.shape[0] == 1
    tok_count, model_width = tokens.shape
    buckets, head_count = bias_table.shape
    head_size = model_width // head_count
    experts = router.shape[1]
    capacity = (10 * tok_count + 4 * experts - 1) // (4 * experts)
    total = experts * capacity
    place = lax.axis_index("wshard")
    where = jnp.stack([place.astype(I32), span_starts[0]])
    diag = jnp.asarray(diagonal_ones(buckets))
    diag_bias = jnp.dot(bias_table.T, diag, precision=PRECISE)
    router_t = router.T
    expert_in = jnp.swapaxes(expert_in[0], 1, 2)
    expert_down = expert_down[0]

    shards = (attn_qkv, attn_out, expert_in, expert_down)
    (
        slots_col, gates, sent_gates, qkv_all, out_all, qkv, mixed, hidden, normed_two, sent,
        outer_rows, in_other, down_other,
    ) = front(
        span_starts, routes, norm_gains, diag_bias, router_t, tokens, cotangent, shards, head_size,
        capacity,
    )
    groups = out_all.shape[0]
    through = moe if capacity % 16 == 0 else moe_plain
    back_rows, back_extra, made, expert_grads, moved = through(
        sent, sent_gates, outer_rows, expert_in, expert_down, in_other, down_other
    )
    far_sum = (expert_grads[1].astype(F32) + moved[1].astype(F32)).astype(BF16)
    if through is moe_plain:
        made = exchange(made.reshape(total, model_width), "dp").reshape(total, model_width)

    output, grad_tokens, early, late, attn_sum, far_got = rear(
        span_starts, norm_gains, diag_bias, diag.astype(BF16), jnp.concatenate([router_t] * 3, 0),
        slots_col, gates, back_extra, tokens, cotangent, hidden, normed_two,
        mixed, back_rows.reshape(total, model_width), made, out_all, qkv_all, qkv, far_sum, head_size,
    )

    def expert_sum(part):
        pieces = (expert_grads[0, part], moved[0, part], far_got[part])
        return functools.reduce(jnp.add, [piece.astype(F32) for piece in pieces])

    grad_expert_in = jnp.swapaxes(expert_sum(slice(0, 2)), 1, 2)[None]
    grad_expert_down = expert_sum(2)[None]
    cols = out_all.shape[2]
    grad_attn_qkv = attn_sum[: 3 * model_width].astype(F32).reshape(3, model_width, cols)
    grad_attn_out = attn_sum[3 * model_width :].astype(F32)
    gain_rows = model_width // TILE
    gain_one = late[:gain_rows].reshape(model_width)
    return (
        output,
        grad_tokens,
        jnp.stack([gain_one, early[experts]]),
        late[gain_rows:, :buckets].T,
        early[:experts].T,
        grad_attn_qkv,
        grad_attn_out,
        grad_expert_in,
        grad_expert_down,
    )


def solution(mesh):
    return jax.shard_map(
        per_device,
        mesh=mesh,
        in_specs=(
            P(("dp", "wshard"), None),
            P(("dp", "wshard"), None),
            P(("dp", "wshard")),
            P(("dp", "wshard"), None),
            P(),
            P(),
            P(),
            P(None, None, "wshard"),
            P(None, "wshard"),
            P("dp", None, None, "wshard"),
            P("dp", "wshard", None),
        ),
        out_specs=(
            P(("dp", "wshard"), None),
            P(("dp", "wshard"), None),
            P(),
            P(),
            P(),
            P(None, None, "wshard"),
            P(None, "wshard"),
            P("dp", None, None, "wshard"),
            P("dp", "wshard", None),
        ),
        check_vma=False,
    )
```

time: 648 us -> 538 us (0.83)
  waiting for transfers between devices: 241 us -> 0 us
  Pallas kernels: 270 us -> 496 us
  starting transfers between devices: 74.1 us -> 0 us
  other arithmetic: 36.6 us -> 24.4 us
  local copies, waits for them, and re-layouts: 13.1 us -> 4 us
    ppermute x49 -> x0, waiting for transfers between devices: 241 us -> none  [swap(): return lax.ppermute(value, axis, [(i, i ^ bit) for i in range(size)])]
    pallas_call x13 -> x2, Pallas kernels: 126 us -> 359 us  [the longest x1 207 us: rear(): pl.pallas_call(functools.partial(rear_body, size, groups, head_size, made...]
    ppermute x49 -> x0, starting transfers between devices: 62.3 us -> none  [swap(): return lax.ppermute(value, axis, [(i, i ^ bit) for i in range(size)])]
    all_to_all x2 -> x0, starting transfers between devices: 11.8 us -> none  [exchange(): return lax.all_to_all(blocks, axis, 0, 0, tiled=True)]
    convert_element_type x14 -> x2, other arithmetic: 17.9 us -> 9 us  [the longest x1 7.95 us: per_device(): far_sum = (expert_grads[1].astype(F32) + moved[1].astype(F32)).astype(BF16)]
    broadcast_in_dim x0 -> x1, other arithmetic: none -> 7.36 us  [per_device(): grad_expert_in = jnp.swapaxes(expert_sum(slice(0, 2)), 1, 2)[None]]
    pallas_call x1, Pallas kernels: 144 us -> 137 us  [moe(): pl.pallas_call(functools.partial(moe_body, size, groups, chunk), out_shap...]
  transfers between devices with their start and end apart: 51 -> 0, of which waited for: 21 -> 0; matrix products, arithmetic and copies ran while one was open for 5% -> 0% of each run, Pallas kernels for 20% -> 0%
where the time goes in v3:
time: 538 us; the launch traced here: 528 us
  Pallas kernels  496 us (92%)
  other arithmetic  24.4 us (5%)
    pallas_call x1, Pallas kernels, rear(): pl.pallas_call(functools.partial(rear_body, size, groups, head_size, made...  207 us
    pallas_call x1, Pallas kernels, front(): pl.pallas_call(functools.partial(front_body, size, groups, head_size), ou...  151 us
    pallas_call x1, Pallas kernels, moe(): pl.pallas_call(functools.partial(moe_body, size, groups, chunk), out_shap...  137 us

profile of v3, /device:TPU:0, one launch (start us, length us, event | category | flops | bytes accessed | tf_op | source)
XLA Modules:
  0.0 527.7 jit_solution(6103215881367864259)
XLA Ops:
  0.6 0.0 copy-start
  0.7 0.7 copy-done
  1.3 1.7 convolution_bitcast_fusion.diag_ref
  3.7 151.3 %front.1 = (s32[512,8]{1,0:T(8,128)}, f32[512,2]{1,0:T(8,128)}, f32[8,8,256]{2,1,0:T(8,128)}, bf16[4,3,1024,256]{3,2,1,0:T(8,128)(2,1)}, bf16[4,1024,256]{2,1,0:...) custom-call(s32[1]{0:T(128)S(6)} %copy.23.span_ref, ...), custom_call_target="tpu_custom_call" | custom-call | flops 1024 | bytes 1024 | tf_op jit(solution)/shard_map/front/pallas_call | solution.py:386
  155.0 137.3 %experts.1 = (bf16[8,160,1024]{2,1,0:T(8,128)(2,1)}, f32[8,8,256]{2,1,0:T(8,128)}, bf16[8,160,1024]{2,1,0:T(8,128)(2,1)}, bf16[2,3,704,1024]{3,2,1,0:T(8,128)(2,1)}, bf16[2,3,704,1024]{3,2,1,0:T(8,128)(2,1)}) custom-call(bf16[8,160,1024]{2,1,0:T(8,128)(2,1)} %get-tuple-element.35.sent_ref, f32[8,8,256]{2,1,0:T(8,128)} %get-tuple-element.36.gates_ref, ...), custom_call_target="tpu_custom_call" | custom-call | flops 1024 | bytes 1024 | tf_op jit(solution)/shard_map/experts/pallas_call | solution.py:686
  292.3 0.0 copy-start.6
  292.3 8.0 %fusion.1.far_hbm = bf16[3,704,1024]{2,1,0:T(8,128)(2,1)} fusion(bf16[2,3,704,1024]{3,2,1,0:T(8,128)(2,1)} %get-tuple-element.50, bf16[2,3,704,1024]{3,2,1,0:T(8,128)(2,1)} %get-tuple-element.49), kind=kLoop, calls=%fused_computation.3 | loop fusion | flops 8650752 | bytes 12976128 | tf_op jit(solution)/shard_map/convert_element_type | solution.py:1398
  300.2 0.0 copy-done.6
  300.2 0.6 pad_maximum_fusion.router_ref
  300.8 207.3 %rear.1 = (bf16[512,1024]{1,0:T(8,128)(2,1)}, bf16[512,1024]{1,0:T(8,128)(2,1)}, f32[16,1024]{1,0:T(8,128)}, f32[24,128]{1,0:T(8,128)}, bf16[4096,256]{1,0:T(8,128)(2,1)}, /*index=5*/bf16[3,704,1024]{2,1,0:T(8,128)(2,1)}) custom-call(s32[1]{0:T(128)S(6)} %copy.23.span_ref, f32[2,1024]{1,0:T(2,128)} %gain_ref.3, f32[16,1024]{1,0:T(8,128)} %convolution_bitcast_fusion.diag_ref, ...), custom_call_target="tpu_custom_call" | custom-call | flops 1024 | bytes 1024 | tf_op jit(solution)/shard_map/rear/pallas_call | solution.py:1275
  508.1 0.0 copy-start.2
  508.2 4.9 bitcast_add_fusion.1
  513.0 0.0 copy-done.2
  513.0 0.0 copy-start.3
  513.0 7.4 %fusion = f32[1,2,1024,704]{2,3,1,0:T(8,128)} fusion(bf16[3,704,1024]{2,1,0:T(8,128)(2,1)S(1)} %copy-done.2, bf16[2,3,704,1024]{3,2,1,0:T(8,128)(2,1)} %get-tuple-element.50, bf16[2,3,704,1024]{3,2,1,0:T(8,128)(2,1)} %get-tuple-element.49), kind=kLoop, calls=%fused_computation.2 | loop fusion | flops 7208960 | bytes 14417920 | tf_op jit(solution)/shard_map/broadcast_in_dim | solution.py:1412
  520.4 0.0 copy-start.8
  520.4 0.0 copy-start.7
  520.4 0.0 copy-done.3
  520.4 0.0 copy-start.5
  520.4 0.1 slice.48
  520.5 0.0 copy-start.4
  520.5 0.0 copy-start.1
  520.5 1.9 convert.1
  522.5 0.0 copy-done.8
  522.5 0.0 copy-done.7
  522.5 0.6 pad_maximum_fusion.1
  523.1 1.0 slice_convert_fusion
  524.1 0.6 slice_bitcast_fusion
  524.8 0.6 slice_bitcast_fusion.1
  525.4 0.0 copy-done.5
  525.4 1.0 copy.24
  526.3 0.0 copy-done.4
  526.3 1.0 copy.25
  527.3 0.0 copy-done.1
  (2 shorter events, 0.0 us)
Async XLA Ops:
  0.6 0.7 copy-start
  292.3 8.0 %copy-start.6 = (bf16[1024,8]{0,1:T(8,128)(2,1)S(1)}, bf16[1024,8]{0,1:T(8,128)(2,1)}, u32[]{:S(2)}) copy-start(bf16[1024,8]{0,1:T(8,128)(2,1)} %param.18) | copy-start | bytes 49156
  508.1 4.9 copy-start.2
  513.0 7.4 %copy-start.3 = (bf16[4096,256]{1,0:T(8,128)(2,1)S(1)}, bf16[4096,256]{1,0:T(8,128)(2,1)}, u32[]{:S(2)}) copy-start(bf16[4096,256]{1,0:T(8,128)(2,1)} %get-tuple-element.55) | copy-start | bytes 6291460
  520.4 2.1 copy-start.8
  520.4 2.1 copy-start.7
  520.4 5.0 copy-start.5
  520.5 5.8 %copy-start.4 = (bf16[512,1024]{1,0:T(8,128)(2,1)S(1)}, bf16[512,1024]{1,0:T(8,128)(2,1)}, u32[]{:S(2)}) copy-start(bf16[512,1024]{1,0:T(8,128)(2,1)} %get-tuple-element.67) | copy-start | bytes 3145732
  520.5 6.8 %copy-start.1 = (f32[32,16]{0,1:T(8,128)S(1)}, f32[32,16]{0,1:T(8,128)}, u32[]{:S(2)}) copy-start(f32[32,16]{0,1:T(8,128)} %param.17) | copy-start | bytes 6148
